TPU v7x, 32 devices: a whole 2x2x4 slice. The times are simulated.
32 devices in a mesh: parts: 2 (over y), expert: 8 (over z, x), dp: 2 (over core).
Axes of the slice: x: 2, y: 2, z: 4, core: 2. Of those that a mesh axis runs over, the one named last changes fastest.
Arguments:
- tokens: bfloat16 [4096, 2048], P(('parts', 'expert', 'dp')), parts along dimension 0, may hold values from -6 to 6
- route_ids: int32 [4096, 2], P(('parts', 'expert', 'dp')), parts along dimension 0, may hold values from 0 to 31, all different within a row; in each aligned block of 128 rows (0 to 127, 128 to 255, ...) at most 10 rows name the same one
- route_gates: float32 [4096, 2], P(('parts', 'expert', 'dp')), parts along dimension 0, may hold values from 0.1 to 1
- gate_weight: bfloat16 [32, 2048, 1408], P('expert', None, 'dp'), may hold values from -0.125 to 0.125
- up_weight: bfloat16 [32, 2048, 1408], P('expert', None, 'dp'), may hold values from -0.125 to 0.125
- down_weight: bfloat16 [32, 1408, 2048], P('expert'), may hold values from -0.15625 to 0.15625
Outputs:
- output: bfloat16 [4096, 2048], P(('parts', 'expert', 'dp')), parts along dimension 0
There are 2 independent parts, one for each index of `parts`. A program takes and returns all parts, laid end to end along the dimension named above; an argument that names none is the same for every part. Nothing has to cross between parts.
Inputs may be any that keep to these rules, and one draw needn't show every extreme that they name: `route_ids`: each row names 2 different experts; within the rows of one device (aligned blocks of 128 rows) no expert is named by more than 10 rows, a bound that some block reaches.
All inputs are finite; a program needn't handle non-finite values.
Results may differ from a plain program's by a relative error of at most 0.0058.
Values may be sent and summed in bfloat16 or wider, within the bound.
No kernel may reach another device: no remote copies, remote signals or barrier semaphores. Data moves between devices by JAX's collectives and lax.ppermute only.
A program may use at most 192 MiB of HBM per device.

v0:
```python
import jax
import jax.numpy as jnp
from jax import lax
from jax.sharding import PartitionSpec as P

FF = 1408
EXPERTS = 32
CAP = 10


def on_device(tokens, route_ids, route_gates, gate_weight, up_weight, down_weight):
    row_count = tokens.shape[0]
    width = tokens.shape[1]
    local_segs = gate_weight.shape[0]
    seg_width = down_weight.shape[1]
    groups = lax.axis_size("expert")
    per_expert = FF // seg_width
    expert_iota = jnp.arange(EXPERTS, dtype=jnp.int32)
    matched = route_ids[:, :, None] == expert_iota[None, None, :]
    member = jnp.sum(matched.astype(jnp.int32), axis=1)
    weighting = jnp.sum(jnp.where(matched, route_gates[:, :, None], jnp.float32(0.0)), axis=1)
    ranking = jnp.cumsum(member, axis=0) - member
    slot_iota = jnp.arange(CAP, dtype=jnp.int32)
    placed = (member[:, :, None] == 1) & (ranking[:, :, None] == slot_iota[None, None, :])
    placed_flat = placed.reshape(row_count, EXPERTS * CAP)
    chooser = placed_flat.astype(jnp.bfloat16)
    packed = jnp.dot(chooser.T, tokens, preferred_element_type=jnp.float32).astype(jnp.bfloat16)
    packed_four = packed.reshape(EXPERTS, 1, CAP, width)
    outgoing = jnp.broadcast_to(packed_four, (EXPERTS, per_expert, CAP, width))
    outgoing = outgoing.reshape(groups, local_segs, CAP, width)
    incoming = lax.all_to_all(outgoing, "expert", split_axis=0, concat_axis=0, tiled=True)
    full_gate, full_up = (
        lax.all_gather(gate_weight, "dp", axis=2, tiled=True),
        lax.all_gather(up_weight, "dp", axis=2, tiled=True),
    )
    gate_val = jnp.einsum("gscd,sdf->gscf", incoming, full_gate, preferred_element_type=jnp.float32)
    up_val = jnp.einsum("gscd,sdf->gscf", incoming, full_up, preferred_element_type=jnp.float32)
    hidden = (jax.nn.silu(gate_val) * up_val).astype(jnp.bfloat16)
    partial_value = jnp.einsum(
        "gscf,sfd->gscd", hidden, down_weight, preferred_element_type=jnp.float32
    ).astype(jnp.bfloat16)
    returned = lax.all_to_all(partial_value, "expert", split_axis=0, concat_axis=0, tiled=True)
    per_seg = returned.reshape(EXPERTS, per_expert, CAP, width).astype(jnp.float32)
    expert_out = jnp.sum(per_seg, axis=1).reshape(EXPERTS * CAP, width)
    combine = jnp.where(placed, weighting[:, :, None], jnp.float32(0.0)).reshape(
        row_count, EXPERTS * CAP
    )
    output = jnp.dot(
        combine, expert_out, precision=lax.Precision.HIGHEST, preferred_element_type=jnp.float32
    )
    return output.astype(jnp.bfloat16)


def solution(mesh):
    placed = (
        P(("parts", "expert", "dp"), None),
        P(("parts", "expert", "dp"), None),
        P(("parts", "expert", "dp"), None),
        P("expert", None, "dp"),
        P("expert", None, "dp"),
        P("expert", None, None),
    )
    return jax.shard_map(
        on_device,
        mesh=mesh,
        in_specs=placed,
        out_specs=P(("parts", "expert", "dp"), None),
        check_vma=False,
    )
```

profile of v0, /device:TPU:0, one launch (start us, length us, event | category | flops | bytes accessed | tf_op | source)
XLA Modules:
  0.0 167.0 jit_solution(10947640230947168460)
XLA Ops:
  6.5 0.0 copy-start
  6.5 0.0 all-gather.3.cloned.1.call-start
  6.5 0.7 all-gather.3.cloned.1.call-update
  7.3 0.0 copy-start.2
  7.3 0.0 all-gather.5.cloned.1.call-start
  7.3 0.7 all-gather.5.cloned.1.call-update
  8.0 0.0 copy-done.2
  8.0 0.1 copy.25
  8.1 0.2 reduce_window_sum.11
  8.3 0.1 copy.27
  8.6 0.1 eq.66
  8.7 0.0 copy-done
  8.7 1.6 convolution_convert_fusion
  10.3 2.3 %reshape_reshape.3 = bf16[8,4,10,2048]{3,2,1,0:T(8,128)(2,1)S(1)} reshape(bf16[320,2048]{1,0:T(8,128)(2,1)} %convolution_convert_fusion) | data formatting | bytes 2621440 | tf_op jit(solution)/shard_map/reshape;reshape | solution.py:30
  12.6 1.0 copy.28
  13.6 38.4 %all_to_all.10 = bf16[8,4,10,2048]{3,1,2,0:T(4,128)(2,1)S(1)} all-to-all(bf16[8,4,10,2048]{3,1,2,0:T(4,128)(2,1)S(1)} %copy.28), channel_id=1, replica_groups=mesh['parts'=2,'expert'=8,'dp'=2] {'expert'}, dimensions={0} | all-to-all | bytes 2621440 | tf_op jit(solution)/shard_map/all_to_all | solution.py:31
  52.1 0.0 all-gather.3.cloned.1.call-done
  52.1 15.3 %fusion.6 = f32[8,4,10,1408]{3,2,0,1:T(8,128)} fusion(bf16[4,2048,1408]{1,2,0:T(8,128)(2,1)} %all-gather.3.cloned.1.call-done, bf16[8,4,10,2048]{3,1,2,0:T(4,128)(2,1)S(1)} %all_to_all.10), kind=kOutput, calls=%fused_computation.6 | convolution fusion | flops 1845493760 | bytes 26181632 | tf_op jit(solution)/shard_map/gscd,sdf->gscf/dot_general | solution.py:36
  67.3 22.3 %all-gather.5.cloned.1.call-done = bf16[4,2048,1408]{1,2,0:T(8,128)(2,1)} async-done(((bf16[4,2048,704]{1,2,0:T(8,128)(2,1)}), bf16[4,2048,1408]{1,2,0:T(8,128)(2,1)}) %all-gather.5.cloned.1.call-update) | async-done | bytes 23068688 | tf_op jit(solution)/shard_map/all_gather | solution.py:34
  89.6 12.9 %fusion.15 = bf16[8,4,10,1408]{3,2,0,1:T(8,128)(2,1)S(1)} fusion(bf16[4,2048,1408]{1,2,0:T(8,128)(2,1)} %all-gather.5.cloned.1.call-done, f32[8,4,10,1408]{3,2,0,1:T(8,128)} %fusion.6, bf16[8,4,10,2048]{3,1,2,0:T(4,128)(2,1)S(1)} %all_to_all.10), kind=kOutput, calls=%fused_computation.9 | convolution fusion | flops 1848197120 | bytes 27082752 | tf_op jit(solution)/shard_map/gscd,sdf->gscf/dot_general | solution.py:37
  102.6 11.0 %fusion.21 = bf16[8,4,10,2048]{3,2,0,1:T(8,128)(2,1)S(1)} fusion(bf16[8,4,10,1408]{3,2,0,1:T(8,128)(2,1)S(1)} %fusion.15, bf16[4,1408,2048]{2,1,0:T(8,128)(2,1)} %param.11), kind=kOutput, calls=%fused_computation.11 | convolution fusion | flops 1846149120 | bytes 25280512 | tf_op jit(solution)/shard_map/gscf,sfd->gscd/dot_general | solution.py:39
  113.6 0.0 copy-start.3
  113.6 2.1 %copy.31 = bf16[8,4,10,2048]{3,1,2,0:T(4,128)(2,1)} copy(bf16[8,4,10,2048]{3,2,0,1:T(8,128)(2,1)S(1)} %fusion.21) | data formatting | bytes 2621440 | tf_op jit(solution)/shard_map/convert_element_type | solution.py:41
  115.7 5.8 %all-to-all-start.1 = ((bf16[8,4,10,2048]{3,1,2,0:T(4,128)(2,1)}), bf16[8,4,10,2048]{3,1,2,0:T(4,128)(2,1)}, u32[]{:S(2)}, u32[]{:S(2)}) async-start(bf16[8,4,10,2048]{3,1,2,0:T(4,128)(2,1)} %copy.31), calls=%async_computation.1 | async-start | bytes 2621440 | tf_op jit(solution)/shard_map/all_to_all | solution.py:42
  121.5 0.0 copy-done.3
  121.5 0.1 fusion.27
  121.6 31.8 %all-to-all-done.1 = bf16[8,4,10,2048]{3,1,2,0:T(4,128)(2,1)} async-done(((bf16[8,4,10,2048]{3,1,2,0:T(4,128)(2,1)}), bf16[8,4,10,2048]{3,1,2,0:T(4,128)(2,1)}, u32[]{:S(2)}, u32[]{:S(2)}) %all-to-all-start.1) | async-done | bytes 1310752 | tf_op jit(solution)/shard_map/all_to_all | solution.py:42
  153.4 0.0 copy-start.1
  153.4 2.3 %copy.32 = bf16[8,4,10,2048]{3,2,1,0:T(8,128)(2,1)S(1)} copy(bf16[8,4,10,2048]{3,1,2,0:T(4,128)(2,1)} %all-to-all-done.1) | data formatting | bytes 2621440 | tf_op jit(solution)/shard_map/all_to_all | solution.py:42
  155.7 1.3 reshape.68
  157.0 3.1 %convolution_convert_fusion.1 = bf16[128,2048]{1,0:T(8,128)(2,1)} fusion(f32[128,320]{0,1:T(8,128)S(1)} %select_n.20, bf16[320,2048]{1,0:T(8,128)(2,1)} %reshape.68), kind=kOutput, calls=%fused_computation.13 | convolution fusion | flops 1006895104 | bytes 1998848 | tf_op jit(solution)/shard_map/dot_general | solution.py:48
  160.1 0.0 copy-done.1
  (10 shorter events, 0.2 us)
Async XLA Ops:
  6.5 2.1 %copy-start = (bf16[128,2048]{1,0:T(8,128)(2,1)S(1)}, bf16[128,2048]{1,0:T(8,128)(2,1)}, u32[]{:S(2)}) copy-start(bf16[128,2048]{1,0:T(8,128)(2,1)} %param.6) | copy-start | bytes 1572868
  6.5 45.6 %all-gather.3.cloned.1.call-start = ((), (), s32[]{:S(2)}) async-start(), calls=%async_computation.2 | async-start | bytes 34603008 | tf_op jit(solution)/shard_map/all_gather | solution.py:33
  7.3 0.8 copy-start.2
  7.3 82.4 %all-gather.5.cloned.1.call-start = ((), (), s32[]{:S(2)}) async-start(), calls=%async_computation.3 | async-start | bytes 34603008 | tf_op jit(solution)/shard_map/all_gather | solution.py:34
  113.6 7.9 %copy-start.3 = (f32[128,2]{0,1:T(2,128)S(1)}, f32[128,2]{0,1:T(2,128)}, u32[]{:S(2)}) copy-start(f32[128,2]{0,1:T(2,128)} %param.8) | copy-start | bytes 3076
  115.7 37.7 %all-to-all-start.1 = ((bf16[8,4,10,2048]{3,1,2,0:T(4,128)(2,1)}), bf16[8,4,10,2048]{3,1,2,0:T(4,128)(2,1)}, u32[]{:S(2)}, u32[]{:S(2)}) async-start(bf16[8,4,10,2048]{3,1,2,0:T(4,128)(2,1)} %copy.31), calls=%async_computation.1 | async-start | bytes 2621440 | tf_op jit(solution)/shard_map/all_to_all | solution.py:42
  153.4 6.7 %copy-start.1 = (bf16[128,2048]{1,0:T(8,128)(2,1)S(1)}, bf16[128,2048]{1,0:T(8,128)(2,1)}, u32[]{:S(2)}) copy-start(bf16[128,2048]{1,0:T(8,128)(2,1)} %param.6) | copy-start | bytes 1572868
Sparse Core Ops, SparseCore 0:
  8.9 40.3 all-gather.2
  50.8 38.7 all-gather.4
where the time goes:
time: 167 us
  waiting for transfers between devices  55.5 us (33%)
  matrix products  43.9 us (26%)
  blocking collectives  38.4 us (23%)
  between operations  13.6 us (8%)
  local copies, waits for them, and re-layouts  9.43 us (6%)
  starting transfers between devices  5.81 us (3%)
    all_to_all x1, blocking collectives, on_device(): lax.all_to_all(outgoing, 'expert', split_axis=0, concat_axis=0, tiled=True)  38.4 us
    all_to_all x1, waiting for transfers between devices, on_device(): lax.all_to_all(partial_value, 'expert', split_axis=0, concat_axis=0, tile...  31.8 us
    all_gather x1, waiting for transfers between devices, on_device(): lax.all_gather(up_weight, 'dp', axis=2, tiled=True)  22.3 us
    dot_general x1, matrix products, on_device(): jnp.einsum('gscd,sdf->gscf', incoming, full_gate, preferred_element_type=...  15.3 us
    dot_general x1, matrix products, on_device(): jnp.einsum('gscd,sdf->gscf', incoming, full_up, preferred_element_type=jn...  12.9 us
    dot_general x1, matrix products, on_device(): jnp.einsum('gscf,sfd->gscd', hidden, down_weight, preferred_element_type=...  11 us
    all_to_all x1, starting transfers between devices, on_device(): lax.all_to_all(partial_value, 'expert', split_axis=0, concat_axis=0, tile...  5.77 us
  transfers between devices with their start and end apart: 3, of which 2 were waited for; matrix products, arithmetic and copies ran while one was open for 13% of the time, Pallas kernels for 0%

commit v1 on v0

--- a/solution.py
+++ b/solution.py
@@ -1,14 +1,19 @@
+import functools
+
 import jax
 import jax.numpy as jnp
 from jax import lax
+from jax.experimental import pallas as pl
+from jax.experimental.pallas import tpu as pltpu
 from jax.sharding import PartitionSpec as P
 
 FF = 1408
 EXPERTS = 32
 CAP = 10
-
-
-def on_device(tokens, route_ids, route_gates, gate_weight, up_weight, down_weight):
+TOPK = 2
+
+
+def general(tokens, route_ids, route_gates, gate_weight, up_weight, down_weight):
     row_count = tokens.shape[0]
     width = tokens.shape[1]
     local_segs = gate_weight.shape[0]
@@ -51,6 +56,242 @@
     return output.astype(jnp.bfloat16)
 
 
+VMEM = pltpu.VMEM
+MIB = 1 << 20
+
+
+def dot(a, b):
+    return jnp.dot(a, b, preferred_element_type=jnp.float32)
+
+
+def dot_nt(a, b):
+    return lax.dot_general(a, b, (((1,), (1,)), ((), ())), preferred_element_type=jnp.float32)
+
+
+def iota(shape, axis):
+    return lax.broadcasted_iota(jnp.int32, shape, axis)
+
+
+def pack_kernel(local_experts, groups, place_ref, ids_ref, tokens_ref, *outs):
+    slots_ref, blocks = outs[0], outs[1:]
+    rows = tokens_ref.shape[0]
+    block = local_experts * CAP
+    me = place_ref[0]
+    ids = ids_ref[...]
+    lane = iota((rows, 128), 1)
+    picks = [(lane == ids[:, k : k + 1]).astype(jnp.float32) for k in range(TOPK)]
+    member = functools.reduce(lambda a, b: a + b, picks)
+    earlier = (iota((rows, rows), 1) < iota((rows, rows), 0)).astype(jnp.bfloat16)
+    ranking = dot(earlier, member.astype(jnp.bfloat16))
+    shift = local_experts.bit_length() - 1
+    slots = []
+    for k in range(TOPK):
+        rank = jnp.sum(picks[k] * ranking, axis=1, keepdims=True).astype(jnp.int32)
+        one = ids[:, k : k + 1]
+        slots.append(((one >> shift) ^ me) * block + (one & (local_experts - 1)) * CAP + rank)
+    slots_ref[...] = jnp.concatenate(slots, axis=1)
+    total = groups * block
+    padded = -(-total // 128) * 128
+    place = iota((rows, padded), 1)
+    chosen = functools.reduce(lambda a, b: a | b, [place == s for s in slots])
+    chooser = chosen.astype(jnp.float32).T.astype(jnp.bfloat16)
+    step = 512
+    for c in range(0, tokens_ref.shape[1], step):
+        got = dot(chooser, tokens_ref[:, c : c + step]).astype(jnp.bfloat16)
+        for g in range(groups):
+            blocks[g][:, c : c + step] = got[g * block : (g + 1) * block, :]
+
+
+def regroup_kernel(local_experts, count, padded, *refs):
+    ins, out_ref, held = refs[:count], refs[count], refs[count + 1]
+    block = local_experts * CAP
+    for b in range(count):
+        held[b * block : (b + 1) * block, :] = ins[b][...]
+    q = iota((local_experts * padded, 1), 0)
+    j = q & (padded - 1)
+    b = (j * 205) >> 11
+    source = b * block + (q >> (padded.bit_length() - 1)) * CAP + (j - b * CAP)
+    source = jnp.where(j < count * CAP, source, -1)
+    mover = (iota((local_experts * padded, count * block), 1) == source).astype(jnp.bfloat16)
+    step = 512
+    for c in range(0, held.shape[1], step):
+        out_ref[:, c : c + step] = dot(mover, held[:, c : c + step]).astype(jnp.bfloat16)
+
+
+def ungroup_kernel(local_experts, count, padded, own_ref, other_ref, *refs):
+    block = local_experts * CAP
+    s = iota((count * block, 1), 0)
+    b = (s * 1639) >> 16
+    t = s - b * block
+    e = (t * 205) >> 11
+    source = e * padded + b * CAP + (t - e * CAP)
+    mover = (iota((count * block, local_experts * padded), 1) == source).astype(jnp.bfloat16)
+    step = 512
+    for c in range(0, own_ref.shape[1], step):
+        whole = own_ref[:, c : c + step] + other_ref[:, c : c + step].astype(jnp.float32)
+        got = dot(mover, whole.astype(jnp.bfloat16)).astype(jnp.bfloat16)
+        for k in range(count):
+            refs[k][:, c : c + step] = got[k * block : (k + 1) * block, :]
+
+
+def ffn_kernel(steps, place_ref, mine_ref, theirs_ref, gate_ref, up_ref, down_ref, own_ref, send_ref, acc):
+    f = pl.program_id(1)
+    rows = jnp.concatenate([mine_ref[...], theirs_ref[...]], axis=0)
+    gate = dot_nt(rows, gate_ref[0])
+    up = dot_nt(rows, up_ref[0])
+    hidden = (gate / (1.0 + jnp.exp(-gate)) * up).astype(jnp.bfloat16)
+    part = dot(hidden, down_ref[0])
+
+    @pl.when(f == 0)
+    def _():
+        acc[...] = part
+
+    @pl.when(f > 0)
+    def _():
+        acc[...] += part
+
+    @pl.when(f == steps - 1)
+    def _():
+        half = mine_ref.shape[0]
+        own_ref[...] = acc[:half, :]
+        send_ref[...] = acc[half:, :].astype(jnp.bfloat16)
+
+
+def combine_kernel(block, slots_ref, gates_ref, *refs):
+    groups = len(refs) - 2
+    ins, out_ref, held = refs[:groups], refs[groups], refs[groups + 1]
+    for g in range(groups):
+        held[g * block : (g + 1) * block, :] = ins[g][...]
+    rows = slots_ref.shape[0]
+    place = iota((rows, groups * block), 1)
+    slots, gates = slots_ref[...], gates_ref[...]
+    picks = [(place == slots[:, k : k + 1]).astype(jnp.bfloat16) for k in range(TOPK)]
+    step = 512
+    for c in range(0, out_ref.shape[1], step):
+        part = held[:, c : c + step]
+        total = sum(gates[:, k : k + 1] * dot(picks[k], part) for k in range(TOPK))
+        out_ref[:, c : c + step] = total.astype(jnp.bfloat16)
+
+
+def params(limit):
+    return pltpu.CompilerParams(vmem_limit_bytes=limit * MIB)
+
+
+def whole(count):
+    return [pl.BlockSpec(memory_space=VMEM)] * count
+
+
+def fast(tokens, route_ids, route_gates, gate_weight, up_weight, down_weight):
+    rows, width = tokens.shape
+    groups = lax.axis_size("expert")
+    local_experts, _, half = gate_weight.shape
+    block = local_experts * CAP
+    bf16 = jnp.bfloat16
+    place = jnp.stack([lax.axis_index("expert"), lax.axis_index("dp")]).astype(jnp.int32)
+    smem = pl.BlockSpec(memory_space=pltpu.SMEM)
+    gate_rows = jnp.swapaxes(gate_weight, 1, 2)
+    up_rows = jnp.swapaxes(up_weight, 1, 2)
+
+    packed = pl.pallas_call(
+        functools.partial(pack_kernel, local_experts, groups),
+        out_shape=[jax.ShapeDtypeStruct((rows, TOPK), jnp.int32)]
+        + [jax.ShapeDtypeStruct((block, width), bf16)] * groups,
+        in_specs=[smem] + whole(2),
+        out_specs=whole(1 + groups),
+        compiler_params=params(16),
+        name="pack",
+    )(place, route_ids, tokens)
+    slots, outgoing = packed[0], packed[1:]
+
+    def hop(x, k):
+        return lax.ppermute(x, "expert", [(i, i ^ k) for i in range(groups)])
+
+    def swap(x):
+        return lax.ppermute(x, "dp", [(0, 1), (1, 0)])
+
+    order = [4, 5, 1, 2, 3, 6, 7]
+    chunks = [[0, 4, 5, 1, 2, 3], [6, 7]]
+    incoming = {0: outgoing[0]}
+    for k in order:
+        incoming[k] = hop(outgoing[k], k)
+
+    steps = 2
+    tile = half // steps
+    returned = {}
+    for chunk in chunks:
+        count = len(chunk)
+        padded = 1 << (count * CAP - 1).bit_length()
+        tall = local_experts * padded
+        mine = pl.pallas_call(
+            functools.partial(regroup_kernel, local_experts, count, padded),
+            out_shape=jax.ShapeDtypeStruct((tall, width), bf16),
+            in_specs=whole(count),
+            out_specs=whole(1)[0],
+            scratch_shapes=[VMEM((count * block, width), bf16)],
+            compiler_params=params(16),
+            name="regroup",
+        )(*[incoming[k] for k in chunk])
+        theirs = swap(mine)
+        own, send = pl.pallas_call(
+            functools.partial(ffn_kernel, steps),
+            out_shape=[
+                jax.ShapeDtypeStruct((tall, width), jnp.float32),
+                jax.ShapeDtypeStruct((tall, width), bf16),
+            ],
+            grid_spec=pltpu.PrefetchScalarGridSpec(
+                num_scalar_prefetch=1,
+                grid=(local_experts, steps),
+                in_specs=[
+                    pl.BlockSpec((padded, width), lambda e, f, at: (e, 0)),
+                    pl.BlockSpec((padded, width), lambda e, f, at: (e, 0)),
+                    pl.BlockSpec((1, tile, width), lambda e, f, at: (e, f, 0)),
+                    pl.BlockSpec((1, tile, width), lambda e, f, at: (e, f, 0)),
+                    pl.BlockSpec((1, tile, width), lambda e, f, at: (e, at[1] * steps + f, 0)),
+                ],
+                out_specs=[
+                    pl.BlockSpec((padded, width), lambda e, f, at: (e, 0)),
+                    pl.BlockSpec((padded, width), lambda e, f, at: (e, 0)),
+                ],
+                scratch_shapes=[VMEM((2 * padded, width), jnp.float32)],
+            ),
+            compiler_params=params(32),
+            name="ffn",
+        )(place, mine, theirs, gate_rows, up_rows, down_weight)
+        other = swap(send)
+        blocks = pl.pallas_call(
+            functools.partial(ungroup_kernel, local_experts, count, padded),
+            out_shape=[jax.ShapeDtypeStruct((block, width), bf16)] * count,
+            in_specs=whole(2),
+            out_specs=whole(count),
+            compiler_params=params(16),
+            name="ungroup",
+        )(own, other)
+        for k, y in zip(chunk, blocks):
+            returned[k] = hop(y, k) if k else y
+
+    return pl.pallas_call(
+        functools.partial(combine_kernel, block),
+        out_shape=jax.ShapeDtypeStruct((rows, width), bf16),
+        in_specs=whole(2 + groups),
+        out_specs=whole(1)[0],
+        scratch_shapes=[VMEM((groups * block, width), bf16)],
+        compiler_params=params(16),
+        name="combine",
+    )(slots, route_gates, *[returned[k] for k in range(groups)])
+
+
+def on_device(tokens, route_ids, route_gates, gate_weight, up_weight, down_weight):
+    suits = (
+        lax.axis_size("expert") == 8
+        and lax.axis_size("dp") == 2
+        and down_weight.shape[1] == FF
+        and gate_weight.shape[0] == 4
+        and tokens.shape[0] == 128
+    )
+    run = fast if suits else general
+    return run(tokens, route_ids, route_gates, gate_weight, up_weight, down_weight)
+
+
 def solution(mesh):
     placed = (
         P(("parts", "expert", "dp"), None),

time: 167 us -> 118 us (0.71)
  matrix products: 43.9 us -> 0 us
  blocking collectives: 38.4 us -> 0 us
  Pallas kernels: 0 us -> 36 us
  starting transfers between devices: 5.81 us -> 41 us
  waiting for transfers between devices: 55.5 us -> 34.2 us
  between operations: 13.6 us -> 0.12 us
  local copies, waits for them, and re-layouts: 9.43 us -> 6.22 us
    dot_general x5 -> x0, matrix products: 43.9 us -> none  [the longest x1 15.3 us: on_device(): jnp.einsum('gscd,sdf->gscf', incoming, full_gate, preferred_element_type=...]
    ppermute x0 -> x18, starting transfers between devices: none -> 41 us  [the longest x14 40.2 us: hop(): return lax.ppermute(x, 'expert', [(i, i ^ k) for i in range(groups)])]
    all_to_all x1 -> x0, blocking collectives: 38.4 us -> none  [on_device(): lax.all_to_all(outgoing, 'expert', split_axis=0, concat_axis=0, tiled=True)]
    pallas_call x0 -> x8, Pallas kernels: none -> 36 us  [the longest x2 31.4 us: fast(): pl.pallas_call(functools.partial(ffn_kernel, steps), out_shape=[jax.Shape...]
    ppermute x0 -> x18, waiting for transfers between devices: none -> 34.2 us  [the longest x14 32.3 us: hop(): return lax.ppermute(x, 'expert', [(i, i ^ k) for i in range(groups)])]
    all_to_all x1 -> x0, waiting for transfers between devices: 31.8 us -> none  [on_device(): lax.all_to_all(partial_value, 'expert', split_axis=0, concat_axis=0, tile...]
    all_gather x2 -> x0, waiting for transfers between devices: 22.3 us -> none  [the longest x1 22.3 us: on_device(): lax.all_gather(up_weight, 'dp', axis=2, tiled=True)]
    unnamed x8 -> x10, local copies, waits for them, and re-layouts: 0.02 us -> 6.22 us
  transfers between devices with their start and end apart: 3 -> 18, of which waited for: 2 -> 10; matrix products, arithmetic and copies ran while one was open for 13% -> 0% of each run, Pallas kernels for 0% -> 28%
where the time goes in v1:
time: 118 us
  starting transfers between devices  41 us (35%)
  Pallas kernels  36 us (31%)
  waiting for transfers between devices  34.2 us (29%)
  local copies, waits for them, and re-layouts  6.22 us (5%)
    ppermute x14, starting transfers between devices, hop(): return lax.ppermute(x, 'expert', [(i, i ^ k) for i in range(groups)])  40.2 us
    ppermute x14, waiting for transfers between devices, hop(): return lax.ppermute(x, 'expert', [(i, i ^ k) for i in range(groups)])  32.3 us
    pallas_call x2, Pallas kernels, fast(): pl.pallas_call(functools.partial(ffn_kernel, steps), out_shape=[jax.Shape...  31.4 us
    unnamed x10, local copies, waits for them, and re-layouts  6.22 us
  transfers between devices with their start and end apart: 18, of which 10 were waited for; matrix products, arithmetic and copies ran while one was open for 0% of the time, Pallas kernels for 28%

profile of v1, /device:TPU:0, one launch (start us, length us, event | category | flops | bytes accessed | tf_op | source)
XLA Modules:
  0.0 117.6 jit_solution(7315934313409404678)
XLA Ops:
  0.0 0.8 copy.7.ids_ref
  0.8 0.1 pad_add_fusion.place_ref
  0.9 0.0 copy-start.2
  0.9 1.0 copy-done.2
  1.9 1.6 %pack.1 = (s32[128,2]{1,0:T(8,128)S(1)}, bf16[40,2048]{1,0:T(8,128)(2,1)S(1)}, bf16[40,2048]{1,0:T(8,128)(2,1)S(1)}, bf16[40,2048]{1,0:T(8,128)(2,1)S(1)}, bf16[...) custom-call(s32[2]{0:T(128)S(1)} %pad_add_fusion.place_ref, ...), custom_call_target="tpu_custom_call" | custom-call | tf_op jit(solution)/shard_map/pack/pallas_call | solution.py:195
  3.5 4.1 %collective-permute-start = (bf16[40,2048]{1,0:T(8,128)(2,1)S(1)}, bf16[40,2048]{1,0:T(8,128)(2,1)S(1)}, u32[]{:S(2)}, u32[]{:S(2)}) collective-permute-start(bf16[40,2048]{1,0:T(8,128)(2,1)S(1)} %get-tuple-element.28), channel_id=1, source_target_pairs={{0,8},{2,10},{4,12},{6,14},{8,0},{10,2},{12,4},{14,6},{1,9},{3,11}... | collective-permute-start | bytes 491528 | tf_op jit(solution)/shard_map/ppermute | solution.py:207
  7.6 1.3 %collective-permute-start.1 = (bf16[40,2048]{1,0:T(8,128)(2,1)S(1)}, bf16[40,2048]{1,0:T(8,128)(2,1)S(1)}, u32[]{:S(2)}, u32[]{:S(2)}) collective-permute-start(bf16[40,2048]{1,0:T(8,128)(2,1)S(1)} %get-tuple-element.29), channel_id=1, source_target_pairs={{0,10},{2,8},{4,14},{6,12},{8,2},{10,0},{12,6},{14,4},{1,11},{3,9}... | collective-permute-start | bytes 491528 | tf_op jit(solution)/shard_map/ppermute | solution.py:207
  8.8 0.3 collective-permute-start.2
  9.1 1.8 %collective-permute-start.3 = (bf16[40,2048]{1,0:T(8,128)(2,1)S(1)}, bf16[40,2048]{1,0:T(8,128)(2,1)S(1)}, u32[]{:S(2)}, u32[]{:S(2)}) collective-permute-start(bf16[40,2048]{1,0:T(8,128)(2,1)S(1)} %get-tuple-element.31), channel_id=1, source_target_pairs={{0,4},{2,6},{4,0},{6,2},{8,12},{10,14},{12,8},{14,10},{1,5},{3,7},... | collective-permute-start | bytes 491528 | tf_op jit(solution)/shard_map/ppermute | solution.py:207
  10.9 1.4 %collective-permute-start.4 = (bf16[40,2048]{1,0:T(8,128)(2,1)S(1)}, bf16[40,2048]{1,0:T(8,128)(2,1)S(1)}, u32[]{:S(2)}, u32[]{:S(2)}) collective-permute-start(bf16[40,2048]{1,0:T(8,128)(2,1)S(1)} %get-tuple-element.32), channel_id=1, source_target_pairs={{0,6},{2,4},{4,2},{6,0},{8,14},{10,12},{12,10},{14,8},{1,7},{3,5},... | collective-permute-start | bytes 491528 | tf_op jit(solution)/shard_map/ppermute | solution.py:207
  12.3 7.4 %collective-permute-done.refs_1_ = bf16[40,2048]{1,0:T(8,128)(2,1)S(1)} collective-permute-done((bf16[40,2048]{1,0:T(8,128)(2,1)S(1)}, bf16[40,2048]{1,0:T(8,128)(2,1)S(1)}, u32[]{:S(2)}, u32[]{:S(2)}) %collective-permute-start) | collective-permute-done | bytes 163872 | tf_op jit(solution)/shard_map/ppermute | solution.py:207
  19.7 3.6 %collective-permute-done.1.refs_2_ = bf16[40,2048]{1,0:T(8,128)(2,1)S(1)} collective-permute-done((bf16[40,2048]{1,0:T(8,128)(2,1)S(1)}, bf16[40,2048]{1,0:T(8,128)(2,1)S(1)}, u32[]{:S(2)}, u32[]{:S(2)}) %collective-permute-start.1) | collective-permute-done | bytes 163872 | tf_op jit(solution)/shard_map/ppermute | solution.py:207
  23.3 0.0 collective-permute-done.2.refs_3_
  23.3 0.0 collective-permute-done.3.refs_4_
  23.3 1.5 %collective-permute-done.4.refs_5_ = bf16[40,2048]{1,0:T(8,128)(2,1)S(1)} collective-permute-done((bf16[40,2048]{1,0:T(8,128)(2,1)S(1)}, bf16[40,2048]{1,0:T(8,128)(2,1)S(1)}, u32[]{:S(2)}, u32[]{:S(2)}) %collective-permute-start.4) | collective-permute-done | bytes 163872 | tf_op jit(solution)/shard_map/ppermute | solution.py:207
  24.8 0.5 regroup.2.mine_ref
  25.3 0.1 collective-permute-start.5
  25.4 4.7 %collective-permute-start.12 = (bf16[40,2048]{1,0:T(8,128)(2,1)S(1)}, bf16[40,2048]{1,0:T(8,128)(2,1)S(1)}, u32[]{:S(2)}, u32[]{:S(2)}) collective-permute-start(bf16[40,2048]{1,0:T(8,128)(2,1)S(1)} %get-tuple-element.41), channel_id=1, source_target_pairs={{0,12},{2,14},{4,8},{6,10},{8,4},{10,6},{12,0},{14,2},{1,13},{3,15... | collective-permute-start | bytes 491528 | tf_op jit(solution)/shard_map/ppermute | solution.py:207
  30.0 0.1 collective-permute-start.13
  30.1 5.1 %collective-permute-done.12.refs_0_ = bf16[40,2048]{1,0:T(8,128)(2,1)S(1)} collective-permute-done((bf16[40,2048]{1,0:T(8,128)(2,1)S(1)}, bf16[40,2048]{1,0:T(8,128)(2,1)S(1)}, u32[]{:S(2)}, u32[]{:S(2)}) %collective-permute-start.12) | collective-permute-done | bytes 163872 | tf_op jit(solution)/shard_map/ppermute | solution.py:207
  35.2 3.9 %collective-permute-done.13.refs_1_ = bf16[40,2048]{1,0:T(8,128)(2,1)S(1)} collective-permute-done((bf16[40,2048]{1,0:T(8,128)(2,1)S(1)}, bf16[40,2048]{1,0:T(8,128)(2,1)S(1)}, u32[]{:S(2)}, u32[]{:S(2)}) %collective-permute-start.13) | collective-permute-done | bytes 163872 | tf_op jit(solution)/shard_map/ppermute | solution.py:207
  39.1 0.3 regroup.3.mine_ref
  39.4 0.1 collective-permute-start.14
  39.5 0.0 collective-permute-done.5.theirs_ref
  39.5 0.0 copy-start
  39.5 4.3 %copy-done = bf16[4,2048,704]{1,2,0:T(8,128)(2,1)S(1)} copy-done((bf16[4,2048,704]{1,2,0:T(8,128)(2,1)S(1)}, bf16[4,2048,704]{1,2,0:T(8,128)(2,1)}, u32[]{:S(2)}) %copy-start) | copy-done | bytes 11534360
  43.8 0.0 copy-start.1
  43.8 16.5 %ffn.2 = (f32[256,2048]{1,0:T(8,128)S(1)}, bf16[256,2048]{1,0:T(8,128)(2,1)S(1)}) custom-call(s32[2]{0:T(128)S(1)} %pad_add_fusion.place_ref, bf16[256,2048]{1,0:T(8,128)(2,1)S(1)} %regroup.2.mine_ref, bf16[256,2048]{1,0:T(8,128)(2,1)S(1)} %collective-permute-done.5.theirs_ref, bf16[4,704,2048]{2,1,0:T(8,128)(2,1)S(1)} %bitcast.4, ...), custom_call_target="tpu_custom_call" | custom-call | tf_op jit(solution)/shard_map/ffn/pallas_call | solution.py:235
  60.3 0.0 copy-start.3
  60.3 0.6 collective-permute-start.6
  60.9 0.0 collective-permute-done.14.theirs_ref
  60.9 0.0 copy-done.1
  60.9 14.9 %ffn.3 = (f32[128,2048]{1,0:T(8,128)S(1)}, bf16[128,2048]{1,0:T(8,128)(2,1)S(1)}) custom-call(s32[2]{0:T(128)S(1)} %pad_add_fusion.place_ref, bf16[128,2048]{1,0:T(8,128)(2,1)S(1)} %regroup.3.mine_ref, bf16[128,2048]{1,0:T(8,128)(2,1)S(1)} %collective-permute-done.14.theirs_ref, bf16[4,704,2048]{2,1,0:T(8,128)(2,1)S(1)} %bitcast.5, ...), custom_call_target="tpu_custom_call" | custom-call | tf_op jit(solution)/shard_map/ffn/pallas_call | solution.py:235
  75.8 0.1 collective-permute-start.15
  75.9 1.9 %collective-permute-done.15.other_ref = bf16[128,2048]{1,0:T(8,128)(2,1)S(1)} collective-permute-done((bf16[128,2048]{1,0:T(8,128)(2,1)S(1)}, bf16[128,2048]{1,0:T(8,128)(2,1)S(1)}, u32[]{:S(2)}, u32[]{:S(2)}) %collective-permute-start.15) | collective-permute-done | bytes 524320 | tf_op jit(solution)/shard_map/ppermute | solution.py:210
  77.7 0.3 ungroup.3
  78.0 2.9 %collective-permute-start.16 = (bf16[40,2048]{1,0:T(8,128)(2,1)S(1)}, bf16[40,2048]{1,0:T(8,128)(2,1)S(1)}, u32[]{:S(2)}, u32[]{:S(2)}) collective-permute-start(bf16[40,2048]{1,0:T(8,128)(2,1)S(1)} %get-tuple-element.45), channel_id=1, source_target_pairs={{0,12},{2,14},{4,8},{6,10},{8,4},{10,6},{12,0},{14,2},{1,13},{3,15... | collective-permute-start | bytes 491528 | tf_op jit(solution)/shard_map/ppermute | solution.py:207
  81.0 1.2 %collective-permute-start.17 = (bf16[40,2048]{1,0:T(8,128)(2,1)S(1)}, bf16[40,2048]{1,0:T(8,128)(2,1)S(1)}, u32[]{:S(2)}, u32[]{:S(2)}) collective-permute-start(bf16[40,2048]{1,0:T(8,128)(2,1)S(1)} %get-tuple-element.46), channel_id=1, source_target_pairs={{0,14},{2,12},{4,10},{6,8},{8,6},{10,4},{12,2},{14,0},{1,15},{3,13... | collective-permute-start | bytes 491528 | tf_op jit(solution)/shard_map/ppermute | solution.py:207
  82.2 0.0 collective-permute-done.6.other_ref
  82.2 0.5 ungroup.2
  82.7 4.1 %collective-permute-start.10 = (bf16[40,2048]{1,0:T(8,128)(2,1)S(1)}, bf16[40,2048]{1,0:T(8,128)(2,1)S(1)}, u32[]{:S(2)}, u32[]{:S(2)}) collective-permute-start(bf16[40,2048]{1,0:T(8,128)(2,1)S(1)} %get-tuple-element.39), channel_id=1, source_target_pairs={{0,8},{2,10},{4,12},{6,14},{8,0},{10,2},{12,4},{14,6},{1,9},{3,11}... | collective-permute-start | bytes 491528 | tf_op jit(solution)/shard_map/ppermute | solution.py:207
  86.8 1.0 collective-permute-start.11
  87.8 0.5 collective-permute-start.7
  88.3 0.0 collective-permute-done.16.refs_6_
  88.3 12.5 %collective-permute-start.8 = (bf16[40,2048]{1,0:T(8,128)(2,1)S(1)}, bf16[40,2048]{1,0:T(8,128)(2,1)S(1)}, u32[]{:S(2)}, u32[]{:S(2)}) collective-permute-start(bf16[40,2048]{1,0:T(8,128)(2,1)S(1)} %get-tuple-element.37), channel_id=1, source_target_pairs={{0,4},{2,6},{4,0},{6,2},{8,12},{10,14},{12,8},{14,10},{1,5},{3,7},... | collective-permute-start | bytes 491528 | tf_op jit(solution)/shard_map/ppermute | solution.py:207
  100.8 0.0 collective-permute-done.17.refs_7_
  100.8 4.4 %collective-permute-start.9 = (bf16[40,2048]{1,0:T(8,128)(2,1)S(1)}, bf16[40,2048]{1,0:T(8,128)(2,1)S(1)}, u32[]{:S(2)}, u32[]{:S(2)}) collective-permute-start(bf16[40,2048]{1,0:T(8,128)(2,1)S(1)} %get-tuple-element.38), channel_id=1, source_target_pairs={{0,6},{2,4},{4,2},{6,0},{8,14},{10,12},{12,10},{14,8},{1,7},{3,5},... | collective-permute-start | bytes 491528 | tf_op jit(solution)/shard_map/ppermute | solution.py:207
  105.2 0.0 copy-done.3
  105.2 0.1 copy.8.gates_ref
  105.3 2.0 %collective-permute-done.10.refs_4_ = bf16[40,2048]{1,0:T(8,128)(2,1)S(1)} collective-permute-done((bf16[40,2048]{1,0:T(8,128)(2,1)S(1)}, bf16[40,2048]{1,0:T(8,128)(2,1)S(1)}, u32[]{:S(2)}, u32[]{:S(2)}) %collective-permute-start.10) | collective-permute-done | bytes 163872 | tf_op jit(solution)/shard_map/ppermute | solution.py:207
  107.4 3.7 %collective-permute-done.11.refs_5_ = bf16[40,2048]{1,0:T(8,128)(2,1)S(1)} collective-permute-done((bf16[40,2048]{1,0:T(8,128)(2,1)S(1)}, bf16[40,2048]{1,0:T(8,128)(2,1)S(1)}, u32[]{:S(2)}, u32[]{:S(2)}) %collective-permute-start.11) | collective-permute-done | bytes 163872 | tf_op jit(solution)/shard_map/ppermute | solution.py:207
  111.1 0.0 collective-permute-done.7.refs_1_
  111.1 1.8 %collective-permute-done.8.refs_2_ = bf16[40,2048]{1,0:T(8,128)(2,1)S(1)} collective-permute-done((bf16[40,2048]{1,0:T(8,128)(2,1)S(1)}, bf16[40,2048]{1,0:T(8,128)(2,1)S(1)}, u32[]{:S(2)}, u32[]{:S(2)}) %collective-permute-start.8) | collective-permute-done | bytes 163872 | tf_op jit(solution)/shard_map/ppermute | solution.py:207
  112.8 3.2 %collective-permute-done.9.refs_3_ = bf16[40,2048]{1,0:T(8,128)(2,1)S(1)} collective-permute-done((bf16[40,2048]{1,0:T(8,128)(2,1)S(1)}, bf16[40,2048]{1,0:T(8,128)(2,1)S(1)}, u32[]{:S(2)}, u32[]{:S(2)}) %collective-permute-start.9) | collective-permute-done | bytes 163872 | tf_op jit(solution)/shard_map/ppermute | solution.py:207
  116.1 1.6 %combine.1 = bf16[128,2048]{1,0:T(8,128)(2,1)} custom-call(s32[128,2]{1,0:T(8,128)S(1)} %get-tuple-element.26.slots_ref, f32[128,2]{1,0:T(8,128)S(1)} %copy.8.gates_ref, bf16[40,2048]{1,0:T(8,128)(2,1)S(1)} %get-tuple-element.35.refs_0_, bf16[40,2048]{1,0:T(8,128)(2,1)S(1)} %collective-permute-done.7.refs_1_, ...), custom_call_target="tpu_custom_call" | custom-call | tf_op jit(solution)/shard_map/combine/pallas_call | solution.py:272
Async XLA Ops:
  0.9 1.0 copy-start.2
  3.5 16.3 %collective-permute-start = (bf16[40,2048]{1,0:T(8,128)(2,1)S(1)}, bf16[40,2048]{1,0:T(8,128)(2,1)S(1)}, u32[]{:S(2)}, u32[]{:S(2)}) collective-permute-start(bf16[40,2048]{1,0:T(8,128)(2,1)S(1)} %get-tuple-element.28), channel_id=1, source_target_pairs={{0,8},{2,10},{4,12},{6,14},{8,0},{10,2},{12,4},{14,6},{1,9},{3,11}... | collective-permute-start | bytes 491528 | tf_op jit(solution)/shard_map/ppermute | solution.py:207
  7.6 15.7 %collective-permute-start.1 = (bf16[40,2048]{1,0:T(8,128)(2,1)S(1)}, bf16[40,2048]{1,0:T(8,128)(2,1)S(1)}, u32[]{:S(2)}, u32[]{:S(2)}) collective-permute-start(bf16[40,2048]{1,0:T(8,128)(2,1)S(1)} %get-tuple-element.29), channel_id=1, source_target_pairs={{0,10},{2,8},{4,14},{6,12},{8,2},{10,0},{12,6},{14,4},{1,11},{3,9}... | collective-permute-start | bytes 491528 | tf_op jit(solution)/shard_map/ppermute | solution.py:207
  8.8 14.5 %collective-permute-start.2 = (bf16[40,2048]{1,0:T(8,128)(2,1)S(1)}, bf16[40,2048]{1,0:T(8,128)(2,1)S(1)}, u32[]{:S(2)}, u32[]{:S(2)}) collective-permute-start(bf16[40,2048]{1,0:T(8,128)(2,1)S(1)} %get-tuple-element.30), channel_id=1, source_target_pairs={{0,2},{2,0},{4,6},{6,4},{8,10},{10,8},{12,14},{14,12},{1,3},{3,1},... | collective-permute-start | bytes 491528 | tf_op jit(solution)/shard_map/ppermute | solution.py:207
  9.1 14.2 %collective-permute-start.3 = (bf16[40,2048]{1,0:T(8,128)(2,1)S(1)}, bf16[40,2048]{1,0:T(8,128)(2,1)S(1)}, u32[]{:S(2)}, u32[]{:S(2)}) collective-permute-start(bf16[40,2048]{1,0:T(8,128)(2,1)S(1)} %get-tuple-element.31), channel_id=1, source_target_pairs={{0,4},{2,6},{4,0},{6,2},{8,12},{10,14},{12,8},{14,10},{1,5},{3,7},... | collective-permute-start | bytes 491528 | tf_op jit(solution)/shard_map/ppermute | solution.py:207
  10.9 13.9 %collective-permute-start.4 = (bf16[40,2048]{1,0:T(8,128)(2,1)S(1)}, bf16[40,2048]{1,0:T(8,128)(2,1)S(1)}, u32[]{:S(2)}, u32[]{:S(2)}) collective-permute-start(bf16[40,2048]{1,0:T(8,128)(2,1)S(1)} %get-tuple-element.32), channel_id=1, source_target_pairs={{0,6},{2,4},{4,2},{6,0},{8,14},{10,12},{12,10},{14,8},{1,7},{3,5},... | collective-permute-start | bytes 491528 | tf_op jit(solution)/shard_map/ppermute | solution.py:207
  25.3 14.2 %collective-permute-start.5 = (bf16[256,2048]{1,0:T(8,128)(2,1)S(1)}, bf16[256,2048]{1,0:T(8,128)(2,1)S(1)}, u32[]{:S(2)}, u32[]{:S(2)}) collective-permute-start(bf16[256,2048]{1,0:T(8,128)(2,1)S(1)} %regroup.2.mine_ref), channel_id=1, source_target_pairs={{0,1},{1,0},{2,3},{3,2},{4,5},{5,4},{6,7},{7,6},{8,9},{9,8},{10,11... | collective-permute-start | bytes 3145736 | tf_op jit(solution)/shard_map/ppermute | solution.py:210
  25.4 9.8 %collective-permute-start.12 = (bf16[40,2048]{1,0:T(8,128)(2,1)S(1)}, bf16[40,2048]{1,0:T(8,128)(2,1)S(1)}, u32[]{:S(2)}, u32[]{:S(2)}) collective-permute-start(bf16[40,2048]{1,0:T(8,128)(2,1)S(1)} %get-tuple-element.41), channel_id=1, source_target_pairs={{0,12},{2,14},{4,8},{6,10},{8,4},{10,6},{12,0},{14,2},{1,13},{3,15... | collective-permute-start | bytes 491528 | tf_op jit(solution)/shard_map/ppermute | solution.py:207
  30.0 9.1 %collective-permute-start.13 = (bf16[40,2048]{1,0:T(8,128)(2,1)S(1)}, bf16[40,2048]{1,0:T(8,128)(2,1)S(1)}, u32[]{:S(2)}, u32[]{:S(2)}) collective-permute-start(bf16[40,2048]{1,0:T(8,128)(2,1)S(1)} %get-tuple-element.42), channel_id=1, source_target_pairs={{0,14},{2,12},{4,10},{6,8},{8,6},{10,4},{12,2},{14,0},{1,15},{3,13... | collective-permute-start | bytes 491528 | tf_op jit(solution)/shard_map/ppermute | solution.py:207
  39.4 21.5 %collective-permute-start.14 = (bf16[128,2048]{1,0:T(8,128)(2,1)S(1)}, bf16[128,2048]{1,0:T(8,128)(2,1)S(1)}, u32[]{:S(2)}, u32[]{:S(2)}) collective-permute-start(bf16[128,2048]{1,0:T(8,128)(2,1)S(1)} %regroup.3.mine_ref), channel_id=1, source_target_pairs={{0,1},{1,0},{2,3},{3,2},{4,5},{5,4},{6,7},{7,6},{8,9},{9,8},{10,11... | collective-permute-start | bytes 1572872 | tf_op jit(solution)/shard_map/ppermute | solution.py:210
  39.5 4.3 %copy-start = (bf16[4,2048,704]{1,2,0:T(8,128)(2,1)S(1)}, bf16[4,2048,704]{1,2,0:T(8,128)(2,1)}, u32[]{:S(2)}) copy-start(bf16[4,2048,704]{1,2,0:T(8,128)(2,1)} %param.9) | copy-start | bytes 34603012
  43.8 17.1 %copy-start.1 = (bf16[4,2048,704]{1,2,0:T(8,128)(2,1)S(1)}, bf16[4,2048,704]{1,2,0:T(8,128)(2,1)}, u32[]{:S(2)}) copy-start(bf16[4,2048,704]{1,2,0:T(8,128)(2,1)} %param.9) | copy-start | bytes 34603012
  60.3 45.0 %copy-start.3 = (f32[128,2]{0,1:T(2,128)S(1)}, f32[128,2]{0,1:T(2,128)}, u32[]{:S(2)}) copy-start(f32[128,2]{0,1:T(2,128)} %param.8) | copy-start | bytes 3076
  60.3 21.9 %collective-permute-start.6 = (bf16[256,2048]{1,0:T(8,128)(2,1)S(1)}, bf16[256,2048]{1,0:T(8,128)(2,1)S(1)}, u32[]{:S(2)}, u32[]{:S(2)}) collective-permute-start(bf16[256,2048]{1,0:T(8,128)(2,1)S(1)} %get-tuple-element.34), channel_id=1, source_target_pairs={{0,1},{1,0},{2,3},{3,2},{4,5},{5,4},{6,7},{7,6},{8,9},{9,8},{10,11... | collective-permute-start | bytes 3145736 | tf_op jit(solution)/shard_map/ppermute | solution.py:210
  75.8 2.0 %collective-permute-start.15 = (bf16[128,2048]{1,0:T(8,128)(2,1)S(1)}, bf16[128,2048]{1,0:T(8,128)(2,1)S(1)}, u32[]{:S(2)}, u32[]{:S(2)}) collective-permute-start(bf16[128,2048]{1,0:T(8,128)(2,1)S(1)} %get-tuple-element.44), channel_id=1, source_target_pairs={{0,1},{1,0},{2,3},{3,2},{4,5},{5,4},{6,7},{7,6},{8,9},{9,8},{10,11... | collective-permute-start | bytes 1572872 | tf_op jit(solution)/shard_map/ppermute | solution.py:210
  78.0 10.3 %collective-permute-start.16 = (bf16[40,2048]{1,0:T(8,128)(2,1)S(1)}, bf16[40,2048]{1,0:T(8,128)(2,1)S(1)}, u32[]{:S(2)}, u32[]{:S(2)}) collective-permute-start(bf16[40,2048]{1,0:T(8,128)(2,1)S(1)} %get-tuple-element.45), channel_id=1, source_target_pairs={{0,12},{2,14},{4,8},{6,10},{8,4},{10,6},{12,0},{14,2},{1,13},{3,15... | collective-permute-start | bytes 491528 | tf_op jit(solution)/shard_map/ppermute | solution.py:207
  81.0 19.9 %collective-permute-start.17 = (bf16[40,2048]{1,0:T(8,128)(2,1)S(1)}, bf16[40,2048]{1,0:T(8,128)(2,1)S(1)}, u32[]{:S(2)}, u32[]{:S(2)}) collective-permute-start(bf16[40,2048]{1,0:T(8,128)(2,1)S(1)} %get-tuple-element.46), channel_id=1, source_target_pairs={{0,14},{2,12},{4,10},{6,8},{8,6},{10,4},{12,2},{14,0},{1,15},{3,13... | collective-permute-start | bytes 491528 | tf_op jit(solution)/shard_map/ppermute | solution.py:207
  82.7 24.7 %collective-permute-start.10 = (bf16[40,2048]{1,0:T(8,128)(2,1)S(1)}, bf16[40,2048]{1,0:T(8,128)(2,1)S(1)}, u32[]{:S(2)}, u32[]{:S(2)}) collective-permute-start(bf16[40,2048]{1,0:T(8,128)(2,1)S(1)} %get-tuple-element.39), channel_id=1, source_target_pairs={{0,8},{2,10},{4,12},{6,14},{8,0},{10,2},{12,4},{14,6},{1,9},{3,11}... | collective-permute-start | bytes 491528 | tf_op jit(solution)/shard_map/ppermute | solution.py:207
  86.8 24.3 %collective-permute-start.11 = (bf16[40,2048]{1,0:T(8,128)(2,1)S(1)}, bf16[40,2048]{1,0:T(8,128)(2,1)S(1)}, u32[]{:S(2)}, u32[]{:S(2)}) collective-permute-start(bf16[40,2048]{1,0:T(8,128)(2,1)S(1)} %get-tuple-element.40), channel_id=1, source_target_pairs={{0,10},{2,8},{4,14},{6,12},{8,2},{10,0},{12,6},{14,4},{1,11},{3,9}... | collective-permute-start | bytes 491528 | tf_op jit(solution)/shard_map/ppermute | solution.py:207
  87.8 23.3 %collective-permute-start.7 = (bf16[40,2048]{1,0:T(8,128)(2,1)S(1)}, bf16[40,2048]{1,0:T(8,128)(2,1)S(1)}, u32[]{:S(2)}, u32[]{:S(2)}) collective-permute-start(bf16[40,2048]{1,0:T(8,128)(2,1)S(1)} %get-tuple-element.36), channel_id=1, source_target_pairs={{0,2},{2,0},{4,6},{6,4},{8,10},{10,8},{12,14},{14,12},{1,3},{3,1},... | collective-permute-start | bytes 491528 | tf_op jit(solution)/shard_map/ppermute | solution.py:207
  88.3 24.5 %collective-permute-start.8 = (bf16[40,2048]{1,0:T(8,128)(2,1)S(1)}, bf16[40,2048]{1,0:T(8,128)(2,1)S(1)}, u32[]{:S(2)}, u32[]{:S(2)}) collective-permute-start(bf16[40,2048]{1,0:T(8,128)(2,1)S(1)} %get-tuple-element.37), channel_id=1, source_target_pairs={{0,4},{2,6},{4,0},{6,2},{8,12},{10,14},{12,8},{14,10},{1,5},{3,7},... | collective-permute-start | bytes 491528 | tf_op jit(solution)/shard_map/ppermute | solution.py:207
  100.8 15.3 %collective-permute-start.9 = (bf16[40,2048]{1,0:T(8,128)(2,1)S(1)}, bf16[40,2048]{1,0:T(8,128)(2,1)S(1)}, u32[]{:S(2)}, u32[]{:S(2)}) collective-permute-start(bf16[40,2048]{1,0:T(8,128)(2,1)S(1)} %get-tuple-element.38), channel_id=1, source_target_pairs={{0,6},{2,4},{4,2},{6,0},{8,14},{10,12},{12,10},{14,8},{1,7},{3,5},... | collective-permute-start | bytes 491528 | tf_op jit(solution)/shard_map/ppermute | solution.py:207

commit v2 on v1

v2 whole, which is shorter than its diff:
```python
import functools

import jax
import jax.numpy as jnp
from jax import lax
from jax.experimental import pallas as pl
from jax.experimental.pallas import tpu as pltpu
from jax.sharding import PartitionSpec as P

FF = 1408
EXPERTS = 32
CAP = 10
TOPK = 2
SPLITS = (4, 4)


def general(tokens, route_ids, route_gates, gate_weight, up_weight, down_weight):
    row_count = tokens.shape[0]
    width = tokens.shape[1]
    local_segs = gate_weight.shape[0]
    seg_width = down_weight.shape[1]
    groups = lax.axis_size("expert")
    per_expert = FF // seg_width
    expert_iota = jnp.arange(EXPERTS, dtype=jnp.int32)
    matched = route_ids[:, :, None] == expert_iota[None, None, :]
    member = jnp.sum(matched.astype(jnp.int32), axis=1)
    weighting = jnp.sum(jnp.where(matched, route_gates[:, :, None], jnp.float32(0.0)), axis=1)
    ranking = jnp.cumsum(member, axis=0) - member
    slot_iota = jnp.arange(CAP, dtype=jnp.int32)
    placed = (member[:, :, None] == 1) & (ranking[:, :, None] == slot_iota[None, None, :])
    placed_flat = placed.reshape(row_count, EXPERTS * CAP)
    chooser = placed_flat.astype(jnp.bfloat16)
    packed = jnp.dot(chooser.T, tokens, preferred_element_type=jnp.float32).astype(jnp.bfloat16)
    packed_four = packed.reshape(EXPERTS, 1, CAP, width)
    outgoing = jnp.broadcast_to(packed_four, (EXPERTS, per_expert, CAP, width))
    outgoing = outgoing.reshape(groups, local_segs, CAP, width)
    incoming = lax.all_to_all(outgoing, "expert", split_axis=0, concat_axis=0, tiled=True)
    full_gate, full_up = (
        lax.all_gather(gate_weight, "dp", axis=2, tiled=True),
        lax.all_gather(up_weight, "dp", axis=2, tiled=True),
    )
    gate_val = jnp.einsum("gscd,sdf->gscf", incoming, full_gate, preferred_element_type=jnp.float32)
    up_val = jnp.einsum("gscd,sdf->gscf", incoming, full_up, preferred_element_type=jnp.float32)
    hidden = (jax.nn.silu(gate_val) * up_val).astype(jnp.bfloat16)
    partial_value = jnp.einsum(
        "gscf,sfd->gscd", hidden, down_weight, preferred_element_type=jnp.float32
    ).astype(jnp.bfloat16)
    returned = lax.all_to_all(partial_value, "expert", split_axis=0, concat_axis=0, tiled=True)
    per_seg = returned.reshape(EXPERTS, per_expert, CAP, width).astype(jnp.float32)
    expert_out = jnp.sum(per_seg, axis=1).reshape(EXPERTS * CAP, width)
    combine = jnp.where(placed, weighting[:, :, None], jnp.float32(0.0)).reshape(
        row_count, EXPERTS * CAP
    )
    output = jnp.dot(
        combine, expert_out, precision=lax.Precision.HIGHEST, preferred_element_type=jnp.float32
    )
    return output.astype(jnp.bfloat16)


VMEM = pltpu.VMEM
MIB = 1 << 20


def dot(a, b):
    return jnp.dot(a, b, preferred_element_type=jnp.float32)


def dot_nt(a, b):
    return lax.dot_general(a, b, (((1,), (1,)), ((), ())), preferred_element_type=jnp.float32)


def iota(shape, axis):
    return lax.broadcasted_iota(jnp.int32, shape, axis)


def pack_kernel(local_experts, groups, place_ref, ids_ref, gates_ref, tokens_ref, *outs):
    route_ref, blocks = outs[0], outs[1:]
    rows = tokens_ref.shape[0]
    block = local_experts * CAP
    me = place_ref[0]
    ids = ids_ref[...]
    expert = iota((EXPERTS, rows), 0)
    picks = [(expert == ids[k : k + 1, :]).astype(jnp.float32) for k in range(TOPK)]
    member = functools.reduce(lambda a, b: a + b, picks)
    earlier = (iota((rows, rows), 0) < iota((rows, rows), 1)).astype(jnp.bfloat16)
    ranking = dot(member.astype(jnp.bfloat16), earlier)
    shift = local_experts.bit_length() - 1
    slots = []
    for k in range(TOPK):
        rank = jnp.sum(picks[k] * ranking, axis=0, keepdims=True).astype(jnp.int32)
        one = ids[k : k + 1, :]
        slots.append(((one >> shift) ^ me) * block + (one & (local_experts - 1)) * CAP + rank)
    place = iota((groups * block, rows), 0)
    chosen = functools.reduce(lambda a, b: a | b, [place == s for s in slots])
    chooser = chosen.astype(jnp.bfloat16)
    step = 512
    for c in range(0, tokens_ref.shape[1], step):
        got = dot(chooser, tokens_ref[:, c : c + step]).astype(jnp.bfloat16)
        for g in range(groups):
            blocks[g][:, c : c + step] = got[g * block : (g + 1) * block, :]
    columns = [s.astype(jnp.float32) for s in slots] + [gates_ref[...]]
    columns.append(jnp.zeros((rows - 2 * TOPK, rows), jnp.float32))
    route_ref[...] = jnp.concatenate(columns, axis=0).T


def regroup_kernel(local_experts, count, padded, *refs):
    ins, out_ref, pieces, held = refs[:count], refs[count], refs[count + 1 : -1], refs[-1]
    each = local_experts * padded // len(pieces)
    block = local_experts * CAP
    for b in range(count):
        held[b * block : (b + 1) * block, :] = ins[b][...]
    q = iota((local_experts * padded, 1), 0)
    j = q & (padded - 1)
    b = (j * 205) >> 11
    source = b * block + (q >> (padded.bit_length() - 1)) * CAP + (j - b * CAP)
    source = jnp.where(j < count * CAP, source, -1)
    mover = (iota((local_experts * padded, count * block), 1) == source).astype(jnp.bfloat16)
    step = 512
    for c in range(0, held.shape[1], step):
        got = dot(mover, held[:, c : c + step]).astype(jnp.bfloat16)
        out_ref[:, c : c + step] = got
        for k in range(len(pieces)):
            pieces[k][:, c : c + step] = got[k * each : (k + 1) * each, :]


def ungroup_kernel(local_experts, count, padded, own_ref, *refs):
    others, refs = refs[:-count], refs[-count:]
    each = local_experts * padded // len(others)
    block = local_experts * CAP
    s = iota((count * block, 1), 0)
    b = (s * 1639) >> 16
    t = s - b * block
    e = (t * 205) >> 11
    source = e * padded + b * CAP + (t - e * CAP)
    mover = (iota((count * block, local_experts * padded), 1) == source).astype(jnp.bfloat16)
    step = 512
    for c in range(0, own_ref.shape[1], step):
        parts = []
        for k, other_ref in enumerate(others):
            part = own_ref[k * each : (k + 1) * each, c : c + step]
            parts.append((part + other_ref[:, c : c + step].astype(jnp.float32)).astype(jnp.bfloat16))
        got = dot(mover, jnp.concatenate(parts, axis=0)).astype(jnp.bfloat16)
        for k in range(count):
            refs[k][:, c : c + step] = got[k * block : (k + 1) * block, :]


def load_kernel(half, place_ref, _, gate_hbm, up_hbm, down_hbm, *refs):
    sems = refs[-1]
    first = pl.multiple_of(place_ref[1] * half, 8)
    copies = []
    for e in range(gate_hbm.shape[0]):
        sources = [gate_hbm.at[e], up_hbm.at[e], down_hbm.at[e, pl.ds(first, half), :]]
        for source in sources:
            at = len(copies)
            copies.append(pltpu.make_async_copy(source, refs[at], sems.at[at]))
    for copy in copies:
        copy.start()
    for copy in copies:
        copy.wait()


def ffn_kernel(padded, pieces, mine_ref, *refs):
    theirs, refs = refs[:pieces], refs[pieces:]
    weights, own_ref, sends = refs[: -1 - pieces], refs[-1 - pieces], refs[-pieces:]
    each = len(weights) // 3 // pieces
    for e in range(len(weights) // 3):
        gate_ref, up_ref, down_ref = weights[3 * e : 3 * e + 3]
        at = slice(e * padded, (e + 1) * padded)
        low = slice((e % each) * padded, (e % each + 1) * padded)
        rows = jnp.concatenate([mine_ref[at, :], theirs[e // each][low, :]], axis=0)
        gate = dot_nt(rows, gate_ref[...])
        up = dot_nt(rows, up_ref[...])
        hidden = (gate / (1.0 + jnp.exp(-gate)) * up).astype(jnp.bfloat16)
        part = dot(hidden, down_ref[...])
        own_ref[at, :] = part[:padded, :]
        sends[e // each][low, :] = part[padded:, :].astype(jnp.bfloat16)


def combine_kernel(block, route_ref, *refs):
    groups = len(refs) - 2
    ins, out_ref, held = refs[:groups], refs[groups], refs[groups + 1]
    for g in range(groups):
        held[g * block : (g + 1) * block, :] = ins[g][...]
    rows = route_ref.shape[0]
    place = iota((rows, groups * block), 1)
    slots = [route_ref[:, k : k + 1].astype(jnp.int32) for k in range(TOPK)]
    gates = [route_ref[:, TOPK + k : TOPK + k + 1] for k in range(TOPK)]
    picks = [(place == s).astype(jnp.bfloat16) for s in slots]
    step = 512
    for c in range(0, out_ref.shape[1], step):
        part = held[:, c : c + step]
        total = sum(gates[k] * dot(picks[k], part) for k in range(TOPK))
        out_ref[:, c : c + step] = total.astype(jnp.bfloat16)


def params(limit):
    return pltpu.CompilerParams(vmem_limit_bytes=limit * MIB)


def cost(flops, moved):
    return pl.CostEstimate(flops=flops, bytes_accessed=moved, transcendentals=0)


def whole(count):
    return [pl.BlockSpec(memory_space=VMEM)] * count


def fast(tokens, route_ids, route_gates, gate_weight, up_weight, down_weight):
    rows, width = tokens.shape
    groups = lax.axis_size("expert")
    local_experts, _, half = gate_weight.shape
    block = local_experts * CAP
    bf16 = jnp.bfloat16
    place = jnp.stack([lax.axis_index("expert"), lax.axis_index("dp")]).astype(jnp.int32)
    smem = pl.BlockSpec(memory_space=pltpu.SMEM)
    hbm = pl.BlockSpec(memory_space=pltpu.HBM)
    gate_rows = pltpu.with_memory_space_constraint(jnp.swapaxes(gate_weight, 1, 2), pltpu.HBM)
    up_rows = pltpu.with_memory_space_constraint(jnp.swapaxes(up_weight, 1, 2), pltpu.HBM)
    down_weight = pltpu.with_memory_space_constraint(down_weight, pltpu.HBM)

    packed = pl.pallas_call(
        functools.partial(pack_kernel, local_experts, groups),
        out_shape=[jax.ShapeDtypeStruct((rows, rows), jnp.float32)]
        + [jax.ShapeDtypeStruct((block, width), bf16)] * groups,
        in_specs=[smem] + whole(3),
        out_specs=whole(1 + groups),
        compiler_params=params(4),
        cost_estimate=cost(2 * groups * block * rows * width, 2 * 3 * rows * width),
        name="pack",
    )(place, route_ids.T, route_gates.T, tokens)
    route, outgoing = packed[0], packed[1:]

    def hop(x, k):
        return lax.ppermute(x, "expert", [(i, i ^ k) for i in range(groups)])

    def swap(x):
        return lax.ppermute(x, "dp", [(0, 1), (1, 0)])

    order = [1, 2, 3, 4, 5, 6, 7]
    after = {6: 1, 7: 2}
    chunks = [[0, 1, 2, 3, 4, 5], [6, 7]]
    incoming = {0: outgoing[0]}
    for k in order:
        held = outgoing[k]
        if k in after:
            held, _ = lax.optimization_barrier((held, incoming[after[k]]))
        incoming[k] = hop(held, k)
    route_now, _, _ = lax.optimization_barrier((route, incoming[1], incoming[2]))

    share = jax.ShapeDtypeStruct((half, width), bf16)
    pieces = 3 * local_experts
    weights = pl.pallas_call(
        functools.partial(load_kernel, half),
        out_shape=[share] * pieces,
        in_specs=[smem] + whole(1) + [hbm] * 3,
        out_specs=whole(pieces),
        scratch_shapes=[pltpu.SemaphoreType.DMA((pieces,))],
        compiler_params=params(1),
        cost_estimate=cost(0, 6 * local_experts * half * width),
        name="load",
    )(place, route_now, gate_rows, up_rows, down_weight)
    incoming[4], gate_now = lax.optimization_barrier((incoming[4], weights[0]))
    weights = [gate_now] + list(weights[1:])

    returned = {}
    last = None
    for chunk in chunks:
        count = len(chunk)
        padded = 1 << (count * CAP - 1).bit_length()
        tall = local_experts * padded
        splits = SPLITS[0] if count > 2 else SPLITS[1]
        piece = jax.ShapeDtypeStruct((tall // splits, width), bf16)
        mine, *cut = pl.pallas_call(
            functools.partial(regroup_kernel, local_experts, count, padded),
            out_shape=[jax.ShapeDtypeStruct((tall, width), bf16)] + [piece] * splits,
            in_specs=whole(count),
            out_specs=whole(1 + splits),
            scratch_shapes=[VMEM((count * block, width), bf16)],
            compiler_params=params(4),
            cost_estimate=cost(2 * tall * count * block * width, 4 * tall * width),
            name="regroup",
        )(*[incoming[k] for k in chunk])
        theirs = [swap(x) for x in cut]
        own, *send = pl.pallas_call(
            functools.partial(ffn_kernel, padded, splits),
            out_shape=[
                jax.ShapeDtypeStruct((tall, width), jnp.float32),
            ]
            + [piece] * splits,
            in_specs=whole(1 + splits + pieces),
            out_specs=whole(1 + splits),
            compiler_params=params(6),
            cost_estimate=cost(12 * tall * width * half, 6 * local_experts * half * width),
            name="ffn",
        )(mine, *theirs, *weights)
        other = [swap(x) for x in send]
        blocks = pl.pallas_call(
            functools.partial(ungroup_kernel, local_experts, count, padded),
            out_shape=[jax.ShapeDtypeStruct((block, width), bf16)] * count,
            in_specs=whole(1 + splits),
            out_specs=whole(count),
            compiler_params=params(4),
            cost_estimate=cost(2 * tall * count * block * width, 4 * tall * width),
            name="ungroup",
        )(own, *other)
        last = blocks[0]
        for k, y in zip(chunk, blocks):
            returned[k] = hop(y, k) if k else y

    return pl.pallas_call(
        functools.partial(combine_kernel, block),
        out_shape=jax.ShapeDtypeStruct((rows, width), bf16),
        in_specs=whole(1 + groups),
        out_specs=whole(1)[0],
        scratch_shapes=[VMEM((groups * block, width), bf16)],
        compiler_params=params(4),
        cost_estimate=cost(4 * rows * groups * block * width, 4 * rows * width),
        name="combine",
    )(route, *[returned[k] for k in range(groups)])


def on_device(tokens, route_ids, route_gates, gate_weight, up_weight, down_weight):
    suits = (
        lax.axis_size("expert") == 8
        and lax.axis_size("dp") == 2
        and down_weight.shape[1] == FF
        and gate_weight.shape[0] == 4
        and tokens.shape[0] == 128
    )
    run = fast if suits else general
    return run(tokens, route_ids, route_gates, gate_weight, up_weight, down_weight)


def solution(mesh):
    placed = (
        P(("parts", "expert", "dp"), None),
        P(("parts", "expert", "dp"), None),
        P(("parts", "expert", "dp"), None),
        P("expert", None, "dp"),
        P("expert", None, "dp"),
        P("expert", None, None),
    )
    return jax.shard_map(
        on_device,
        mesh=mesh,
        in_specs=placed,
        out_specs=P(("parts", "expert", "dp"), None),
        check_vma=False,
    )
```

time: 118 us -> 97.4 us (0.83)
  waiting for transfers between devices: 34.2 us -> 16.6 us
  local copies, waits for them, and re-layouts: 6.22 us -> 2.4 us
  starting transfers between devices: 41 us -> 43.8 us
  Pallas kernels: 36 us -> 34.2 us
    ppermute x14, waiting for transfers between devices: 32.3 us -> 16.2 us  [hop(): return lax.ppermute(x, 'expert', [(i, i ^ k) for i in range(groups)])]
    unnamed x10 -> x6, local copies, waits for them, and re-layouts: 6.22 us -> 2.4 us
    ppermute x4 -> x16, starting transfers between devices: 0.8 us -> 4.26 us  [swap(): return lax.ppermute(x, 'dp', [(0, 1), (1, 0)])]
    ppermute x4 -> x16, waiting for transfers between devices: 1.89 us -> 0.42 us  [swap(): return lax.ppermute(x, 'dp', [(0, 1), (1, 0)])]
    pallas_call x2 -> x3, Pallas kernels: 31.4 us -> 30 us  [the longest x2 18.3 us: fast(): pl.pallas_call(functools.partial(ffn_kernel, padded, splits), out_shape=[...]
  transfers between devices with their start and end apart: 18 -> 30, of which waited for: 10 -> 6; matrix products, arithmetic and copies ran while one was open for 0% -> 0% of each run, Pallas kernels for 28% -> 32%
where the time goes in v2:
time: 97.4 us; the launch traced here: 97.2 us
  starting transfers between devices  43.8 us (45%)
  Pallas kernels  34.2 us (35%)
  waiting for transfers between devices  16.6 us (17%)
  local copies, waits for them, and re-layouts  2.4 us (2%)
    ppermute x14, starting transfers between devices, hop(): return lax.ppermute(x, 'expert', [(i, i ^ k) for i in range(groups)])  39.6 us
    pallas_call x2, Pallas kernels, fast(): pl.pallas_call(functools.partial(ffn_kernel, padded, splits), out_shape=[...  18.3 us
    ppermute x14, waiting for transfers between devices, hop(): return lax.ppermute(x, 'expert', [(i, i ^ k) for i in range(groups)])  16.2 us
    pallas_call x1, Pallas kernels, fast(): pl.pallas_call(functools.partial(load_kernel, half), out_shape=[share] *...  11.7 us
    ppermute x16, starting transfers between devices, swap(): return lax.ppermute(x, 'dp', [(0, 1), (1, 0)])  4.26 us
    unnamed x6, local copies, waits for them, and re-layouts  2.4 us
  transfers between devices with their start and end apart: 30, of which 6 were waited for; matrix products, arithmetic and copies ran while one was open for 0% of the time, Pallas kernels for 32%

profile of v2, /device:TPU:0, one launch (start us, length us, event | category | flops | bytes accessed | tf_op | source)
XLA Modules:
  0.0 97.2 jit_solution(16997157896516339108)
XLA Ops:
  0.0 0.1 pad_add_fusion.place_ref
  0.1 1.0 %copy-done = bf16[128,2048]{1,0:T(8,128)(2,1)S(1)} copy-done((bf16[128,2048]{1,0:T(8,128)(2,1)S(1)}, bf16[128,2048]{1,0:T(8,128)(2,1)}, u32[]{:S(2)}) %copy-start) | copy-done | bytes 524312
  1.1 0.7 copy-done.1
  1.8 0.7 copy-done.2
  2.5 1.2 %pack.1 = (f32[128,128]{1,0:T(8,128)S(1)}, bf16[40,2048]{1,0:T(8,128)(2,1)S(1)}, bf16[40,2048]{1,0:T(8,128)(2,1)S(1)}, bf16[40,2048]{1,0:T(8,128)(2,1)S(1)}, bf1...) custom-call(s32[2]{0:T(128)S(1)} %pad_add_fusion.place_ref, ...), custom_call_target="tpu_custom_call" | custom-call | flops 167772160 | bytes 1572864 | tf_op jit(solution)/shard_map/pack/pallas_call | solution.py:221
  3.7 3.0 %collective-permute-start = (bf16[40,2048]{1,0:T(8,128)(2,1)S(1)}, bf16[40,2048]{1,0:T(8,128)(2,1)S(1)}, u32[]{:S(2)}, u32[]{:S(2)}) collective-permute-start(bf16[40,2048]{1,0:T(8,128)(2,1)S(1)} %get-tuple-element.61), channel_id=1, source_target_pairs={{0,2},{2,0},{4,6},{6,4},{8,10},{10,8},{12,14},{14,12},{1,3},{3,1},... | collective-permute-start | bytes 491528 | tf_op jit(solution)/shard_map/ppermute | solution.py:234
  6.7 1.6 %collective-permute-start.1 = (bf16[40,2048]{1,0:T(8,128)(2,1)S(1)}, bf16[40,2048]{1,0:T(8,128)(2,1)S(1)}, u32[]{:S(2)}, u32[]{:S(2)}) collective-permute-start(bf16[40,2048]{1,0:T(8,128)(2,1)S(1)} %get-tuple-element.62), channel_id=1, source_target_pairs={{0,4},{2,6},{4,0},{6,2},{8,12},{10,14},{12,8},{14,10},{1,5},{3,7},... | collective-permute-start | bytes 491528 | tf_op jit(solution)/shard_map/ppermute | solution.py:234
  8.2 2.6 %collective-permute-start.3 = (bf16[40,2048]{1,0:T(8,128)(2,1)S(1)}, bf16[40,2048]{1,0:T(8,128)(2,1)S(1)}, u32[]{:S(2)}, u32[]{:S(2)}) collective-permute-start(bf16[40,2048]{1,0:T(8,128)(2,1)S(1)} %get-tuple-element.64), channel_id=1, source_target_pairs={{0,8},{2,10},{4,12},{6,14},{8,0},{10,2},{12,4},{14,6},{1,9},{3,11}... | collective-permute-start | bytes 491528 | tf_op jit(solution)/shard_map/ppermute | solution.py:234
  10.8 0.4 collective-permute-start.2
  11.3 1.3 %collective-permute-start.4 = (bf16[40,2048]{1,0:T(8,128)(2,1)S(1)}, bf16[40,2048]{1,0:T(8,128)(2,1)S(1)}, u32[]{:S(2)}, u32[]{:S(2)}) collective-permute-start(bf16[40,2048]{1,0:T(8,128)(2,1)S(1)} %get-tuple-element.68), channel_id=1, source_target_pairs={{0,10},{2,8},{4,14},{6,12},{8,2},{10,0},{12,6},{14,4},{1,11},{3,9}... | collective-permute-start | bytes 491528 | tf_op jit(solution)/shard_map/ppermute | solution.py:234
  12.5 0.0 collective-permute-done.refs_1_
  12.5 3.6 %collective-permute-start.18 = (bf16[40,2048]{1,0:T(8,128)(2,1)S(1)}, bf16[40,2048]{1,0:T(8,128)(2,1)S(1)}, u32[]{:S(2)}, u32[]{:S(2)}) collective-permute-start(bf16[40,2048]{1,0:T(8,128)(2,1)S(1)} %get-tuple-element.98), channel_id=1, source_target_pairs={{0,12},{2,14},{4,8},{6,10},{8,4},{10,6},{12,0},{14,2},{1,13},{3,15... | collective-permute-start | bytes 491528 | tf_op jit(solution)/shard_map/ppermute | solution.py:234
  16.1 1.0 %collective-permute-done.1.refs_2_ = bf16[40,2048]{1,0:T(8,128)(2,1)S(1)} collective-permute-done((bf16[40,2048]{1,0:T(8,128)(2,1)S(1)}, bf16[40,2048]{1,0:T(8,128)(2,1)S(1)}, u32[]{:S(2)}, u32[]{:S(2)}) %collective-permute-start.1) | collective-permute-done | bytes 163872 | tf_op jit(solution)/shard_map/ppermute | solution.py:234
  17.1 11.7 %load.1 = (bf16[704,2048]{1,0:T(8,128)(2,1)S(1)}, bf16[704,2048]{1,0:T(8,128)(2,1)S(1)}, bf16[704,2048]{1,0:T(8,128)(2,1)S(1)}, bf16[704,2048]{1,0:T(8,128)(2,1)...) custom-call(s32[2]{0:T(128)S(1)} %pad_add_fusion.place_ref, ...), custom_call_target="tpu_custom_call" | custom-call | bytes 34603008 | tf_op jit(solution)/shard_map/load/pallas_call | solution.py:252
  28.8 0.0 collective-permute-done.3.refs_4_
  28.9 0.0 collective-permute-done.2.refs_3_
  28.9 0.6 collective-permute-done.4.refs_5_
  29.4 0.5 regroup.2
  29.9 0.1 collective-permute-start.5
  30.0 0.5 collective-permute-start.6
  30.5 0.1 collective-permute-start.7
  30.6 0.4 collective-permute-start.8
  31.0 0.0 collective-permute-done.18.refs_0_
  31.0 3.9 %collective-permute-start.19 = (bf16[40,2048]{1,0:T(8,128)(2,1)S(1)}, bf16[40,2048]{1,0:T(8,128)(2,1)S(1)}, u32[]{:S(2)}, u32[]{:S(2)}) collective-permute-start(bf16[40,2048]{1,0:T(8,128)(2,1)S(1)} %get-tuple-element.100), channel_id=1, source_target_pairs={{0,14},{2,12},{4,10},{6,8},{8,6},{10,4},{12,2},{14,0},{1,15},{3,13... | collective-permute-start | bytes 491528 | tf_op jit(solution)/shard_map/ppermute | solution.py:234
  34.9 5.0 %collective-permute-done.19.refs_1_ = bf16[40,2048]{1,0:T(8,128)(2,1)S(1)} collective-permute-done((bf16[40,2048]{1,0:T(8,128)(2,1)S(1)}, bf16[40,2048]{1,0:T(8,128)(2,1)S(1)}, u32[]{:S(2)}, u32[]{:S(2)}) %collective-permute-start.19) | collective-permute-done | bytes 163872 | tf_op jit(solution)/shard_map/ppermute | solution.py:234
  40.0 0.3 regroup.3
  40.3 0.1 collective-permute-start.20
  40.3 0.0 collective-permute-done.5.refs_0_
  40.4 0.5 collective-permute-start.21
  40.8 0.0 collective-permute-done.6.refs_1_
  40.9 0.1 collective-permute-start.22
  40.9 0.0 collective-permute-done.7.refs_2_
  40.9 0.4 collective-permute-start.23
  41.4 9.1 %ffn.2 = (f32[256,2048]{1,0:T(8,128)S(1)}, bf16[64,2048]{1,0:T(8,128)(2,1)S(1)}, bf16[64,2048]{1,0:T(8,128)(2,1)S(1)}, bf16[64,2048]{1,0:T(8,128)(2,1)S(1)}, bf16[64,2048]{1,0:T(8,128)(2,1)S(1)}) custom-call(bf16[256,2048]{1,0:T(8,128)(2,1)S(1)} %get-tuple-element.69.mine_ref, bf16[64,2048]{1,0:T(8,128)(2,1)S(1)} %collective-permute-done.5.refs_0_, ...), custom_call_target="tpu_custom_call" | custom-call | flops 4429185024 | bytes 34603008 | tf_op jit(solution)/shard_map/ffn/pallas_call | solution.py:284
  50.5 0.2 collective-permute-start.9
  50.7 0.0 collective-permute-done.20.refs_0_
  50.7 0.0 collective-permute-done.21.refs_1_
  50.7 0.0 collective-permute-done.23.refs_3_
  50.7 9.1 %ffn.3 = (f32[128,2048]{1,0:T(8,128)S(1)}, bf16[32,2048]{1,0:T(8,128)(2,1)S(1)}, bf16[32,2048]{1,0:T(8,128)(2,1)S(1)}, bf16[32,2048]{1,0:T(8,128)(2,1)S(1)}, bf16[32,2048]{1,0:T(8,128)(2,1)S(1)}) custom-call(bf16[128,2048]{1,0:T(8,128)(2,1)S(1)} %get-tuple-element.101.mine_ref, bf16[32,2048]{1,0:T(8,128)(2,1)S(1)} %collective-permute-done.20.refs_0_, ...), custom_call_target="tpu_custom_call" | custom-call | flops 2214592512 | bytes 34603008 | tf_op jit(solution)/shard_map/ffn/pallas_call | solution.py:284
  59.8 0.5 collective-permute-start.24
  60.3 0.1 collective-permute-start.25
  60.4 0.4 collective-permute-start.26
  60.8 0.1 collective-permute-start.27
  60.9 0.4 collective-permute-done.24.refs_0_
  61.3 0.4 collective-permute-start.10
  61.7 0.0 collective-permute-done.25.refs_1_
  61.7 0.2 collective-permute-start.11
  61.8 0.3 collective-permute-start.12
  62.2 0.3 ungroup.3
  62.4 4.0 %collective-permute-start.28 = (bf16[40,2048]{1,0:T(8,128)(2,1)S(1)}, bf16[40,2048]{1,0:T(8,128)(2,1)S(1)}, u32[]{:S(2)}, u32[]{:S(2)}) collective-permute-start(bf16[40,2048]{1,0:T(8,128)(2,1)S(1)} %get-tuple-element.111), channel_id=1, source_target_pairs={{0,12},{2,14},{4,8},{6,10},{8,4},{10,6},{12,0},{14,2},{1,13},{3,15... | collective-permute-start | bytes 491528 | tf_op jit(solution)/shard_map/ppermute | solution.py:234
  66.4 0.0 collective-permute-done.9.refs_0_
  66.4 0.8 collective-permute-start.29
  67.3 0.0 collective-permute-done.12.refs_3_
  67.3 0.5 ungroup.2
  67.8 0.8 collective-permute-start.13
  68.5 0.5 collective-permute-start.14
  69.0 2.3 %collective-permute-start.15 = (bf16[40,2048]{1,0:T(8,128)(2,1)S(1)}, bf16[40,2048]{1,0:T(8,128)(2,1)S(1)}, u32[]{:S(2)}, u32[]{:S(2)}) collective-permute-start(bf16[40,2048]{1,0:T(8,128)(2,1)S(1)} %get-tuple-element.94), channel_id=1, source_target_pairs={{0,6},{2,4},{4,2},{6,0},{8,14},{10,12},{12,10},{14,8},{1,7},{3,5},... | collective-permute-start | bytes 491528 | tf_op jit(solution)/shard_map/ppermute | solution.py:234
  71.3 8.7 %collective-permute-start.16 = (bf16[40,2048]{1,0:T(8,128)(2,1)S(1)}, bf16[40,2048]{1,0:T(8,128)(2,1)S(1)}, u32[]{:S(2)}, u32[]{:S(2)}) collective-permute-start(bf16[40,2048]{1,0:T(8,128)(2,1)S(1)} %get-tuple-element.95), channel_id=1, source_target_pairs={{0,8},{2,10},{4,12},{6,14},{8,0},{10,2},{12,4},{14,6},{1,9},{3,11}... | collective-permute-start | bytes 491528 | tf_op jit(solution)/shard_map/ppermute | solution.py:234
  80.1 6.0 %collective-permute-start.17 = (bf16[40,2048]{1,0:T(8,128)(2,1)S(1)}, bf16[40,2048]{1,0:T(8,128)(2,1)S(1)}, u32[]{:S(2)}, u32[]{:S(2)}) collective-permute-start(bf16[40,2048]{1,0:T(8,128)(2,1)S(1)} %get-tuple-element.96), channel_id=1, source_target_pairs={{0,10},{2,8},{4,14},{6,12},{8,2},{10,0},{12,6},{14,4},{1,11},{3,9}... | collective-permute-start | bytes 491528 | tf_op jit(solution)/shard_map/ppermute | solution.py:234
  86.1 0.0 collective-permute-done.14.refs_2_
  86.1 0.0 collective-permute-done.15.refs_3_
  86.1 6.6 %collective-permute-done.16.refs_4_ = bf16[40,2048]{1,0:T(8,128)(2,1)S(1)} collective-permute-done((bf16[40,2048]{1,0:T(8,128)(2,1)S(1)}, bf16[40,2048]{1,0:T(8,128)(2,1)S(1)}, u32[]{:S(2)}, u32[]{:S(2)}) %collective-permute-start.16) | collective-permute-done | bytes 163872 | tf_op jit(solution)/shard_map/ppermute | solution.py:234
  92.7 2.9 %collective-permute-done.17.refs_5_ = bf16[40,2048]{1,0:T(8,128)(2,1)S(1)} collective-permute-done((bf16[40,2048]{1,0:T(8,128)(2,1)S(1)}, bf16[40,2048]{1,0:T(8,128)(2,1)S(1)}, u32[]{:S(2)}, u32[]{:S(2)}) %collective-permute-start.17) | collective-permute-done | bytes 163872 | tf_op jit(solution)/shard_map/ppermute | solution.py:234
  95.7 1.6 %combine.1 = bf16[128,2048]{1,0:T(8,128)(2,1)} custom-call(f32[128,128]{1,0:T(8,128)S(1)} %get-tuple-element.65._.route_ref, bf16[40,2048]{1,0:T(8,128)(2,1)S(1)} %get-tuple-element.91.refs_0_, bf16[40,2048]{1,0:T(8,128)(2,1)S(1)} %collective-permute-done.13.refs_1_, bf16[40,2048]{1,0:T(8,128)(2,1)S(1)} %collective-permute-done.14.refs_2_, ...), custom_call_target="tpu_custom_call" | custom-call | flops 335544320 | bytes 1048576 | tf_op jit(solution)/shard_map/combine/pallas_call | solution.py:310
  (12 shorter events, 0.0 us)
Async XLA Ops:
  0.1 1.0 %copy-start = (bf16[128,2048]{1,0:T(8,128)(2,1)S(1)}, bf16[128,2048]{1,0:T(8,128)(2,1)}, u32[]{:S(2)}) copy-start(bf16[128,2048]{1,0:T(8,128)(2,1)} %tokens_ref.1) | copy-start | bytes 1572868
  1.1 0.7 copy-start.1
  1.8 0.7 copy-start.2
  3.7 8.9 %collective-permute-start = (bf16[40,2048]{1,0:T(8,128)(2,1)S(1)}, bf16[40,2048]{1,0:T(8,128)(2,1)S(1)}, u32[]{:S(2)}, u32[]{:S(2)}) collective-permute-start(bf16[40,2048]{1,0:T(8,128)(2,1)S(1)} %get-tuple-element.61), channel_id=1, source_target_pairs={{0,2},{2,0},{4,6},{6,4},{8,10},{10,8},{12,14},{14,12},{1,3},{3,1},... | collective-permute-start | bytes 491528 | tf_op jit(solution)/shard_map/ppermute | solution.py:234
  6.7 10.5 %collective-permute-start.1 = (bf16[40,2048]{1,0:T(8,128)(2,1)S(1)}, bf16[40,2048]{1,0:T(8,128)(2,1)S(1)}, u32[]{:S(2)}, u32[]{:S(2)}) collective-permute-start(bf16[40,2048]{1,0:T(8,128)(2,1)S(1)} %get-tuple-element.62), channel_id=1, source_target_pairs={{0,4},{2,6},{4,0},{6,2},{8,12},{10,14},{12,8},{14,10},{1,5},{3,7},... | collective-permute-start | bytes 491528 | tf_op jit(solution)/shard_map/ppermute | solution.py:234
  8.2 20.6 %collective-permute-start.3 = (bf16[40,2048]{1,0:T(8,128)(2,1)S(1)}, bf16[40,2048]{1,0:T(8,128)(2,1)S(1)}, u32[]{:S(2)}, u32[]{:S(2)}) collective-permute-start(bf16[40,2048]{1,0:T(8,128)(2,1)S(1)} %get-tuple-element.64), channel_id=1, source_target_pairs={{0,8},{2,10},{4,12},{6,14},{8,0},{10,2},{12,4},{14,6},{1,9},{3,11}... | collective-permute-start | bytes 491528 | tf_op jit(solution)/shard_map/ppermute | solution.py:234
  10.8 18.0 %collective-permute-start.2 = (bf16[40,2048]{1,0:T(8,128)(2,1)S(1)}, bf16[40,2048]{1,0:T(8,128)(2,1)S(1)}, u32[]{:S(2)}, u32[]{:S(2)}) collective-permute-start(bf16[40,2048]{1,0:T(8,128)(2,1)S(1)} %get-tuple-element.63), channel_id=1, source_target_pairs={{0,6},{2,4},{4,2},{6,0},{8,14},{10,12},{12,10},{14,8},{1,7},{3,5},... | collective-permute-start | bytes 491528 | tf_op jit(solution)/shard_map/ppermute | solution.py:234
  11.3 18.2 %collective-permute-start.4 = (bf16[40,2048]{1,0:T(8,128)(2,1)S(1)}, bf16[40,2048]{1,0:T(8,128)(2,1)S(1)}, u32[]{:S(2)}, u32[]{:S(2)}) collective-permute-start(bf16[40,2048]{1,0:T(8,128)(2,1)S(1)} %get-tuple-element.68), channel_id=1, source_target_pairs={{0,10},{2,8},{4,14},{6,12},{8,2},{10,0},{12,6},{14,4},{1,11},{3,9}... | collective-permute-start | bytes 491528 | tf_op jit(solution)/shard_map/ppermute | solution.py:234
  12.5 18.5 %collective-permute-start.18 = (bf16[40,2048]{1,0:T(8,128)(2,1)S(1)}, bf16[40,2048]{1,0:T(8,128)(2,1)S(1)}, u32[]{:S(2)}, u32[]{:S(2)}) collective-permute-start(bf16[40,2048]{1,0:T(8,128)(2,1)S(1)} %get-tuple-element.98), channel_id=1, source_target_pairs={{0,12},{2,14},{4,8},{6,10},{8,4},{10,6},{12,0},{14,2},{1,13},{3,15... | collective-permute-start | bytes 491528 | tf_op jit(solution)/shard_map/ppermute | solution.py:234
  29.9 10.4 %collective-permute-start.5 = (bf16[64,2048]{1,0:T(8,128)(2,1)S(1)}, bf16[64,2048]{1,0:T(8,128)(2,1)S(1)}, u32[]{:S(2)}, u32[]{:S(2)}) collective-permute-start(bf16[64,2048]{1,0:T(8,128)(2,1)S(1)} %get-tuple-element.70), channel_id=1, source_target_pairs={{0,1},{1,0},{2,3},{3,2},{4,5},{5,4},{6,7},{7,6},{8,9},{9,8},{10,11... | collective-permute-start | bytes 786440 | tf_op jit(solution)/shard_map/ppermute | solution.py:237
  30.0 10.9 %collective-permute-start.6 = (bf16[64,2048]{1,0:T(8,128)(2,1)S(1)}, bf16[64,2048]{1,0:T(8,128)(2,1)S(1)}, u32[]{:S(2)}, u32[]{:S(2)}) collective-permute-start(bf16[64,2048]{1,0:T(8,128)(2,1)S(1)} %get-tuple-element.71), channel_id=1, source_target_pairs={{0,1},{1,0},{2,3},{3,2},{4,5},{5,4},{6,7},{7,6},{8,9},{9,8},{10,11... | collective-permute-start | bytes 786440 | tf_op jit(solution)/shard_map/ppermute | solution.py:237
  30.5 10.5 %collective-permute-start.7 = (bf16[64,2048]{1,0:T(8,128)(2,1)S(1)}, bf16[64,2048]{1,0:T(8,128)(2,1)S(1)}, u32[]{:S(2)}, u32[]{:S(2)}) collective-permute-start(bf16[64,2048]{1,0:T(8,128)(2,1)S(1)} %get-tuple-element.72), channel_id=1, source_target_pairs={{0,1},{1,0},{2,3},{3,2},{4,5},{5,4},{6,7},{7,6},{8,9},{9,8},{10,11... | collective-permute-start | bytes 786440 | tf_op jit(solution)/shard_map/ppermute | solution.py:237
  30.6 10.8 %collective-permute-start.8 = (bf16[64,2048]{1,0:T(8,128)(2,1)S(1)}, bf16[64,2048]{1,0:T(8,128)(2,1)S(1)}, u32[]{:S(2)}, u32[]{:S(2)}) collective-permute-start(bf16[64,2048]{1,0:T(8,128)(2,1)S(1)} %get-tuple-element.73), channel_id=1, source_target_pairs={{0,1},{1,0},{2,3},{3,2},{4,5},{5,4},{6,7},{7,6},{8,9},{9,8},{10,11... | collective-permute-start | bytes 786440 | tf_op jit(solution)/shard_map/ppermute | solution.py:237
  31.0 9.0 %collective-permute-start.19 = (bf16[40,2048]{1,0:T(8,128)(2,1)S(1)}, bf16[40,2048]{1,0:T(8,128)(2,1)S(1)}, u32[]{:S(2)}, u32[]{:S(2)}) collective-permute-start(bf16[40,2048]{1,0:T(8,128)(2,1)S(1)} %get-tuple-element.100), channel_id=1, source_target_pairs={{0,14},{2,12},{4,10},{6,8},{8,6},{10,4},{12,2},{14,0},{1,15},{3,13... | collective-permute-start | bytes 491528 | tf_op jit(solution)/shard_map/ppermute | solution.py:234
  40.3 10.4 %collective-permute-start.20 = (bf16[32,2048]{1,0:T(8,128)(2,1)S(1)}, bf16[32,2048]{1,0:T(8,128)(2,1)S(1)}, u32[]{:S(2)}, u32[]{:S(2)}) collective-permute-start(bf16[32,2048]{1,0:T(8,128)(2,1)S(1)} %get-tuple-element.102), channel_id=1, source_target_pairs={{0,1},{1,0},{2,3},{3,2},{4,5},{5,4},{6,7},{7,6},{8,9},{9,8},{10,11... | collective-permute-start | bytes 393224 | tf_op jit(solution)/shard_map/ppermute | solution.py:237
  40.4 10.3 %collective-permute-start.21 = (bf16[32,2048]{1,0:T(8,128)(2,1)S(1)}, bf16[32,2048]{1,0:T(8,128)(2,1)S(1)}, u32[]{:S(2)}, u32[]{:S(2)}) collective-permute-start(bf16[32,2048]{1,0:T(8,128)(2,1)S(1)} %get-tuple-element.103), channel_id=1, source_target_pairs={{0,1},{1,0},{2,3},{3,2},{4,5},{5,4},{6,7},{7,6},{8,9},{9,8},{10,11... | collective-permute-start | bytes 393224 | tf_op jit(solution)/shard_map/ppermute | solution.py:237
  40.9 9.8 %collective-permute-start.22 = (bf16[32,2048]{1,0:T(8,128)(2,1)S(1)}, bf16[32,2048]{1,0:T(8,128)(2,1)S(1)}, u32[]{:S(2)}, u32[]{:S(2)}) collective-permute-start(bf16[32,2048]{1,0:T(8,128)(2,1)S(1)} %get-tuple-element.104), channel_id=1, source_target_pairs={{0,1},{1,0},{2,3},{3,2},{4,5},{5,4},{6,7},{7,6},{8,9},{9,8},{10,11... | collective-permute-start | bytes 393224 | tf_op jit(solution)/shard_map/ppermute | solution.py:237
  40.9 9.7 %collective-permute-start.23 = (bf16[32,2048]{1,0:T(8,128)(2,1)S(1)}, bf16[32,2048]{1,0:T(8,128)(2,1)S(1)}, u32[]{:S(2)}, u32[]{:S(2)}) collective-permute-start(bf16[32,2048]{1,0:T(8,128)(2,1)S(1)} %get-tuple-element.105), channel_id=1, source_target_pairs={{0,1},{1,0},{2,3},{3,2},{4,5},{5,4},{6,7},{7,6},{8,9},{9,8},{10,11... | collective-permute-start | bytes 393224 | tf_op jit(solution)/shard_map/ppermute | solution.py:237
  50.5 15.9 %collective-permute-start.9 = (bf16[64,2048]{1,0:T(8,128)(2,1)S(1)}, bf16[64,2048]{1,0:T(8,128)(2,1)S(1)}, u32[]{:S(2)}, u32[]{:S(2)}) collective-permute-start(bf16[64,2048]{1,0:T(8,128)(2,1)S(1)} %get-tuple-element.87), channel_id=1, source_target_pairs={{0,1},{1,0},{2,3},{3,2},{4,5},{5,4},{6,7},{7,6},{8,9},{9,8},{10,11... | collective-permute-start | bytes 786440 | tf_op jit(solution)/shard_map/ppermute | solution.py:237
  59.8 1.5 %collective-permute-start.24 = (bf16[32,2048]{1,0:T(8,128)(2,1)S(1)}, bf16[32,2048]{1,0:T(8,128)(2,1)S(1)}, u32[]{:S(2)}, u32[]{:S(2)}) collective-permute-start(bf16[32,2048]{1,0:T(8,128)(2,1)S(1)} %get-tuple-element.107), channel_id=1, source_target_pairs={{0,1},{1,0},{2,3},{3,2},{4,5},{5,4},{6,7},{7,6},{8,9},{9,8},{10,11... | collective-permute-start | bytes 393224 | tf_op jit(solution)/shard_map/ppermute | solution.py:237
  60.3 1.4 %collective-permute-start.25 = (bf16[32,2048]{1,0:T(8,128)(2,1)S(1)}, bf16[32,2048]{1,0:T(8,128)(2,1)S(1)}, u32[]{:S(2)}, u32[]{:S(2)}) collective-permute-start(bf16[32,2048]{1,0:T(8,128)(2,1)S(1)} %get-tuple-element.108), channel_id=1, source_target_pairs={{0,1},{1,0},{2,3},{3,2},{4,5},{5,4},{6,7},{7,6},{8,9},{9,8},{10,11... | collective-permute-start | bytes 393224 | tf_op jit(solution)/shard_map/ppermute | solution.py:237
  60.4 1.4 %collective-permute-start.26 = (bf16[32,2048]{1,0:T(8,128)(2,1)S(1)}, bf16[32,2048]{1,0:T(8,128)(2,1)S(1)}, u32[]{:S(2)}, u32[]{:S(2)}) collective-permute-start(bf16[32,2048]{1,0:T(8,128)(2,1)S(1)} %get-tuple-element.109), channel_id=1, source_target_pairs={{0,1},{1,0},{2,3},{3,2},{4,5},{5,4},{6,7},{7,6},{8,9},{9,8},{10,11... | collective-permute-start | bytes 393224 | tf_op jit(solution)/shard_map/ppermute | solution.py:237
  60.8 1.4 %collective-permute-start.27 = (bf16[32,2048]{1,0:T(8,128)(2,1)S(1)}, bf16[32,2048]{1,0:T(8,128)(2,1)S(1)}, u32[]{:S(2)}, u32[]{:S(2)}) collective-permute-start(bf16[32,2048]{1,0:T(8,128)(2,1)S(1)} %get-tuple-element.110), channel_id=1, source_target_pairs={{0,1},{1,0},{2,3},{3,2},{4,5},{5,4},{6,7},{7,6},{8,9},{9,8},{10,11... | collective-permute-start | bytes 393224 | tf_op jit(solution)/shard_map/ppermute | solution.py:237
  61.3 6.0 %collective-permute-start.10 = (bf16[64,2048]{1,0:T(8,128)(2,1)S(1)}, bf16[64,2048]{1,0:T(8,128)(2,1)S(1)}, u32[]{:S(2)}, u32[]{:S(2)}) collective-permute-start(bf16[64,2048]{1,0:T(8,128)(2,1)S(1)} %get-tuple-element.88), channel_id=1, source_target_pairs={{0,1},{1,0},{2,3},{3,2},{4,5},{5,4},{6,7},{7,6},{8,9},{9,8},{10,11... | collective-permute-start | bytes 786440 | tf_op jit(solution)/shard_map/ppermute | solution.py:237
  61.7 5.6 %collective-permute-start.11 = (bf16[64,2048]{1,0:T(8,128)(2,1)S(1)}, bf16[64,2048]{1,0:T(8,128)(2,1)S(1)}, u32[]{:S(2)}, u32[]{:S(2)}) collective-permute-start(bf16[64,2048]{1,0:T(8,128)(2,1)S(1)} %get-tuple-element.89), channel_id=1, source_target_pairs={{0,1},{1,0},{2,3},{3,2},{4,5},{5,4},{6,7},{7,6},{8,9},{9,8},{10,11... | collective-permute-start | bytes 786440 | tf_op jit(solution)/shard_map/ppermute | solution.py:237
  61.8 5.4 %collective-permute-start.12 = (bf16[64,2048]{1,0:T(8,128)(2,1)S(1)}, bf16[64,2048]{1,0:T(8,128)(2,1)S(1)}, u32[]{:S(2)}, u32[]{:S(2)}) collective-permute-start(bf16[64,2048]{1,0:T(8,128)(2,1)S(1)} %get-tuple-element.90), channel_id=1, source_target_pairs={{0,1},{1,0},{2,3},{3,2},{4,5},{5,4},{6,7},{7,6},{8,9},{9,8},{10,11... | collective-permute-start | bytes 786440 | tf_op jit(solution)/shard_map/ppermute | solution.py:237
  62.4 8.9 %collective-permute-start.28 = (bf16[40,2048]{1,0:T(8,128)(2,1)S(1)}, bf16[40,2048]{1,0:T(8,128)(2,1)S(1)}, u32[]{:S(2)}, u32[]{:S(2)}) collective-permute-start(bf16[40,2048]{1,0:T(8,128)(2,1)S(1)} %get-tuple-element.111), channel_id=1, source_target_pairs={{0,12},{2,14},{4,8},{6,10},{8,4},{10,6},{12,0},{14,2},{1,13},{3,15... | collective-permute-start | bytes 491528 | tf_op jit(solution)/shard_map/ppermute | solution.py:234
  66.4 13.6 %collective-permute-start.29 = (bf16[40,2048]{1,0:T(8,128)(2,1)S(1)}, bf16[40,2048]{1,0:T(8,128)(2,1)S(1)}, u32[]{:S(2)}, u32[]{:S(2)}) collective-permute-start(bf16[40,2048]{1,0:T(8,128)(2,1)S(1)} %get-tuple-element.112), channel_id=1, source_target_pairs={{0,14},{2,12},{4,10},{6,8},{8,6},{10,4},{12,2},{14,0},{1,15},{3,13... | collective-permute-start | bytes 491528 | tf_op jit(solution)/shard_map/ppermute | solution.py:234
  67.8 18.3 %collective-permute-start.13 = (bf16[40,2048]{1,0:T(8,128)(2,1)S(1)}, bf16[40,2048]{1,0:T(8,128)(2,1)S(1)}, u32[]{:S(2)}, u32[]{:S(2)}) collective-permute-start(bf16[40,2048]{1,0:T(8,128)(2,1)S(1)} %get-tuple-element.92), channel_id=1, source_target_pairs={{0,2},{2,0},{4,6},{6,4},{8,10},{10,8},{12,14},{14,12},{1,3},{3,1},... | collective-permute-start | bytes 491528 | tf_op jit(solution)/shard_map/ppermute | solution.py:234
  68.5 17.6 %collective-permute-start.14 = (bf16[40,2048]{1,0:T(8,128)(2,1)S(1)}, bf16[40,2048]{1,0:T(8,128)(2,1)S(1)}, u32[]{:S(2)}, u32[]{:S(2)}) collective-permute-start(bf16[40,2048]{1,0:T(8,128)(2,1)S(1)} %get-tuple-element.93), channel_id=1, source_target_pairs={{0,4},{2,6},{4,0},{6,2},{8,12},{10,14},{12,8},{14,10},{1,5},{3,7},... | collective-permute-start | bytes 491528 | tf_op jit(solution)/shard_map/ppermute | solution.py:234
  69.0 17.1 %collective-permute-start.15 = (bf16[40,2048]{1,0:T(8,128)(2,1)S(1)}, bf16[40,2048]{1,0:T(8,128)(2,1)S(1)}, u32[]{:S(2)}, u32[]{:S(2)}) collective-permute-start(bf16[40,2048]{1,0:T(8,128)(2,1)S(1)} %get-tuple-element.94), channel_id=1, source_target_pairs={{0,6},{2,4},{4,2},{6,0},{8,14},{10,12},{12,10},{14,8},{1,7},{3,5},... | collective-permute-start | bytes 491528 | tf_op jit(solution)/shard_map/ppermute | solution.py:234
  71.3 21.4 %collective-permute-start.16 = (bf16[40,2048]{1,0:T(8,128)(2,1)S(1)}, bf16[40,2048]{1,0:T(8,128)(2,1)S(1)}, u32[]{:S(2)}, u32[]{:S(2)}) collective-permute-start(bf16[40,2048]{1,0:T(8,128)(2,1)S(1)} %get-tuple-element.95), channel_id=1, source_target_pairs={{0,8},{2,10},{4,12},{6,14},{8,0},{10,2},{12,4},{14,6},{1,9},{3,11}... | collective-permute-start | bytes 491528 | tf_op jit(solution)/shard_map/ppermute | solution.py:234
  80.1 15.6 %collective-permute-start.17 = (bf16[40,2048]{1,0:T(8,128)(2,1)S(1)}, bf16[40,2048]{1,0:T(8,128)(2,1)S(1)}, u32[]{:S(2)}, u32[]{:S(2)}) collective-permute-start(bf16[40,2048]{1,0:T(8,128)(2,1)S(1)} %get-tuple-element.96), channel_id=1, source_target_pairs={{0,10},{2,8},{4,14},{6,12},{8,2},{10,0},{12,6},{14,4},{1,11},{3,9}... | collective-permute-start | bytes 491528 | tf_op jit(solution)/shard_map/ppermute | solution.py:234

commit v3 on v2

--- a/solution.py
+++ b/solution.py
@@ -11,7 +11,6 @@
 EXPERTS = 32
 CAP = 10
 TOPK = 2
-SPLITS = (4, 4)
 
 
 def general(tokens, route_ids, route_gates, gate_weight, up_weight, down_weight):
@@ -103,45 +102,42 @@
     route_ref[...] = jnp.concatenate(columns, axis=0).T
 
 
-def regroup_kernel(local_experts, count, padded, *refs):
-    ins, out_ref, pieces, held = refs[:count], refs[count], refs[count + 1 : -1], refs[-1]
-    each = local_experts * padded // len(pieces)
-    block = local_experts * CAP
+def regroup_kernel(local_experts, count, *refs):
+    ins, low_ref, high_ref, held = refs[:count], refs[count], refs[count + 1], refs[count + 2]
+    block, each = local_experts * CAP, count * CAP
     for b in range(count):
         held[b * block : (b + 1) * block, :] = ins[b][...]
-    q = iota((local_experts * padded, 1), 0)
-    j = q & (padded - 1)
+    q = iota((local_experts * each, 1), 0)
+    e = sum((q >= k * each).astype(jnp.int32) for k in range(1, local_experts))
+    j = q - e * each
     b = (j * 205) >> 11
-    source = b * block + (q >> (padded.bit_length() - 1)) * CAP + (j - b * CAP)
-    source = jnp.where(j < count * CAP, source, -1)
-    mover = (iota((local_experts * padded, count * block), 1) == source).astype(jnp.bfloat16)
-    step = 512
+    source = b * block + e * CAP + (j - b * CAP)
+    mover = (iota((local_experts * each, count * block), 1) == source).astype(jnp.bfloat16)
+    step, middle = 512, low_ref.shape[0]
     for c in range(0, held.shape[1], step):
         got = dot(mover, held[:, c : c + step]).astype(jnp.bfloat16)
-        out_ref[:, c : c + step] = got
-        for k in range(len(pieces)):
-            pieces[k][:, c : c + step] = got[k * each : (k + 1) * each, :]
-
-
-def ungroup_kernel(local_experts, count, padded, own_ref, *refs):
-    others, refs = refs[:-count], refs[-count:]
-    each = local_experts * padded // len(others)
-    block = local_experts * CAP
+        low_ref[:, c : c + step] = got[:middle, :]
+        high_ref[:, c : c + step] = got[middle:, :]
+
+
+def ungroup_kernel(local_experts, count, own_low, own_high, other_low, other_high, *refs):
+    block, each = local_experts * CAP, count * CAP
     s = iota((count * block, 1), 0)
     b = (s * 1639) >> 16
     t = s - b * block
     e = (t * 205) >> 11
-    source = e * padded + b * CAP + (t - e * CAP)
-    mover = (iota((count * block, local_experts * padded), 1) == source).astype(jnp.bfloat16)
+    source = e * each + b * CAP + (t - e * CAP)
+    mover = (iota((count * block, local_experts * each), 1) == source).astype(jnp.bfloat16)
     step = 512
-    for c in range(0, own_ref.shape[1], step):
-        parts = []
-        for k, other_ref in enumerate(others):
-            part = own_ref[k * each : (k + 1) * each, c : c + step]
-            parts.append((part + other_ref[:, c : c + step].astype(jnp.float32)).astype(jnp.bfloat16))
+    for c in range(0, own_low.shape[1], step):
+        at = slice(c, c + step)
+        parts = [
+            (own[:, at] + other[:, at].astype(jnp.float32)).astype(jnp.bfloat16)
+            for own, other in ((own_low, other_low), (own_high, other_high))
+        ]
         got = dot(mover, jnp.concatenate(parts, axis=0)).astype(jnp.bfloat16)
         for k in range(count):
-            refs[k][:, c : c + step] = got[k * block : (k + 1) * block, :]
+            refs[k][:, at] = got[k * block : (k + 1) * block, :]
 
 
 def load_kernel(half, place_ref, _, gate_hbm, up_hbm, down_hbm, *refs):
@@ -159,21 +155,18 @@
         copy.wait()
 
 
-def ffn_kernel(padded, pieces, mine_ref, *refs):
-    theirs, refs = refs[:pieces], refs[pieces:]
-    weights, own_ref, sends = refs[: -1 - pieces], refs[-1 - pieces], refs[-pieces:]
-    each = len(weights) // 3 // pieces
+def ffn_kernel(padded, mine_ref, theirs_ref, *refs):
+    weights, own_ref, send_ref = refs[:-2], refs[-2], refs[-1]
     for e in range(len(weights) // 3):
         gate_ref, up_ref, down_ref = weights[3 * e : 3 * e + 3]
         at = slice(e * padded, (e + 1) * padded)
-        low = slice((e % each) * padded, (e % each + 1) * padded)
-        rows = jnp.concatenate([mine_ref[at, :], theirs[e // each][low, :]], axis=0)
+        rows = jnp.concatenate([mine_ref[at, :], theirs_ref[at, :]], axis=0)
         gate = dot_nt(rows, gate_ref[...])
         up = dot_nt(rows, up_ref[...])
         hidden = (gate / (1.0 + jnp.exp(-gate)) * up).astype(jnp.bfloat16)
         part = dot(hidden, down_ref[...])
         own_ref[at, :] = part[:padded, :]
-        sends[e // each][low, :] = part[padded:, :].astype(jnp.bfloat16)
+        send_ref[at, :] = part[padded:, :].astype(jnp.bfloat16)
 
 
 def combine_kernel(block, route_ref, *refs):
@@ -237,13 +230,11 @@
         return lax.ppermute(x, "dp", [(0, 1), (1, 0)])
 
     order = [1, 2, 3, 4, 5, 6, 7]
-    after = {6: 1, 7: 2}
-    chunks = [[0, 1, 2, 3, 4, 5], [6, 7]]
     incoming = {0: outgoing[0]}
     for k in order:
         held = outgoing[k]
-        if k in after:
-            held, _ = lax.optimization_barrier((held, incoming[after[k]]))
+        if k > 5:
+            held, _ = lax.optimization_barrier((held, incoming[1]))
         incoming[k] = hop(held, k)
     route_now, _, _ = lax.optimization_barrier((route, incoming[1], incoming[2]))
 
@@ -262,50 +253,42 @@
     incoming[4], gate_now = lax.optimization_barrier((incoming[4], weights[0]))
     weights = [gate_now] + list(weights[1:])
 
-    returned = {}
-    last = None
-    for chunk in chunks:
-        count = len(chunk)
-        padded = 1 << (count * CAP - 1).bit_length()
-        tall = local_experts * padded
-        splits = SPLITS[0] if count > 2 else SPLITS[1]
-        piece = jax.ShapeDtypeStruct((tall // splits, width), bf16)
-        mine, *cut = pl.pallas_call(
-            functools.partial(regroup_kernel, local_experts, count, padded),
-            out_shape=[jax.ShapeDtypeStruct((tall, width), bf16)] + [piece] * splits,
-            in_specs=whole(count),
-            out_specs=whole(1 + splits),
-            scratch_shapes=[VMEM((count * block, width), bf16)],
-            compiler_params=params(4),
-            cost_estimate=cost(2 * tall * count * block * width, 4 * tall * width),
-            name="regroup",
-        )(*[incoming[k] for k in chunk])
-        theirs = [swap(x) for x in cut]
-        own, *send = pl.pallas_call(
-            functools.partial(ffn_kernel, padded, splits),
-            out_shape=[
-                jax.ShapeDtypeStruct((tall, width), jnp.float32),
-            ]
-            + [piece] * splits,
-            in_specs=whole(1 + splits + pieces),
-            out_specs=whole(1 + splits),
-            compiler_params=params(6),
-            cost_estimate=cost(12 * tall * width * half, 6 * local_experts * half * width),
+    tall = groups * CAP * local_experts
+    half_rows = jax.ShapeDtypeStruct((tall // 2, width), bf16)
+    mine = pl.pallas_call(
+        functools.partial(regroup_kernel, local_experts, groups),
+        out_shape=[half_rows] * 2,
+        in_specs=whole(groups),
+        out_specs=whole(2),
+        scratch_shapes=[VMEM((groups * block, width), bf16)],
+        compiler_params=params(4),
+        cost_estimate=cost(2 * tall * groups * block * width, 4 * tall * width),
+        name="regroup",
+    )(*[incoming[k] for k in range(groups)])
+    own, other = [], []
+    for h in range(2):
+        theirs = swap(mine[h])
+        kept, send = pl.pallas_call(
+            functools.partial(ffn_kernel, groups * CAP),
+            out_shape=[jax.ShapeDtypeStruct((tall // 2, width), jnp.float32), half_rows],
+            in_specs=whole(2 + pieces // 2),
+            out_specs=whole(2),
+            compiler_params=params(8),
+            cost_estimate=cost(6 * tall * width * half, 3 * local_experts * half * width),
             name="ffn",
-        )(mine, *theirs, *weights)
-        other = [swap(x) for x in send]
-        blocks = pl.pallas_call(
-            functools.partial(ungroup_kernel, local_experts, count, padded),
-            out_shape=[jax.ShapeDtypeStruct((block, width), bf16)] * count,
-            in_specs=whole(1 + splits),
-            out_specs=whole(count),
-            compiler_params=params(4),
-            cost_estimate=cost(2 * tall * count * block * width, 4 * tall * width),
-            name="ungroup",
-        )(own, *other)
-        last = blocks[0]
-        for k, y in zip(chunk, blocks):
-            returned[k] = hop(y, k) if k else y
+        )(mine[h], theirs, *weights[h * pieces // 2 : (h + 1) * pieces // 2])
+        own.append(kept)
+        other.append(swap(send))
+    blocks = pl.pallas_call(
+        functools.partial(ungroup_kernel, local_experts, groups),
+        out_shape=[jax.ShapeDtypeStruct((block, width), bf16)] * groups,
+        in_specs=whole(4),
+        out_specs=whole(groups),
+        compiler_params=params(4),
+        cost_estimate=cost(2 * tall * groups * block * width, 4 * tall * width),
+        name="ungroup",
+    )(*own, *other)
+    returned = {k: hop(blocks[k], k) if k else blocks[k] for k in [0] + order}
 
     return pl.pallas_call(
         functools.partial(combine_kernel, block),

time: 97.4 us -> 90.1 us (0.925)
  the two profiles are of different devices: /device:TPU:0 before, /device:TPU:14 now
where the time goes in v3:
time: 90.1 us; the launch traced here: 89.9 us
  waiting for transfers between devices  39.1 us (43%)
  Pallas kernels  25.7 us (29%)
  starting transfers between devices  22.6 us (25%)
  local copies, waits for them, and re-layouts  2.4 us (3%)
    ppermute x14, waiting for transfers between devices, hop(): return lax.ppermute(x, 'expert', [(i, i ^ k) for i in range(groups)])  35.8 us
    ppermute x14, starting transfers between devices, hop(): return lax.ppermute(x, 'expert', [(i, i ^ k) for i in range(groups)])  21.3 us
    pallas_call x1, Pallas kernels, fast(): pl.pallas_call(functools.partial(load_kernel, half), out_shape=[share] *...  11.7 us
    pallas_call x2, Pallas kernels, fast(): pl.pallas_call(functools.partial(ffn_kernel, groups * CAP), out_shape=[ja...  9.56 us
    ppermute x4, waiting for transfers between devices, swap(): return lax.ppermute(x, 'dp', [(0, 1), (1, 0)])  3.31 us
    unnamed x6, local copies, waits for them, and re-layouts  2.4 us
  transfers between devices with their start and end apart: 18, of which 12 were waited for; matrix products, arithmetic and copies ran while one was open for 0% of the time, Pallas kernels for 24%

profile of v3, /device:TPU:14, one launch (start us, length us, event | category | flops | bytes accessed | tf_op | source)
XLA Modules:
  0.0 89.9 jit_solution(11702108845296391818)
XLA Ops:
  0.0 0.1 pad_add_fusion.place_ref
  0.1 0.0 copy-start
  0.1 1.0 %copy-done = bf16[128,2048]{1,0:T(8,128)(2,1)S(1)} copy-done((bf16[128,2048]{1,0:T(8,128)(2,1)S(1)}, bf16[128,2048]{1,0:T(8,128)(2,1)}, u32[]{:S(2)}) %copy-start) | copy-done | bytes 524312
  1.1 0.0 copy-start.1
  1.1 0.7 copy-done.1
  1.8 0.0 copy-start.2
  1.8 0.7 copy-done.2
  2.5 1.2 %pack.1 = (f32[128,128]{1,0:T(8,128)S(1)}, bf16[40,2048]{1,0:T(8,128)(2,1)S(1)}, bf16[40,2048]{1,0:T(8,128)(2,1)S(1)}, bf16[40,2048]{1,0:T(8,128)(2,1)S(1)}, bf1...) custom-call(s32[2]{0:T(128)S(1)} %pad_add_fusion.place_ref, ...), custom_call_target="tpu_custom_call" | custom-call | flops 167772160 | bytes 1572864 | tf_op jit(solution)/shard_map/pack/pallas_call | solution.py:214
  3.7 0.6 collective-permute-start
  4.3 0.4 collective-permute-start.1
  4.7 2.5 %collective-permute-start.2 = (bf16[40,2048]{1,0:T(8,128)(2,1)S(1)}, bf16[40,2048]{1,0:T(8,128)(2,1)S(1)}, u32[]{:S(2)}, u32[]{:S(2)}) collective-permute-start(bf16[40,2048]{1,0:T(8,128)(2,1)S(1)} %get-tuple-element.49), channel_id=1, source_target_pairs={{0,6},{2,4},{4,2},{6,0},{8,14},{10,12},{12,10},{14,8},{1,7},{3,5},... | collective-permute-start | bytes 491528 | tf_op jit(solution)/shard_map/ppermute | solution.py:227
  7.2 2.6 %collective-permute-start.3 = (bf16[40,2048]{1,0:T(8,128)(2,1)S(1)}, bf16[40,2048]{1,0:T(8,128)(2,1)S(1)}, u32[]{:S(2)}, u32[]{:S(2)}) collective-permute-start(bf16[40,2048]{1,0:T(8,128)(2,1)S(1)} %get-tuple-element.50), channel_id=1, source_target_pairs={{0,8},{2,10},{4,12},{6,14},{8,0},{10,2},{12,4},{14,6},{1,9},{3,11}... | collective-permute-start | bytes 491528 | tf_op jit(solution)/shard_map/ppermute | solution.py:227
  9.8 0.3 collective-permute-start.4
  10.1 0.0 collective-permute-done.refs_1_
  10.1 1.6 %collective-permute-start.5 = (bf16[40,2048]{1,0:T(8,128)(2,1)S(1)}, bf16[40,2048]{1,0:T(8,128)(2,1)S(1)}, u32[]{:S(2)}, u32[]{:S(2)}) collective-permute-start(bf16[40,2048]{1,0:T(8,128)(2,1)S(1)} %get-tuple-element.56), channel_id=1, source_target_pairs={{0,12},{2,14},{4,8},{6,10},{8,4},{10,6},{12,0},{14,2},{1,13},{3,15... | collective-permute-start | bytes 491528 | tf_op jit(solution)/shard_map/ppermute | solution.py:227
  11.7 2.5 %collective-permute-done.1.refs_2_ = bf16[40,2048]{1,0:T(8,128)(2,1)S(1)} collective-permute-done((bf16[40,2048]{1,0:T(8,128)(2,1)S(1)}, bf16[40,2048]{1,0:T(8,128)(2,1)S(1)}, u32[]{:S(2)}, u32[]{:S(2)}) %collective-permute-start.1) | collective-permute-done | bytes 163872 | tf_op jit(solution)/shard_map/ppermute | solution.py:227
  14.2 3.3 %collective-permute-start.6 = (bf16[40,2048]{1,0:T(8,128)(2,1)S(1)}, bf16[40,2048]{1,0:T(8,128)(2,1)S(1)}, u32[]{:S(2)}, u32[]{:S(2)}) collective-permute-start(bf16[40,2048]{1,0:T(8,128)(2,1)S(1)} %get-tuple-element.58), channel_id=1, source_target_pairs={{0,14},{2,12},{4,10},{6,8},{8,6},{10,4},{12,2},{14,0},{1,15},{3,13... | collective-permute-start | bytes 491528 | tf_op jit(solution)/shard_map/ppermute | solution.py:227
  17.5 11.7 %load.1 = (bf16[704,2048]{1,0:T(8,128)(2,1)S(1)}, bf16[704,2048]{1,0:T(8,128)(2,1)S(1)}, bf16[704,2048]{1,0:T(8,128)(2,1)S(1)}, bf16[704,2048]{1,0:T(8,128)(2,1)...) custom-call(s32[2]{0:T(128)S(1)} %pad_add_fusion.place_ref, ...), custom_call_target="tpu_custom_call" | custom-call | bytes 34603008 | tf_op jit(solution)/shard_map/load/pallas_call | solution.py:243
  29.2 0.0 collective-permute-done.3.refs_4_
  29.2 0.0 collective-permute-done.2.refs_3_
  29.2 2.8 %collective-permute-done.4.refs_5_ = bf16[40,2048]{1,0:T(8,128)(2,1)S(1)} collective-permute-done((bf16[40,2048]{1,0:T(8,128)(2,1)S(1)}, bf16[40,2048]{1,0:T(8,128)(2,1)S(1)}, u32[]{:S(2)}, u32[]{:S(2)}) %collective-permute-start.4) | collective-permute-done | bytes 163872 | tf_op jit(solution)/shard_map/ppermute | solution.py:227
  32.0 3.3 %collective-permute-done.5.refs_6_ = bf16[40,2048]{1,0:T(8,128)(2,1)S(1)} collective-permute-done((bf16[40,2048]{1,0:T(8,128)(2,1)S(1)}, bf16[40,2048]{1,0:T(8,128)(2,1)S(1)}, u32[]{:S(2)}, u32[]{:S(2)}) %collective-permute-start.5) | collective-permute-done | bytes 163872 | tf_op jit(solution)/shard_map/ppermute | solution.py:227
  35.3 1.8 %collective-permute-done.6.refs_7_ = bf16[40,2048]{1,0:T(8,128)(2,1)S(1)} collective-permute-done((bf16[40,2048]{1,0:T(8,128)(2,1)S(1)}, bf16[40,2048]{1,0:T(8,128)(2,1)S(1)}, u32[]{:S(2)}, u32[]{:S(2)}) %collective-permute-start.6) | collective-permute-done | bytes 163872 | tf_op jit(solution)/shard_map/ppermute | solution.py:227
  37.0 0.8 regroup.1
  37.9 0.1 collective-permute-start.7
  38.0 0.5 collective-permute-start.8
  38.5 1.6 %collective-permute-done.7.theirs_ref = bf16[160,2048]{1,0:T(8,128)(2,1)S(1)} collective-permute-done((bf16[160,2048]{1,0:T(8,128)(2,1)S(1)}, bf16[160,2048]{1,0:T(8,128)(2,1)S(1)}, u32[]{:S(2)}, u32[]{:S(2)}) %collective-permute-start.7) | collective-permute-done | bytes 655392 | tf_op jit(solution)/shard_map/ppermute | solution.py:230
  40.1 4.8 %ffn.2 = (f32[160,2048]{1,0:T(8,128)S(1)}, bf16[160,2048]{1,0:T(8,128)(2,1)S(1)}) custom-call(bf16[160,2048]{1,0:T(8,128)(2,1)S(1)} %get-tuple-element.59.mine_ref, bf16[160,2048]{1,0:T(8,128)(2,1)S(1)} %collective-permute-done.7.theirs_ref, bf16[704,2048]{1,0:T(8,128)(2,1)S(1)} %get-tuple-element.60.refs_0_, ...), custom_call_target="tpu_custom_call" | custom-call | flops 2768240640 | bytes 17301504 | tf_op jit(solution)/shard_map/ffn/pallas_call | solution.py:271
  44.9 0.2 collective-permute-start.9
  45.1 0.0 collective-permute-done.8.theirs_ref
  45.1 4.8 %ffn.3 = (f32[160,2048]{1,0:T(8,128)S(1)}, bf16[160,2048]{1,0:T(8,128)(2,1)S(1)}) custom-call(bf16[160,2048]{1,0:T(8,128)(2,1)S(1)} %get-tuple-element.67.mine_ref, bf16[160,2048]{1,0:T(8,128)(2,1)S(1)} %collective-permute-done.8.theirs_ref, bf16[704,2048]{1,0:T(8,128)(2,1)S(1)} %get-tuple-element.68.refs_0_, ...), custom_call_target="tpu_custom_call" | custom-call | flops 2768240640 | bytes 17301504 | tf_op jit(solution)/shard_map/ffn/pallas_call | solution.py:271
  49.8 0.4 collective-permute-start.10
  50.3 0.0 collective-permute-done.9.other_low
  50.3 1.7 %collective-permute-done.10.other_high = bf16[160,2048]{1,0:T(8,128)(2,1)S(1)} collective-permute-done((bf16[160,2048]{1,0:T(8,128)(2,1)S(1)}, bf16[160,2048]{1,0:T(8,128)(2,1)S(1)}, u32[]{:S(2)}, u32[]{:S(2)}) %collective-permute-start.10) | collective-permute-done | bytes 655392 | tf_op jit(solution)/shard_map/ppermute | solution.py:230
  52.0 0.9 %ungroup.1 = (bf16[40,2048]{1,0:T(8,128)(2,1)S(1)}, bf16[40,2048]{1,0:T(8,128)(2,1)S(1)}, bf16[40,2048]{1,0:T(8,128)(2,1)S(1)}, bf16[40,2048]{1,0:T(8,128)(2,1)S...) custom-call(f32[160,2048]{1,0:T(8,128)S(1)} %get-tuple-element.66.ow, ...), custom_call_target="tpu_custom_call" | custom-call | flops 419430400 | bytes 2621440 | tf_op jit(solution)/shard_map/ungroup/pallas_call | solution.py:282
  52.9 1.5 %collective-permute-start.11 = (bf16[40,2048]{1,0:T(8,128)(2,1)S(1)}, bf16[40,2048]{1,0:T(8,128)(2,1)S(1)}, u32[]{:S(2)}, u32[]{:S(2)}) collective-permute-start(bf16[40,2048]{1,0:T(8,128)(2,1)S(1)} %get-tuple-element.78), channel_id=1, source_target_pairs={{0,2},{2,0},{4,6},{6,4},{8,10},{10,8},{12,14},{14,12},{1,3},{3,1},... | collective-permute-start | bytes 491528 | tf_op jit(solution)/shard_map/ppermute | solution.py:227
  54.4 0.0 collective-permute-start.12
  54.4 2.1 %collective-permute-start.13 = (bf16[40,2048]{1,0:T(8,128)(2,1)S(1)}, bf16[40,2048]{1,0:T(8,128)(2,1)S(1)}, u32[]{:S(2)}, u32[]{:S(2)}) collective-permute-start(bf16[40,2048]{1,0:T(8,128)(2,1)S(1)} %get-tuple-element.80), channel_id=1, source_target_pairs={{0,6},{2,4},{4,2},{6,0},{8,14},{10,12},{12,10},{14,8},{1,7},{3,5},... | collective-permute-start | bytes 491528 | tf_op jit(solution)/shard_map/ppermute | solution.py:227
  56.5 1.9 %collective-permute-start.14 = (bf16[40,2048]{1,0:T(8,128)(2,1)S(1)}, bf16[40,2048]{1,0:T(8,128)(2,1)S(1)}, u32[]{:S(2)}, u32[]{:S(2)}) collective-permute-start(bf16[40,2048]{1,0:T(8,128)(2,1)S(1)} %get-tuple-element.81), channel_id=1, source_target_pairs={{0,8},{2,10},{4,12},{6,14},{8,0},{10,2},{12,4},{14,6},{1,9},{3,11}... | collective-permute-start | bytes 491528 | tf_op jit(solution)/shard_map/ppermute | solution.py:227
  58.4 1.9 %collective-permute-start.15 = (bf16[40,2048]{1,0:T(8,128)(2,1)S(1)}, bf16[40,2048]{1,0:T(8,128)(2,1)S(1)}, u32[]{:S(2)}, u32[]{:S(2)}) collective-permute-start(bf16[40,2048]{1,0:T(8,128)(2,1)S(1)} %get-tuple-element.82), channel_id=1, source_target_pairs={{0,10},{2,8},{4,14},{6,12},{8,2},{10,0},{12,6},{14,4},{1,11},{3,9}... | collective-permute-start | bytes 491528 | tf_op jit(solution)/shard_map/ppermute | solution.py:227
  60.3 0.0 collective-permute-done.11.refs_1_
  60.3 2.5 %collective-permute-start.16 = (bf16[40,2048]{1,0:T(8,128)(2,1)S(1)}, bf16[40,2048]{1,0:T(8,128)(2,1)S(1)}, u32[]{:S(2)}, u32[]{:S(2)}) collective-permute-start(bf16[40,2048]{1,0:T(8,128)(2,1)S(1)} %get-tuple-element.83), channel_id=1, source_target_pairs={{0,12},{2,14},{4,8},{6,10},{8,4},{10,6},{12,0},{14,2},{1,13},{3,15... | collective-permute-start | bytes 491528 | tf_op jit(solution)/shard_map/ppermute | solution.py:227
  62.8 1.7 %collective-permute-done.12.refs_2_ = bf16[40,2048]{1,0:T(8,128)(2,1)S(1)} collective-permute-done((bf16[40,2048]{1,0:T(8,128)(2,1)S(1)}, bf16[40,2048]{1,0:T(8,128)(2,1)S(1)}, u32[]{:S(2)}, u32[]{:S(2)}) %collective-permute-start.12) | collective-permute-done | bytes 163872 | tf_op jit(solution)/shard_map/ppermute | solution.py:227
  64.5 0.2 collective-permute-start.17
  64.7 3.4 %collective-permute-done.13.refs_3_ = bf16[40,2048]{1,0:T(8,128)(2,1)S(1)} collective-permute-done((bf16[40,2048]{1,0:T(8,128)(2,1)S(1)}, bf16[40,2048]{1,0:T(8,128)(2,1)S(1)}, u32[]{:S(2)}, u32[]{:S(2)}) %collective-permute-start.13) | collective-permute-done | bytes 163872 | tf_op jit(solution)/shard_map/ppermute | solution.py:227
  68.1 2.5 %collective-permute-done.14.refs_4_ = bf16[40,2048]{1,0:T(8,128)(2,1)S(1)} collective-permute-done((bf16[40,2048]{1,0:T(8,128)(2,1)S(1)}, bf16[40,2048]{1,0:T(8,128)(2,1)S(1)}, u32[]{:S(2)}, u32[]{:S(2)}) %collective-permute-start.14) | collective-permute-done | bytes 163872 | tf_op jit(solution)/shard_map/ppermute | solution.py:227
  70.6 10.0 %collective-permute-done.15.refs_5_ = bf16[40,2048]{1,0:T(8,128)(2,1)S(1)} collective-permute-done((bf16[40,2048]{1,0:T(8,128)(2,1)S(1)}, bf16[40,2048]{1,0:T(8,128)(2,1)S(1)}, u32[]{:S(2)}, u32[]{:S(2)}) %collective-permute-start.15) | collective-permute-done | bytes 163872 | tf_op jit(solution)/shard_map/ppermute | solution.py:227
  80.6 4.9 %collective-permute-done.16.refs_6_ = bf16[40,2048]{1,0:T(8,128)(2,1)S(1)} collective-permute-done((bf16[40,2048]{1,0:T(8,128)(2,1)S(1)}, bf16[40,2048]{1,0:T(8,128)(2,1)S(1)}, u32[]{:S(2)}, u32[]{:S(2)}) %collective-permute-start.16) | collective-permute-done | bytes 163872 | tf_op jit(solution)/shard_map/ppermute | solution.py:227
  85.5 2.9 %collective-permute-done.17.refs_7_ = bf16[40,2048]{1,0:T(8,128)(2,1)S(1)} collective-permute-done((bf16[40,2048]{1,0:T(8,128)(2,1)S(1)}, bf16[40,2048]{1,0:T(8,128)(2,1)S(1)}, u32[]{:S(2)}, u32[]{:S(2)}) %collective-permute-start.17) | collective-permute-done | bytes 163872 | tf_op jit(solution)/shard_map/ppermute | solution.py:227
  88.4 1.6 %combine.1 = bf16[128,2048]{1,0:T(8,128)(2,1)} custom-call(f32[128,128]{1,0:T(8,128)S(1)} %get-tuple-element.51._.route_ref, bf16[40,2048]{1,0:T(8,128)(2,1)S(1)} %get-tuple-element.77.refs_0_, bf16[40,2048]{1,0:T(8,128)(2,1)S(1)} %collective-permute-done.11.refs_1_, bf16[40,2048]{1,0:T(8,128)(2,1)S(1)} %collective-permute-done.12.refs_2_, ...), custom_call_target="tpu_custom_call" | custom-call | flops 335544320 | bytes 1048576 | tf_op jit(solution)/shard_map/combine/pallas_call | solution.py:293
Async XLA Ops:
  0.1 1.0 %copy-start = (bf16[128,2048]{1,0:T(8,128)(2,1)S(1)}, bf16[128,2048]{1,0:T(8,128)(2,1)}, u32[]{:S(2)}) copy-start(bf16[128,2048]{1,0:T(8,128)(2,1)} %tokens_ref.1) | copy-start | bytes 1572868
  1.1 0.7 copy-start.1
  1.8 0.7 copy-start.2
  3.7 6.5 %collective-permute-start = (bf16[40,2048]{1,0:T(8,128)(2,1)S(1)}, bf16[40,2048]{1,0:T(8,128)(2,1)S(1)}, u32[]{:S(2)}, u32[]{:S(2)}) collective-permute-start(bf16[40,2048]{1,0:T(8,128)(2,1)S(1)} %get-tuple-element.47), channel_id=1, source_target_pairs={{0,2},{2,0},{4,6},{6,4},{8,10},{10,8},{12,14},{14,12},{1,3},{3,1},... | collective-permute-start | bytes 491528 | tf_op jit(solution)/shard_map/ppermute | solution.py:227
  4.3 10.0 %collective-permute-start.1 = (bf16[40,2048]{1,0:T(8,128)(2,1)S(1)}, bf16[40,2048]{1,0:T(8,128)(2,1)S(1)}, u32[]{:S(2)}, u32[]{:S(2)}) collective-permute-start(bf16[40,2048]{1,0:T(8,128)(2,1)S(1)} %get-tuple-element.48), channel_id=1, source_target_pairs={{0,4},{2,6},{4,0},{6,2},{8,12},{10,14},{12,8},{14,10},{1,5},{3,7},... | collective-permute-start | bytes 491528 | tf_op jit(solution)/shard_map/ppermute | solution.py:227
  4.7 24.5 %collective-permute-start.2 = (bf16[40,2048]{1,0:T(8,128)(2,1)S(1)}, bf16[40,2048]{1,0:T(8,128)(2,1)S(1)}, u32[]{:S(2)}, u32[]{:S(2)}) collective-permute-start(bf16[40,2048]{1,0:T(8,128)(2,1)S(1)} %get-tuple-element.49), channel_id=1, source_target_pairs={{0,6},{2,4},{4,2},{6,0},{8,14},{10,12},{12,10},{14,8},{1,7},{3,5},... | collective-permute-start | bytes 491528 | tf_op jit(solution)/shard_map/ppermute | solution.py:227
  7.2 22.0 %collective-permute-start.3 = (bf16[40,2048]{1,0:T(8,128)(2,1)S(1)}, bf16[40,2048]{1,0:T(8,128)(2,1)S(1)}, u32[]{:S(2)}, u32[]{:S(2)}) collective-permute-start(bf16[40,2048]{1,0:T(8,128)(2,1)S(1)} %get-tuple-element.50), channel_id=1, source_target_pairs={{0,8},{2,10},{4,12},{6,14},{8,0},{10,2},{12,4},{14,6},{1,9},{3,11}... | collective-permute-start | bytes 491528 | tf_op jit(solution)/shard_map/ppermute | solution.py:227
  9.8 22.2 %collective-permute-start.4 = (bf16[40,2048]{1,0:T(8,128)(2,1)S(1)}, bf16[40,2048]{1,0:T(8,128)(2,1)S(1)}, u32[]{:S(2)}, u32[]{:S(2)}) collective-permute-start(bf16[40,2048]{1,0:T(8,128)(2,1)S(1)} %get-tuple-element.54), channel_id=1, source_target_pairs={{0,10},{2,8},{4,14},{6,12},{8,2},{10,0},{12,6},{14,4},{1,11},{3,9}... | collective-permute-start | bytes 491528 | tf_op jit(solution)/shard_map/ppermute | solution.py:227
  10.1 25.2 %collective-permute-start.5 = (bf16[40,2048]{1,0:T(8,128)(2,1)S(1)}, bf16[40,2048]{1,0:T(8,128)(2,1)S(1)}, u32[]{:S(2)}, u32[]{:S(2)}) collective-permute-start(bf16[40,2048]{1,0:T(8,128)(2,1)S(1)} %get-tuple-element.56), channel_id=1, source_target_pairs={{0,12},{2,14},{4,8},{6,10},{8,4},{10,6},{12,0},{14,2},{1,13},{3,15... | collective-permute-start | bytes 491528 | tf_op jit(solution)/shard_map/ppermute | solution.py:227
  14.2 22.8 %collective-permute-start.6 = (bf16[40,2048]{1,0:T(8,128)(2,1)S(1)}, bf16[40,2048]{1,0:T(8,128)(2,1)S(1)}, u32[]{:S(2)}, u32[]{:S(2)}) collective-permute-start(bf16[40,2048]{1,0:T(8,128)(2,1)S(1)} %get-tuple-element.58), channel_id=1, source_target_pairs={{0,14},{2,12},{4,10},{6,8},{8,6},{10,4},{12,2},{14,0},{1,15},{3,13... | collective-permute-start | bytes 491528 | tf_op jit(solution)/shard_map/ppermute | solution.py:227
  37.9 2.2 %collective-permute-start.7 = (bf16[160,2048]{1,0:T(8,128)(2,1)S(1)}, bf16[160,2048]{1,0:T(8,128)(2,1)S(1)}, u32[]{:S(2)}, u32[]{:S(2)}) collective-permute-start(bf16[160,2048]{1,0:T(8,128)(2,1)S(1)} %get-tuple-element.59.mine_ref), channel_id=1, source_target_pairs={{0,1},{1,0},{2,3},{3,2},{4,5},{5,4},{6,7},{7,6},{8,9},{9,8},{10,11... | collective-permute-start | bytes 1966088 | tf_op jit(solution)/shard_map/ppermute | solution.py:230
  38.0 7.1 %collective-permute-start.8 = (bf16[160,2048]{1,0:T(8,128)(2,1)S(1)}, bf16[160,2048]{1,0:T(8,128)(2,1)S(1)}, u32[]{:S(2)}, u32[]{:S(2)}) collective-permute-start(bf16[160,2048]{1,0:T(8,128)(2,1)S(1)} %get-tuple-element.67.mine_ref), channel_id=1, source_target_pairs={{0,1},{1,0},{2,3},{3,2},{4,5},{5,4},{6,7},{7,6},{8,9},{9,8},{10,11... | collective-permute-start | bytes 1966088 | tf_op jit(solution)/shard_map/ppermute | solution.py:230
  44.9 5.4 %collective-permute-start.9 = (bf16[160,2048]{1,0:T(8,128)(2,1)S(1)}, bf16[160,2048]{1,0:T(8,128)(2,1)S(1)}, u32[]{:S(2)}, u32[]{:S(2)}) collective-permute-start(bf16[160,2048]{1,0:T(8,128)(2,1)S(1)} %get-tuple-element.75), channel_id=1, source_target_pairs={{0,1},{1,0},{2,3},{3,2},{4,5},{5,4},{6,7},{7,6},{8,9},{9,8},{10,11... | collective-permute-start | bytes 1966088 | tf_op jit(solution)/shard_map/ppermute | solution.py:230
  49.8 2.2 %collective-permute-start.10 = (bf16[160,2048]{1,0:T(8,128)(2,1)S(1)}, bf16[160,2048]{1,0:T(8,128)(2,1)S(1)}, u32[]{:S(2)}, u32[]{:S(2)}) collective-permute-start(bf16[160,2048]{1,0:T(8,128)(2,1)S(1)} %get-tuple-element.76), channel_id=1, source_target_pairs={{0,1},{1,0},{2,3},{3,2},{4,5},{5,4},{6,7},{7,6},{8,9},{9,8},{10,11... | collective-permute-start | bytes 1966088 | tf_op jit(solution)/shard_map/ppermute | solution.py:230
  52.9 7.3 %collective-permute-start.11 = (bf16[40,2048]{1,0:T(8,128)(2,1)S(1)}, bf16[40,2048]{1,0:T(8,128)(2,1)S(1)}, u32[]{:S(2)}, u32[]{:S(2)}) collective-permute-start(bf16[40,2048]{1,0:T(8,128)(2,1)S(1)} %get-tuple-element.78), channel_id=1, source_target_pairs={{0,2},{2,0},{4,6},{6,4},{8,10},{10,8},{12,14},{14,12},{1,3},{3,1},... | collective-permute-start | bytes 491528 | tf_op jit(solution)/shard_map/ppermute | solution.py:227
  54.4 10.1 %collective-permute-start.12 = (bf16[40,2048]{1,0:T(8,128)(2,1)S(1)}, bf16[40,2048]{1,0:T(8,128)(2,1)S(1)}, u32[]{:S(2)}, u32[]{:S(2)}) collective-permute-start(bf16[40,2048]{1,0:T(8,128)(2,1)S(1)} %get-tuple-element.79), channel_id=1, source_target_pairs={{0,4},{2,6},{4,0},{6,2},{8,12},{10,14},{12,8},{14,10},{1,5},{3,7},... | collective-permute-start | bytes 491528 | tf_op jit(solution)/shard_map/ppermute | solution.py:227
  54.4 13.6 %collective-permute-start.13 = (bf16[40,2048]{1,0:T(8,128)(2,1)S(1)}, bf16[40,2048]{1,0:T(8,128)(2,1)S(1)}, u32[]{:S(2)}, u32[]{:S(2)}) collective-permute-start(bf16[40,2048]{1,0:T(8,128)(2,1)S(1)} %get-tuple-element.80), channel_id=1, source_target_pairs={{0,6},{2,4},{4,2},{6,0},{8,14},{10,12},{12,10},{14,8},{1,7},{3,5},... | collective-permute-start | bytes 491528 | tf_op jit(solution)/shard_map/ppermute | solution.py:227
  56.5 14.1 %collective-permute-start.14 = (bf16[40,2048]{1,0:T(8,128)(2,1)S(1)}, bf16[40,2048]{1,0:T(8,128)(2,1)S(1)}, u32[]{:S(2)}, u32[]{:S(2)}) collective-permute-start(bf16[40,2048]{1,0:T(8,128)(2,1)S(1)} %get-tuple-element.81), channel_id=1, source_target_pairs={{0,8},{2,10},{4,12},{6,14},{8,0},{10,2},{12,4},{14,6},{1,9},{3,11}... | collective-permute-start | bytes 491528 | tf_op jit(solution)/shard_map/ppermute | solution.py:227
  58.4 22.2 %collective-permute-start.15 = (bf16[40,2048]{1,0:T(8,128)(2,1)S(1)}, bf16[40,2048]{1,0:T(8,128)(2,1)S(1)}, u32[]{:S(2)}, u32[]{:S(2)}) collective-permute-start(bf16[40,2048]{1,0:T(8,128)(2,1)S(1)} %get-tuple-element.82), channel_id=1, source_target_pairs={{0,10},{2,8},{4,14},{6,12},{8,2},{10,0},{12,6},{14,4},{1,11},{3,9}... | collective-permute-start | bytes 491528 | tf_op jit(solution)/shard_map/ppermute | solution.py:227
  60.3 25.2 %collective-permute-start.16 = (bf16[40,2048]{1,0:T(8,128)(2,1)S(1)}, bf16[40,2048]{1,0:T(8,128)(2,1)S(1)}, u32[]{:S(2)}, u32[]{:S(2)}) collective-permute-start(bf16[40,2048]{1,0:T(8,128)(2,1)S(1)} %get-tuple-element.83), channel_id=1, source_target_pairs={{0,12},{2,14},{4,8},{6,10},{8,4},{10,6},{12,0},{14,2},{1,13},{3,15... | collective-permute-start | bytes 491528 | tf_op jit(solution)/shard_map/ppermute | solution.py:227
  64.5 23.9 %collective-permute-start.17 = (bf16[40,2048]{1,0:T(8,128)(2,1)S(1)}, bf16[40,2048]{1,0:T(8,128)(2,1)S(1)}, u32[]{:S(2)}, u32[]{:S(2)}) collective-permute-start(bf16[40,2048]{1,0:T(8,128)(2,1)S(1)} %get-tuple-element.84), channel_id=1, source_target_pairs={{0,14},{2,12},{4,10},{6,8},{8,6},{10,4},{12,2},{14,0},{1,15},{3,13... | collective-permute-start | bytes 491528 | tf_op jit(solution)/shard_map/ppermute | solution.py:227

commit v4 on v3

--- a/solution.py
+++ b/solution.py
@@ -72,8 +72,18 @@
     return lax.broadcasted_iota(jnp.int32, shape, axis)
 
 
-def pack_kernel(local_experts, groups, place_ref, ids_ref, gates_ref, tokens_ref, *outs):
-    route_ref, blocks = outs[0], outs[1:]
+def pack_kernel(local_experts, groups, place_ref, ids_hbm, gates_hbm, tokens_hbm, *outs):
+    route_ref, blocks = outs[0], outs[1 : 1 + groups]
+    ids_ref, gates_ref, tokens_ref, sems = outs[1 + groups :]
+    copies = [
+        pltpu.make_async_copy(source, target, sems.at[at])
+        for at, (source, target) in enumerate(
+            ((ids_hbm, ids_ref), (gates_hbm, gates_ref), (tokens_hbm, tokens_ref))
+        )
+    ]
+    for copy in copies:
+        copy.start()
+    copies[0].wait()
     rows = tokens_ref.shape[0]
     block = local_experts * CAP
     me = place_ref[0]
@@ -92,6 +102,8 @@
     place = iota((groups * block, rows), 0)
     chosen = functools.reduce(lambda a, b: a | b, [place == s for s in slots])
     chooser = chosen.astype(jnp.bfloat16)
+    copies[1].wait()
+    copies[2].wait()
     step = 512
     for c in range(0, tokens_ref.shape[1], step):
         got = dot(chooser, tokens_ref[:, c : c + step]).astype(jnp.bfloat16)
@@ -141,17 +153,29 @@
 
 
 def load_kernel(half, place_ref, _, gate_hbm, up_hbm, down_hbm, *refs):
-    sems = refs[-1]
+    count = 3 * gate_hbm.shape[0]
+    outs, staged, sems = refs[:count], refs[count], refs[count + 1]
+    depth = staged.shape[0]
     first = pl.multiple_of(place_ref[1] * half, 8)
-    copies = []
+    turned, plain = [], []
     for e in range(gate_hbm.shape[0]):
-        sources = [gate_hbm.at[e], up_hbm.at[e], down_hbm.at[e, pl.ds(first, half), :]]
-        for source in sources:
-            at = len(copies)
-            copies.append(pltpu.make_async_copy(source, refs[at], sems.at[at]))
-    for copy in copies:
-        copy.start()
-    for copy in copies:
+        for at, source in ((3 * e, gate_hbm.at[e]), (3 * e + 1, up_hbm.at[e])):
+            slot = len(turned) % depth
+            turned.append((pltpu.make_async_copy(source, staged.at[slot], sems.at[at]), at, slot))
+        source = down_hbm.at[e, pl.ds(first, half), :]
+        plain.append(pltpu.make_async_copy(source, outs[3 * e + 2], sems.at[3 * e + 2]))
+    for at in range(depth):
+        turned[at][0].start()
+    for n, (copy, at, slot) in enumerate(turned):
+        copy.wait()
+        step = 256
+        for c in range(0, staged.shape[2], step):
+            outs[at][c : c + step, :] = staged[slot, :, c : c + step].T
+        if n + depth < len(turned):
+            turned[n + depth][0].start()
+        if n % 2 == 0:
+            plain[n // 2].start()
+    for copy in plain:
         copy.wait()
 
 
@@ -161,21 +185,26 @@
         gate_ref, up_ref, down_ref = weights[3 * e : 3 * e + 3]
         at = slice(e * padded, (e + 1) * padded)
         rows = jnp.concatenate([mine_ref[at, :], theirs_ref[at, :]], axis=0)
-        gate = dot_nt(rows, gate_ref[...])
-        up = dot_nt(rows, up_ref[...])
+        gate = dot(rows, gate_ref[...])
+        up = dot(rows, up_ref[...])
         hidden = (gate / (1.0 + jnp.exp(-gate)) * up).astype(jnp.bfloat16)
         part = dot(hidden, down_ref[...])
         own_ref[at, :] = part[:padded, :]
         send_ref[at, :] = part[padded:, :].astype(jnp.bfloat16)
 
 
-def combine_kernel(block, route_ref, *refs):
-    groups = len(refs) - 2
-    ins, out_ref, held = refs[:groups], refs[groups], refs[groups + 1]
-    for g in range(groups):
-        held[g * block : (g + 1) * block, :] = ins[g][...]
+def combine_kernel(block, members, first, *refs):
+    count = len(members)
+    held = refs[-1]
+    out_ref = refs[-2]
+    route_ref, ins = refs[0], refs[1 : 1 + count]
+    for at in range(count):
+        held[at * block : (at + 1) * block, :] = ins[at][...]
     rows = route_ref.shape[0]
-    place = iota((rows, groups * block), 1)
+    lane = iota((rows, count * block), 1)
+    place = lane
+    for at, k in enumerate(members):
+        place = jnp.where((lane >= at * block) & (lane < (at + 1) * block), lane + (k - at) * block, place)
     slots = [route_ref[:, k : k + 1].astype(jnp.int32) for k in range(TOPK)]
     gates = [route_ref[:, TOPK + k : TOPK + k + 1] for k in range(TOPK)]
     picks = [(place == s).astype(jnp.bfloat16) for s in slots]
@@ -183,7 +212,9 @@
     for c in range(0, out_ref.shape[1], step):
         part = held[:, c : c + step]
         total = sum(gates[k] * dot(picks[k], part) for k in range(TOPK))
-        out_ref[:, c : c + step] = total.astype(jnp.bfloat16)
+        if not first:
+            total = total + refs[1 + count][:, c : c + step]
+        out_ref[:, c : c + step] = total.astype(out_ref.dtype)
 
 
 def params(limit):
@@ -215,12 +246,18 @@
         functools.partial(pack_kernel, local_experts, groups),
         out_shape=[jax.ShapeDtypeStruct((rows, rows), jnp.float32)]
         + [jax.ShapeDtypeStruct((block, width), bf16)] * groups,
-        in_specs=[smem] + whole(3),
+        in_specs=[smem] + [hbm] * 3,
         out_specs=whole(1 + groups),
+        scratch_shapes=[
+            VMEM((TOPK, rows), jnp.int32),
+            VMEM((TOPK, rows), jnp.float32),
+            VMEM((rows, width), bf16),
+            pltpu.SemaphoreType.DMA((3,)),
+        ],
         compiler_params=params(4),
         cost_estimate=cost(2 * groups * block * rows * width, 2 * 3 * rows * width),
         name="pack",
-    )(place, route_ids.T, route_gates.T, tokens)
+    )(place, *[pltpu.with_memory_space_constraint(x, pltpu.HBM) for x in (route_ids.T, route_gates.T, tokens)])
     route, outgoing = packed[0], packed[1:]
 
     def hop(x, k):
@@ -239,14 +276,15 @@
     route_now, _, _ = lax.optimization_barrier((route, incoming[1], incoming[2]))
 
     share = jax.ShapeDtypeStruct((half, width), bf16)
+    turned = jax.ShapeDtypeStruct((width, half), bf16)
     pieces = 3 * local_experts
     weights = pl.pallas_call(
         functools.partial(load_kernel, half),
-        out_shape=[share] * pieces,
+        out_shape=[turned, turned, share] * local_experts,
         in_specs=[smem] + whole(1) + [hbm] * 3,
         out_specs=whole(pieces),
-        scratch_shapes=[pltpu.SemaphoreType.DMA((pieces,))],
-        compiler_params=params(1),
+        scratch_shapes=[VMEM((3, half, width), bf16), pltpu.SemaphoreType.DMA((pieces,))],
+        compiler_params=params(4 + 3 * 3),
         cost_estimate=cost(0, 6 * local_experts * half * width),
         name="load",
     )(place, route_now, gate_rows, up_rows, down_weight)
@@ -290,16 +328,22 @@
     )(*own, *other)
     returned = {k: hop(blocks[k], k) if k else blocks[k] for k in [0] + order}
 
-    return pl.pallas_call(
-        functools.partial(combine_kernel, block),
-        out_shape=jax.ShapeDtypeStruct((rows, width), bf16),
-        in_specs=whole(1 + groups),
-        out_specs=whole(1)[0],
-        scratch_shapes=[VMEM((groups * block, width), bf16)],
-        compiler_params=params(4),
-        cost_estimate=cost(4 * rows * groups * block * width, 4 * rows * width),
-        name="combine",
-    )(route, *[returned[k] for k in range(groups)])
+    total = None
+    parts = [[0, 1, 2, 3, 4], [5, 6, 7]]
+    for chunk in parts:
+        first, final = total is None, chunk is parts[-1]
+        count = len(chunk)
+        total = pl.pallas_call(
+            functools.partial(combine_kernel, block, chunk, first),
+            out_shape=jax.ShapeDtypeStruct((rows, width), bf16 if final else jnp.float32),
+            in_specs=whole(1 + count + (not first)),
+            out_specs=whole(1)[0],
+            scratch_shapes=[VMEM((count * block, width), bf16)],
+            compiler_params=params(4),
+            cost_estimate=cost(4 * rows * count * block * width, 4 * rows * width),
+            name="combine",
+        )(route, *[returned[k] for k in chunk], *([] if first else [total]))
+    return total
 
 
 def on_device(tokens, route_ids, route_gates, gate_weight, up_weight, down_weight):

time: 90.1 us -> 85.9 us (0.953)
  the two profiles are of different devices: /device:TPU:14 before, /device:TPU:10 now
where the time goes in v4:
time: 85.9 us; the launch traced here: 85.7 us
  waiting for transfers between devices  37.6 us (44%)
  Pallas kernels  24.6 us (29%)
  starting transfers between devices  23.3 us (27%)
    ppermute x14, waiting for transfers between devices, hop(): return lax.ppermute(x, 'expert', [(i, i ^ k) for i in range(groups)])  34.3 us
    ppermute x14, starting transfers between devices, hop(): return lax.ppermute(x, 'expert', [(i, i ^ k) for i in range(groups)])  22.1 us
    pallas_call x1, Pallas kernels, fast(): pl.pallas_call(functools.partial(load_kernel, half), out_shape=[turned, t...  11.9 us
    pallas_call x2, Pallas kernels, fast(): pl.pallas_call(functools.partial(ffn_kernel, groups * CAP), out_shape=[ja...  7.05 us
    ppermute x4, waiting for transfers between devices, swap(): return lax.ppermute(x, 'dp', [(0, 1), (1, 0)])  3.31 us
    pallas_call x1, Pallas kernels, fast(): pl.pallas_call(functools.partial(pack_kernel, local_experts, groups), out...  2.14 us
    pallas_call x2, Pallas kernels, fast(): pl.pallas_call(functools.partial(combine_kernel, block, chunk, first), ou...  1.78 us
  transfers between devices with their start and end apart: 18, of which 12 were waited for; matrix products, arithmetic and copies ran while one was open for 0% of the time, Pallas kernels for 23%

profile of v4, /device:TPU:10, one launch (start us, length us, event | category | flops | bytes accessed | tf_op | source)
XLA Modules:
  0.0 85.7 jit_solution(17223825397323120315)
XLA Ops:
  0.0 0.1 pad_add_fusion.place_ref
  0.1 2.1 %pack.1 = (f32[128,128]{1,0:T(8,128)S(1)}, bf16[40,2048]{1,0:T(8,128)(2,1)S(1)}, bf16[40,2048]{1,0:T(8,128)(2,1)S(1)}, bf16[40,2048]{1,0:T(8,128)(2,1)S(1)}, bf1...) custom-call(s32[2]{0:T(128)S(1)} %pad_add_fusion.place_ref, ...), custom_call_target="tpu_custom_call" | custom-call | flops 167772160 | bytes 1572864 | tf_op jit(solution)/shard_map/pack/pallas_call | solution.py:245
  2.2 0.6 collective-permute-start
  2.8 0.0 collective-permute-start.1
  2.8 3.0 %collective-permute-start.2 = (bf16[40,2048]{1,0:T(8,128)(2,1)S(1)}, bf16[40,2048]{1,0:T(8,128)(2,1)S(1)}, u32[]{:S(2)}, u32[]{:S(2)}) collective-permute-start(bf16[40,2048]{1,0:T(8,128)(2,1)S(1)} %get-tuple-element.49), channel_id=1, source_target_pairs={{0,6},{2,4},{4,2},{6,0},{8,14},{10,12},{12,10},{14,8},{1,7},{3,5},... | collective-permute-start | bytes 491528 | tf_op jit(solution)/shard_map/ppermute | solution.py:264
  5.8 2.6 %collective-permute-start.3 = (bf16[40,2048]{1,0:T(8,128)(2,1)S(1)}, bf16[40,2048]{1,0:T(8,128)(2,1)S(1)}, u32[]{:S(2)}, u32[]{:S(2)}) collective-permute-start(bf16[40,2048]{1,0:T(8,128)(2,1)S(1)} %get-tuple-element.50), channel_id=1, source_target_pairs={{0,8},{2,10},{4,12},{6,14},{8,0},{10,2},{12,4},{14,6},{1,9},{3,11}... | collective-permute-start | bytes 491528 | tf_op jit(solution)/shard_map/ppermute | solution.py:264
  8.4 0.3 collective-permute-start.4
  8.7 0.0 collective-permute-done.refs_1_
  8.7 1.6 %collective-permute-start.5 = (bf16[40,2048]{1,0:T(8,128)(2,1)S(1)}, bf16[40,2048]{1,0:T(8,128)(2,1)S(1)}, u32[]{:S(2)}, u32[]{:S(2)}) collective-permute-start(bf16[40,2048]{1,0:T(8,128)(2,1)S(1)} %get-tuple-element.56), channel_id=1, source_target_pairs={{0,12},{2,14},{4,8},{6,10},{8,4},{10,6},{12,0},{14,2},{1,13},{3,15... | collective-permute-start | bytes 491528 | tf_op jit(solution)/shard_map/ppermute | solution.py:264
  10.3 1.8 %collective-permute-done.1.refs_2_ = bf16[40,2048]{1,0:T(8,128)(2,1)S(1)} collective-permute-done((bf16[40,2048]{1,0:T(8,128)(2,1)S(1)}, bf16[40,2048]{1,0:T(8,128)(2,1)S(1)}, u32[]{:S(2)}, u32[]{:S(2)}) %collective-permute-start.1) | collective-permute-done | bytes 163872 | tf_op jit(solution)/shard_map/ppermute | solution.py:264
  12.0 4.0 %collective-permute-start.6 = (bf16[40,2048]{1,0:T(8,128)(2,1)S(1)}, bf16[40,2048]{1,0:T(8,128)(2,1)S(1)}, u32[]{:S(2)}, u32[]{:S(2)}) collective-permute-start(bf16[40,2048]{1,0:T(8,128)(2,1)S(1)} %get-tuple-element.58), channel_id=1, source_target_pairs={{0,14},{2,12},{4,10},{6,8},{8,6},{10,4},{12,2},{14,0},{1,15},{3,13... | collective-permute-start | bytes 491528 | tf_op jit(solution)/shard_map/ppermute | solution.py:264
  16.1 11.9 %load.1 = (bf16[2048,704]{1,0:T(8,128)(2,1)S(1)}, bf16[2048,704]{1,0:T(8,128)(2,1)S(1)}, bf16[704,2048]{1,0:T(8,128)(2,1)S(1)}, bf16[2048,704]{1,0:T(8,128)(2,1)...) custom-call(s32[2]{0:T(128)S(1)} %pad_add_fusion.place_ref, ...), custom_call_target="tpu_custom_call" | custom-call | bytes 34603008 | tf_op jit(solution)/shard_map/load/pallas_call | solution.py:281
  28.0 0.0 collective-permute-done.3.refs_4_
  28.0 0.0 collective-permute-done.2.refs_3_
  28.0 2.6 %collective-permute-done.4.refs_5_ = bf16[40,2048]{1,0:T(8,128)(2,1)S(1)} collective-permute-done((bf16[40,2048]{1,0:T(8,128)(2,1)S(1)}, bf16[40,2048]{1,0:T(8,128)(2,1)S(1)}, u32[]{:S(2)}, u32[]{:S(2)}) %collective-permute-start.4) | collective-permute-done | bytes 163872 | tf_op jit(solution)/shard_map/ppermute | solution.py:264
  30.6 3.3 %collective-permute-done.5.refs_6_ = bf16[40,2048]{1,0:T(8,128)(2,1)S(1)} collective-permute-done((bf16[40,2048]{1,0:T(8,128)(2,1)S(1)}, bf16[40,2048]{1,0:T(8,128)(2,1)S(1)}, u32[]{:S(2)}, u32[]{:S(2)}) %collective-permute-start.5) | collective-permute-done | bytes 163872 | tf_op jit(solution)/shard_map/ppermute | solution.py:264
  33.9 1.8 %collective-permute-done.6.refs_7_ = bf16[40,2048]{1,0:T(8,128)(2,1)S(1)} collective-permute-done((bf16[40,2048]{1,0:T(8,128)(2,1)S(1)}, bf16[40,2048]{1,0:T(8,128)(2,1)S(1)}, u32[]{:S(2)}, u32[]{:S(2)}) %collective-permute-start.6) | collective-permute-done | bytes 163872 | tf_op jit(solution)/shard_map/ppermute | solution.py:264
  35.6 0.8 regroup.1
  36.5 0.1 collective-permute-start.7
  36.6 0.5 collective-permute-start.8
  37.1 1.6 %collective-permute-done.7.theirs_ref = bf16[160,2048]{1,0:T(8,128)(2,1)S(1)} collective-permute-done((bf16[160,2048]{1,0:T(8,128)(2,1)S(1)}, bf16[160,2048]{1,0:T(8,128)(2,1)S(1)}, u32[]{:S(2)}, u32[]{:S(2)}) %collective-permute-start.7) | collective-permute-done | bytes 655392 | tf_op jit(solution)/shard_map/ppermute | solution.py:267
  38.6 3.4 %ffn.2 = (f32[160,2048]{1,0:T(8,128)S(1)}, bf16[160,2048]{1,0:T(8,128)(2,1)S(1)}) custom-call(bf16[160,2048]{1,0:T(8,128)(2,1)S(1)} %get-tuple-element.59.mine_ref, bf16[160,2048]{1,0:T(8,128)(2,1)S(1)} %collective-permute-done.7.theirs_ref, bf16[2048,704]{1,0:T(8,128)(2,1)S(1)} %get-tuple-element.60.refs_0_, ...), custom_call_target="tpu_custom_call" | custom-call | flops 2768240640 | bytes 17301504 | tf_op jit(solution)/shard_map/ffn/pallas_call | solution.py:309
  42.1 0.2 collective-permute-start.9
  42.3 0.0 collective-permute-done.8.theirs_ref
  42.3 3.6 %ffn.3 = (f32[160,2048]{1,0:T(8,128)S(1)}, bf16[160,2048]{1,0:T(8,128)(2,1)S(1)}) custom-call(bf16[160,2048]{1,0:T(8,128)(2,1)S(1)} %get-tuple-element.67.mine_ref, bf16[160,2048]{1,0:T(8,128)(2,1)S(1)} %collective-permute-done.8.theirs_ref, bf16[2048,704]{1,0:T(8,128)(2,1)S(1)} %get-tuple-element.68.refs_0_, ...), custom_call_target="tpu_custom_call" | custom-call | flops 2768240640 | bytes 17301504 | tf_op jit(solution)/shard_map/ffn/pallas_call | solution.py:309
  45.9 0.4 collective-permute-start.10
  46.3 0.0 collective-permute-done.9.other_low
  46.3 1.7 %collective-permute-done.10.other_high = bf16[160,2048]{1,0:T(8,128)(2,1)S(1)} collective-permute-done((bf16[160,2048]{1,0:T(8,128)(2,1)S(1)}, bf16[160,2048]{1,0:T(8,128)(2,1)S(1)}, u32[]{:S(2)}, u32[]{:S(2)}) %collective-permute-start.10) | collective-permute-done | bytes 655392 | tf_op jit(solution)/shard_map/ppermute | solution.py:267
  48.1 0.9 %ungroup.1 = (bf16[40,2048]{1,0:T(8,128)(2,1)S(1)}, bf16[40,2048]{1,0:T(8,128)(2,1)S(1)}, bf16[40,2048]{1,0:T(8,128)(2,1)S(1)}, bf16[40,2048]{1,0:T(8,128)(2,1)S...) custom-call(f32[160,2048]{1,0:T(8,128)S(1)} %get-tuple-element.66.ow, ...), custom_call_target="tpu_custom_call" | custom-call | flops 419430400 | bytes 2621440 | tf_op jit(solution)/shard_map/ungroup/pallas_call | solution.py:320
  49.0 1.5 %collective-permute-start.14 = (bf16[40,2048]{1,0:T(8,128)(2,1)S(1)}, bf16[40,2048]{1,0:T(8,128)(2,1)S(1)}, u32[]{:S(2)}, u32[]{:S(2)}) collective-permute-start(bf16[40,2048]{1,0:T(8,128)(2,1)S(1)} %get-tuple-element.81), channel_id=1, source_target_pairs={{0,2},{2,0},{4,6},{6,4},{8,10},{10,8},{12,14},{14,12},{1,3},{3,1},... | collective-permute-start | bytes 491528 | tf_op jit(solution)/shard_map/ppermute | solution.py:264
  50.5 0.0 collective-permute-start.15
  50.5 2.1 %collective-permute-start.16 = (bf16[40,2048]{1,0:T(8,128)(2,1)S(1)}, bf16[40,2048]{1,0:T(8,128)(2,1)S(1)}, u32[]{:S(2)}, u32[]{:S(2)}) collective-permute-start(bf16[40,2048]{1,0:T(8,128)(2,1)S(1)} %get-tuple-element.83), channel_id=1, source_target_pairs={{0,6},{2,4},{4,2},{6,0},{8,14},{10,12},{12,10},{14,8},{1,7},{3,5},... | collective-permute-start | bytes 491528 | tf_op jit(solution)/shard_map/ppermute | solution.py:264
  52.5 1.9 %collective-permute-start.17 = (bf16[40,2048]{1,0:T(8,128)(2,1)S(1)}, bf16[40,2048]{1,0:T(8,128)(2,1)S(1)}, u32[]{:S(2)}, u32[]{:S(2)}) collective-permute-start(bf16[40,2048]{1,0:T(8,128)(2,1)S(1)} %get-tuple-element.84), channel_id=1, source_target_pairs={{0,8},{2,10},{4,12},{6,14},{8,0},{10,2},{12,4},{14,6},{1,9},{3,11}... | collective-permute-start | bytes 491528 | tf_op jit(solution)/shard_map/ppermute | solution.py:264
  54.5 1.9 %collective-permute-start.11 = (bf16[40,2048]{1,0:T(8,128)(2,1)S(1)}, bf16[40,2048]{1,0:T(8,128)(2,1)S(1)}, u32[]{:S(2)}, u32[]{:S(2)}) collective-permute-start(bf16[40,2048]{1,0:T(8,128)(2,1)S(1)} %get-tuple-element.77), channel_id=1, source_target_pairs={{0,10},{2,8},{4,14},{6,12},{8,2},{10,0},{12,6},{14,4},{1,11},{3,9}... | collective-permute-start | bytes 491528 | tf_op jit(solution)/shard_map/ppermute | solution.py:264
  56.3 0.0 collective-permute-done.14.refs_2_
  56.3 2.5 %collective-permute-start.12 = (bf16[40,2048]{1,0:T(8,128)(2,1)S(1)}, bf16[40,2048]{1,0:T(8,128)(2,1)S(1)}, u32[]{:S(2)}, u32[]{:S(2)}) collective-permute-start(bf16[40,2048]{1,0:T(8,128)(2,1)S(1)} %get-tuple-element.78), channel_id=1, source_target_pairs={{0,12},{2,14},{4,8},{6,10},{8,4},{10,6},{12,0},{14,2},{1,13},{3,15... | collective-permute-start | bytes 491528 | tf_op jit(solution)/shard_map/ppermute | solution.py:264
  58.9 1.7 %collective-permute-done.15.refs_3_ = bf16[40,2048]{1,0:T(8,128)(2,1)S(1)} collective-permute-done((bf16[40,2048]{1,0:T(8,128)(2,1)S(1)}, bf16[40,2048]{1,0:T(8,128)(2,1)S(1)}, u32[]{:S(2)}, u32[]{:S(2)}) %collective-permute-start.15) | collective-permute-done | bytes 163872 | tf_op jit(solution)/shard_map/ppermute | solution.py:264
  60.6 0.2 collective-permute-start.13
  60.7 3.4 %collective-permute-done.16.refs_4_ = bf16[40,2048]{1,0:T(8,128)(2,1)S(1)} collective-permute-done((bf16[40,2048]{1,0:T(8,128)(2,1)S(1)}, bf16[40,2048]{1,0:T(8,128)(2,1)S(1)}, u32[]{:S(2)}, u32[]{:S(2)}) %collective-permute-start.16) | collective-permute-done | bytes 163872 | tf_op jit(solution)/shard_map/ppermute | solution.py:264
  64.1 2.5 %collective-permute-done.17.refs_5_ = bf16[40,2048]{1,0:T(8,128)(2,1)S(1)} collective-permute-done((bf16[40,2048]{1,0:T(8,128)(2,1)S(1)}, bf16[40,2048]{1,0:T(8,128)(2,1)S(1)}, u32[]{:S(2)}, u32[]{:S(2)}) %collective-permute-start.17) | collective-permute-done | bytes 163872 | tf_op jit(solution)/shard_map/ppermute | solution.py:264
  66.6 0.5 combine.2.refs_4_
  67.1 9.5 %collective-permute-done.11.refs_1_ = bf16[40,2048]{1,0:T(8,128)(2,1)S(1)} collective-permute-done((bf16[40,2048]{1,0:T(8,128)(2,1)S(1)}, bf16[40,2048]{1,0:T(8,128)(2,1)S(1)}, u32[]{:S(2)}, u32[]{:S(2)}) %collective-permute-start.11) | collective-permute-done | bytes 163872 | tf_op jit(solution)/shard_map/ppermute | solution.py:264
  76.6 4.9 %collective-permute-done.12.refs_2_ = bf16[40,2048]{1,0:T(8,128)(2,1)S(1)} collective-permute-done((bf16[40,2048]{1,0:T(8,128)(2,1)S(1)}, bf16[40,2048]{1,0:T(8,128)(2,1)S(1)}, u32[]{:S(2)}, u32[]{:S(2)}) %collective-permute-start.12) | collective-permute-done | bytes 163872 | tf_op jit(solution)/shard_map/ppermute | solution.py:264
  81.5 2.9 %collective-permute-done.13.refs_3_ = bf16[40,2048]{1,0:T(8,128)(2,1)S(1)} collective-permute-done((bf16[40,2048]{1,0:T(8,128)(2,1)S(1)}, bf16[40,2048]{1,0:T(8,128)(2,1)S(1)}, u32[]{:S(2)}, u32[]{:S(2)}) %collective-permute-start.13) | collective-permute-done | bytes 163872 | tf_op jit(solution)/shard_map/ppermute | solution.py:264
  84.4 1.3 %combine.3 = bf16[128,2048]{1,0:T(8,128)(2,1)} custom-call(f32[128,128]{1,0:T(8,128)S(1)} %get-tuple-element.51._.refs_0_, bf16[40,2048]{1,0:T(8,128)(2,1)S(1)} %collective-permute-done.11.refs_1_, bf16[40,2048]{1,0:T(8,128)(2,1)S(1)} %collective-permute-done.12.refs_2_, bf16[40,2048]{1,0:T(8,128)(2,1)S(1)} %collective-permute-done.13.refs_3_, ...), custom_call_target="tpu_custom_call" | custom-call | flops 125829120 | bytes 1048576 | tf_op jit(solution)/shard_map/combine/pallas_call | solution.py:336
Async XLA Ops:
  2.2 6.5 %collective-permute-start = (bf16[40,2048]{1,0:T(8,128)(2,1)S(1)}, bf16[40,2048]{1,0:T(8,128)(2,1)S(1)}, u32[]{:S(2)}, u32[]{:S(2)}) collective-permute-start(bf16[40,2048]{1,0:T(8,128)(2,1)S(1)} %get-tuple-element.47), channel_id=1, source_target_pairs={{0,2},{2,0},{4,6},{6,4},{8,10},{10,8},{12,14},{14,12},{1,3},{3,1},... | collective-permute-start | bytes 491528 | tf_op jit(solution)/shard_map/ppermute | solution.py:264
  2.8 9.2 %collective-permute-start.1 = (bf16[40,2048]{1,0:T(8,128)(2,1)S(1)}, bf16[40,2048]{1,0:T(8,128)(2,1)S(1)}, u32[]{:S(2)}, u32[]{:S(2)}) collective-permute-start(bf16[40,2048]{1,0:T(8,128)(2,1)S(1)} %get-tuple-element.48), channel_id=1, source_target_pairs={{0,4},{2,6},{4,0},{6,2},{8,12},{10,14},{12,8},{14,10},{1,5},{3,7},... | collective-permute-start | bytes 491528 | tf_op jit(solution)/shard_map/ppermute | solution.py:264
  2.8 25.2 %collective-permute-start.2 = (bf16[40,2048]{1,0:T(8,128)(2,1)S(1)}, bf16[40,2048]{1,0:T(8,128)(2,1)S(1)}, u32[]{:S(2)}, u32[]{:S(2)}) collective-permute-start(bf16[40,2048]{1,0:T(8,128)(2,1)S(1)} %get-tuple-element.49), channel_id=1, source_target_pairs={{0,6},{2,4},{4,2},{6,0},{8,14},{10,12},{12,10},{14,8},{1,7},{3,5},... | collective-permute-start | bytes 491528 | tf_op jit(solution)/shard_map/ppermute | solution.py:264
  5.8 22.2 %collective-permute-start.3 = (bf16[40,2048]{1,0:T(8,128)(2,1)S(1)}, bf16[40,2048]{1,0:T(8,128)(2,1)S(1)}, u32[]{:S(2)}, u32[]{:S(2)}) collective-permute-start(bf16[40,2048]{1,0:T(8,128)(2,1)S(1)} %get-tuple-element.50), channel_id=1, source_target_pairs={{0,8},{2,10},{4,12},{6,14},{8,0},{10,2},{12,4},{14,6},{1,9},{3,11}... | collective-permute-start | bytes 491528 | tf_op jit(solution)/shard_map/ppermute | solution.py:264
  8.4 22.2 %collective-permute-start.4 = (bf16[40,2048]{1,0:T(8,128)(2,1)S(1)}, bf16[40,2048]{1,0:T(8,128)(2,1)S(1)}, u32[]{:S(2)}, u32[]{:S(2)}) collective-permute-start(bf16[40,2048]{1,0:T(8,128)(2,1)S(1)} %get-tuple-element.54), channel_id=1, source_target_pairs={{0,10},{2,8},{4,14},{6,12},{8,2},{10,0},{12,6},{14,4},{1,11},{3,9}... | collective-permute-start | bytes 491528 | tf_op jit(solution)/shard_map/ppermute | solution.py:264
  8.7 25.2 %collective-permute-start.5 = (bf16[40,2048]{1,0:T(8,128)(2,1)S(1)}, bf16[40,2048]{1,0:T(8,128)(2,1)S(1)}, u32[]{:S(2)}, u32[]{:S(2)}) collective-permute-start(bf16[40,2048]{1,0:T(8,128)(2,1)S(1)} %get-tuple-element.56), channel_id=1, source_target_pairs={{0,12},{2,14},{4,8},{6,10},{8,4},{10,6},{12,0},{14,2},{1,13},{3,15... | collective-permute-start | bytes 491528 | tf_op jit(solution)/shard_map/ppermute | solution.py:264
  12.0 23.6 %collective-permute-start.6 = (bf16[40,2048]{1,0:T(8,128)(2,1)S(1)}, bf16[40,2048]{1,0:T(8,128)(2,1)S(1)}, u32[]{:S(2)}, u32[]{:S(2)}) collective-permute-start(bf16[40,2048]{1,0:T(8,128)(2,1)S(1)} %get-tuple-element.58), channel_id=1, source_target_pairs={{0,14},{2,12},{4,10},{6,8},{8,6},{10,4},{12,2},{14,0},{1,15},{3,13... | collective-permute-start | bytes 491528 | tf_op jit(solution)/shard_map/ppermute | solution.py:264
  36.5 2.2 %collective-permute-start.7 = (bf16[160,2048]{1,0:T(8,128)(2,1)S(1)}, bf16[160,2048]{1,0:T(8,128)(2,1)S(1)}, u32[]{:S(2)}, u32[]{:S(2)}) collective-permute-start(bf16[160,2048]{1,0:T(8,128)(2,1)S(1)} %get-tuple-element.59.mine_ref), channel_id=1, source_target_pairs={{0,1},{1,0},{2,3},{3,2},{4,5},{5,4},{6,7},{7,6},{8,9},{9,8},{10,11... | collective-permute-start | bytes 1966088 | tf_op jit(solution)/shard_map/ppermute | solution.py:267
  36.6 5.7 %collective-permute-start.8 = (bf16[160,2048]{1,0:T(8,128)(2,1)S(1)}, bf16[160,2048]{1,0:T(8,128)(2,1)S(1)}, u32[]{:S(2)}, u32[]{:S(2)}) collective-permute-start(bf16[160,2048]{1,0:T(8,128)(2,1)S(1)} %get-tuple-element.67.mine_ref), channel_id=1, source_target_pairs={{0,1},{1,0},{2,3},{3,2},{4,5},{5,4},{6,7},{7,6},{8,9},{9,8},{10,11... | collective-permute-start | bytes 1966088 | tf_op jit(solution)/shard_map/ppermute | solution.py:267
  42.1 4.3 %collective-permute-start.9 = (bf16[160,2048]{1,0:T(8,128)(2,1)S(1)}, bf16[160,2048]{1,0:T(8,128)(2,1)S(1)}, u32[]{:S(2)}, u32[]{:S(2)}) collective-permute-start(bf16[160,2048]{1,0:T(8,128)(2,1)S(1)} %get-tuple-element.75), channel_id=1, source_target_pairs={{0,1},{1,0},{2,3},{3,2},{4,5},{5,4},{6,7},{7,6},{8,9},{9,8},{10,11... | collective-permute-start | bytes 1966088 | tf_op jit(solution)/shard_map/ppermute | solution.py:267
  45.9 2.2 %collective-permute-start.10 = (bf16[160,2048]{1,0:T(8,128)(2,1)S(1)}, bf16[160,2048]{1,0:T(8,128)(2,1)S(1)}, u32[]{:S(2)}, u32[]{:S(2)}) collective-permute-start(bf16[160,2048]{1,0:T(8,128)(2,1)S(1)} %get-tuple-element.76), channel_id=1, source_target_pairs={{0,1},{1,0},{2,3},{3,2},{4,5},{5,4},{6,7},{7,6},{8,9},{9,8},{10,11... | collective-permute-start | bytes 1966088 | tf_op jit(solution)/shard_map/ppermute | solution.py:267
  49.0 7.3 %collective-permute-start.14 = (bf16[40,2048]{1,0:T(8,128)(2,1)S(1)}, bf16[40,2048]{1,0:T(8,128)(2,1)S(1)}, u32[]{:S(2)}, u32[]{:S(2)}) collective-permute-start(bf16[40,2048]{1,0:T(8,128)(2,1)S(1)} %get-tuple-element.81), channel_id=1, source_target_pairs={{0,2},{2,0},{4,6},{6,4},{8,10},{10,8},{12,14},{14,12},{1,3},{3,1},... | collective-permute-start | bytes 491528 | tf_op jit(solution)/shard_map/ppermute | solution.py:264
  50.5 10.1 %collective-permute-start.15 = (bf16[40,2048]{1,0:T(8,128)(2,1)S(1)}, bf16[40,2048]{1,0:T(8,128)(2,1)S(1)}, u32[]{:S(2)}, u32[]{:S(2)}) collective-permute-start(bf16[40,2048]{1,0:T(8,128)(2,1)S(1)} %get-tuple-element.82), channel_id=1, source_target_pairs={{0,4},{2,6},{4,0},{6,2},{8,12},{10,14},{12,8},{14,10},{1,5},{3,7},... | collective-permute-start | bytes 491528 | tf_op jit(solution)/shard_map/ppermute | solution.py:264
  50.5 13.6 %collective-permute-start.16 = (bf16[40,2048]{1,0:T(8,128)(2,1)S(1)}, bf16[40,2048]{1,0:T(8,128)(2,1)S(1)}, u32[]{:S(2)}, u32[]{:S(2)}) collective-permute-start(bf16[40,2048]{1,0:T(8,128)(2,1)S(1)} %get-tuple-element.83), channel_id=1, source_target_pairs={{0,6},{2,4},{4,2},{6,0},{8,14},{10,12},{12,10},{14,8},{1,7},{3,5},... | collective-permute-start | bytes 491528 | tf_op jit(solution)/shard_map/ppermute | solution.py:264
  52.5 14.1 %collective-permute-start.17 = (bf16[40,2048]{1,0:T(8,128)(2,1)S(1)}, bf16[40,2048]{1,0:T(8,128)(2,1)S(1)}, u32[]{:S(2)}, u32[]{:S(2)}) collective-permute-start(bf16[40,2048]{1,0:T(8,128)(2,1)S(1)} %get-tuple-element.84), channel_id=1, source_target_pairs={{0,8},{2,10},{4,12},{6,14},{8,0},{10,2},{12,4},{14,6},{1,9},{3,11}... | collective-permute-start | bytes 491528 | tf_op jit(solution)/shard_map/ppermute | solution.py:264
  54.5 22.2 %collective-permute-start.11 = (bf16[40,2048]{1,0:T(8,128)(2,1)S(1)}, bf16[40,2048]{1,0:T(8,128)(2,1)S(1)}, u32[]{:S(2)}, u32[]{:S(2)}) collective-permute-start(bf16[40,2048]{1,0:T(8,128)(2,1)S(1)} %get-tuple-element.77), channel_id=1, source_target_pairs={{0,10},{2,8},{4,14},{6,12},{8,2},{10,0},{12,6},{14,4},{1,11},{3,9}... | collective-permute-start | bytes 491528 | tf_op jit(solution)/shard_map/ppermute | solution.py:264
  56.3 25.2 %collective-permute-start.12 = (bf16[40,2048]{1,0:T(8,128)(2,1)S(1)}, bf16[40,2048]{1,0:T(8,128)(2,1)S(1)}, u32[]{:S(2)}, u32[]{:S(2)}) collective-permute-start(bf16[40,2048]{1,0:T(8,128)(2,1)S(1)} %get-tuple-element.78), channel_id=1, source_target_pairs={{0,12},{2,14},{4,8},{6,10},{8,4},{10,6},{12,0},{14,2},{1,13},{3,15... | collective-permute-start | bytes 491528 | tf_op jit(solution)/shard_map/ppermute | solution.py:264
  60.6 23.9 %collective-permute-start.13 = (bf16[40,2048]{1,0:T(8,128)(2,1)S(1)}, bf16[40,2048]{1,0:T(8,128)(2,1)S(1)}, u32[]{:S(2)}, u32[]{:S(2)}) collective-permute-start(bf16[40,2048]{1,0:T(8,128)(2,1)S(1)} %get-tuple-element.79), channel_id=1, source_target_pairs={{0,14},{2,12},{4,10},{6,8},{8,6},{10,4},{12,2},{14,0},{1,15},{3,13... | collective-permute-start | bytes 491528 | tf_op jit(solution)/shard_map/ppermute | solution.py:264

commit v5 on v4

--- a/solution.py
+++ b/solution.py
@@ -266,11 +266,11 @@
     def swap(x):
         return lax.ppermute(x, "dp", [(0, 1), (1, 0)])
 
-    order = [1, 2, 3, 4, 5, 6, 7]
+    order = [1, 2, 4, 5, 6, 3, 7]
     incoming = {0: outgoing[0]}
     for k in order:
         held = outgoing[k]
-        if k > 5:
+        if k in (3, 7):
             held, _ = lax.optimization_barrier((held, incoming[1]))
         incoming[k] = hop(held, k)
     route_now, _, _ = lax.optimization_barrier((route, incoming[1], incoming[2]))
@@ -329,7 +329,7 @@
     returned = {k: hop(blocks[k], k) if k else blocks[k] for k in [0] + order}
 
     total = None
-    parts = [[0, 1, 2, 3, 4], [5, 6, 7]]
+    parts = [[0, 1, 6, 7], [2, 3, 4, 5]]
     for chunk in parts:
         first, final = total is None, chunk is parts[-1]
         count = len(chunk)

time: 85.9 us -> 81.3 us (0.946)
  the two profiles are of different devices: /device:TPU:10 before, /device:TPU:0 now
where the time goes in v5:
time: 81.3 us; the launch traced here: 81.2 us
  starting transfers between devices  34.9 us (43%)
  Pallas kernels  24.7 us (30%)
  waiting for transfers between devices  21.5 us (26%)
    ppermute x14, starting transfers between devices, hop(): return lax.ppermute(x, 'expert', [(i, i ^ k) for i in range(groups)])  33.7 us
    ppermute x14, waiting for transfers between devices, hop(): return lax.ppermute(x, 'expert', [(i, i ^ k) for i in range(groups)])  18.2 us
    pallas_call x1, Pallas kernels, fast(): pl.pallas_call(functools.partial(load_kernel, half), out_shape=[turned, t...  11.9 us
    pallas_call x2, Pallas kernels, fast(): pl.pallas_call(functools.partial(ffn_kernel, groups * CAP), out_shape=[ja...  7.04 us
    ppermute x4, waiting for transfers between devices, swap(): return lax.ppermute(x, 'dp', [(0, 1), (1, 0)])  3.31 us
    pallas_call x1, Pallas kernels, fast(): pl.pallas_call(functools.partial(pack_kernel, local_experts, groups), out...  2.14 us
    pallas_call x2, Pallas kernels, fast(): pl.pallas_call(functools.partial(combine_kernel, block, chunk, first), ou...  1.79 us
  transfers between devices with their start and end apart: 18, of which 7 were waited for; matrix products, arithmetic and copies ran while one was open for 0% of the time, Pallas kernels for 24%

profile of v5, /device:TPU:0, one launch (start us, length us, event | category | flops | bytes accessed | tf_op | source)
XLA Modules:
  0.0 81.2 jit_solution(13931521547308222335)
XLA Ops:
  0.0 0.1 pad_add_fusion.place_ref
  0.1 2.1 %pack.1 = (f32[128,128]{1,0:T(8,128)S(1)}, bf16[40,2048]{1,0:T(8,128)(2,1)S(1)}, bf16[40,2048]{1,0:T(8,128)(2,1)S(1)}, bf16[40,2048]{1,0:T(8,128)(2,1)S(1)}, bf1...) custom-call(s32[2]{0:T(128)S(1)} %pad_add_fusion.place_ref, ...), custom_call_target="tpu_custom_call" | custom-call | flops 167772160 | bytes 1572864 | tf_op jit(solution)/shard_map/pack/pallas_call | solution.py:245
  2.2 3.0 %collective-permute-start = (bf16[40,2048]{1,0:T(8,128)(2,1)S(1)}, bf16[40,2048]{1,0:T(8,128)(2,1)S(1)}, u32[]{:S(2)}, u32[]{:S(2)}) collective-permute-start(bf16[40,2048]{1,0:T(8,128)(2,1)S(1)} %get-tuple-element.47), channel_id=1, source_target_pairs={{0,2},{2,0},{4,6},{6,4},{8,10},{10,8},{12,14},{14,12},{1,3},{3,1},... | collective-permute-start | bytes 491528 | tf_op jit(solution)/shard_map/ppermute | solution.py:264
  5.2 1.6 %collective-permute-start.1 = (bf16[40,2048]{1,0:T(8,128)(2,1)S(1)}, bf16[40,2048]{1,0:T(8,128)(2,1)S(1)}, u32[]{:S(2)}, u32[]{:S(2)}) collective-permute-start(bf16[40,2048]{1,0:T(8,128)(2,1)S(1)} %get-tuple-element.48), channel_id=1, source_target_pairs={{0,4},{2,6},{4,0},{6,2},{8,12},{10,14},{12,8},{14,10},{1,5},{3,7},... | collective-permute-start | bytes 491528 | tf_op jit(solution)/shard_map/ppermute | solution.py:264
  6.8 2.6 %collective-permute-start.3 = (bf16[40,2048]{1,0:T(8,128)(2,1)S(1)}, bf16[40,2048]{1,0:T(8,128)(2,1)S(1)}, u32[]{:S(2)}, u32[]{:S(2)}) collective-permute-start(bf16[40,2048]{1,0:T(8,128)(2,1)S(1)} %get-tuple-element.51), channel_id=1, source_target_pairs={{0,8},{2,10},{4,12},{6,14},{8,0},{10,2},{12,4},{14,6},{1,9},{3,11}... | collective-permute-start | bytes 491528 | tf_op jit(solution)/shard_map/ppermute | solution.py:264
  9.4 0.3 collective-permute-start.4
  9.7 2.5 %collective-permute-start.5 = (bf16[40,2048]{1,0:T(8,128)(2,1)S(1)}, bf16[40,2048]{1,0:T(8,128)(2,1)S(1)}, u32[]{:S(2)}, u32[]{:S(2)}) collective-permute-start(bf16[40,2048]{1,0:T(8,128)(2,1)S(1)} %get-tuple-element.56), channel_id=1, source_target_pairs={{0,12},{2,14},{4,8},{6,10},{8,4},{10,6},{12,0},{14,2},{1,13},{3,15... | collective-permute-start | bytes 491528 | tf_op jit(solution)/shard_map/ppermute | solution.py:264
  12.2 0.0 collective-permute-done.refs_1_
  12.2 1.6 %collective-permute-start.2 = (bf16[40,2048]{1,0:T(8,128)(2,1)S(1)}, bf16[40,2048]{1,0:T(8,128)(2,1)S(1)}, u32[]{:S(2)}, u32[]{:S(2)}) collective-permute-start(bf16[40,2048]{1,0:T(8,128)(2,1)S(1)} %get-tuple-element.50), channel_id=1, source_target_pairs={{0,6},{2,4},{4,2},{6,0},{8,14},{10,12},{12,10},{14,8},{1,7},{3,5},... | collective-permute-start | bytes 491528 | tf_op jit(solution)/shard_map/ppermute | solution.py:264
  13.8 0.2 collective-permute-done.1.refs_2_
  14.0 3.5 %collective-permute-start.6 = (bf16[40,2048]{1,0:T(8,128)(2,1)S(1)}, bf16[40,2048]{1,0:T(8,128)(2,1)S(1)}, u32[]{:S(2)}, u32[]{:S(2)}) collective-permute-start(bf16[40,2048]{1,0:T(8,128)(2,1)S(1)} %get-tuple-element.58), channel_id=1, source_target_pairs={{0,14},{2,12},{4,10},{6,8},{8,6},{10,4},{12,2},{14,0},{1,15},{3,13... | collective-permute-start | bytes 491528 | tf_op jit(solution)/shard_map/ppermute | solution.py:264
  17.5 11.9 %load.1 = (bf16[2048,704]{1,0:T(8,128)(2,1)S(1)}, bf16[2048,704]{1,0:T(8,128)(2,1)S(1)}, bf16[704,2048]{1,0:T(8,128)(2,1)S(1)}, bf16[2048,704]{1,0:T(8,128)(2,1)...) custom-call(s32[2]{0:T(128)S(1)} %pad_add_fusion.place_ref, ...), custom_call_target="tpu_custom_call" | custom-call | bytes 34603008 | tf_op jit(solution)/shard_map/load/pallas_call | solution.py:281
  29.4 0.0 collective-permute-done.3.refs_4_
  29.4 2.2 %collective-permute-done.4.refs_5_ = bf16[40,2048]{1,0:T(8,128)(2,1)S(1)} collective-permute-done((bf16[40,2048]{1,0:T(8,128)(2,1)S(1)}, bf16[40,2048]{1,0:T(8,128)(2,1)S(1)}, u32[]{:S(2)}, u32[]{:S(2)}) %collective-permute-start.4) | collective-permute-done | bytes 163872 | tf_op jit(solution)/shard_map/ppermute | solution.py:264
  31.6 0.0 collective-permute-done.5.refs_6_
  31.6 0.0 collective-permute-done.2.refs_3_
  31.6 0.0 collective-permute-done.6.refs_7_
  31.6 0.8 %regroup.1 = (bf16[160,2048]{1,0:T(8,128)(2,1)S(1)}, bf16[160,2048]{1,0:T(8,128)(2,1)S(1)}) custom-call(bf16[40,2048]{1,0:T(8,128)(2,1)S(1)} %get-tuple-element.46.refs_0_, bf16[40,2048]{1,0:T(8,128)(2,1)S(1)} %collective-permute-done.refs_1_, bf16[40,2048]{1,0:T(8,128)(2,1)S(1)} %collective-permute-done.1.refs_2_, ...), custom_call_target="tpu_custom_call" | custom-call | flops 419430400 | bytes 2621440 | tf_op jit(solution)/shard_map/regroup/pallas_call | solution.py:296
  32.5 0.1 collective-permute-start.7
  32.5 0.5 collective-permute-start.8
  33.0 1.6 %collective-permute-done.7.theirs_ref = bf16[160,2048]{1,0:T(8,128)(2,1)S(1)} collective-permute-done((bf16[160,2048]{1,0:T(8,128)(2,1)S(1)}, bf16[160,2048]{1,0:T(8,128)(2,1)S(1)}, u32[]{:S(2)}, u32[]{:S(2)}) %collective-permute-start.7) | collective-permute-done | bytes 655392 | tf_op jit(solution)/shard_map/ppermute | solution.py:267
  34.6 3.4 %ffn.2 = (f32[160,2048]{1,0:T(8,128)S(1)}, bf16[160,2048]{1,0:T(8,128)(2,1)S(1)}) custom-call(bf16[160,2048]{1,0:T(8,128)(2,1)S(1)} %get-tuple-element.59.mine_ref, bf16[160,2048]{1,0:T(8,128)(2,1)S(1)} %collective-permute-done.7.theirs_ref, bf16[2048,704]{1,0:T(8,128)(2,1)S(1)} %get-tuple-element.60.refs_0_, ...), custom_call_target="tpu_custom_call" | custom-call | flops 2768240640 | bytes 17301504 | tf_op jit(solution)/shard_map/ffn/pallas_call | solution.py:309
  38.0 0.2 collective-permute-start.9
  38.2 0.0 collective-permute-done.8.theirs_ref
  38.2 3.6 %ffn.3 = (f32[160,2048]{1,0:T(8,128)S(1)}, bf16[160,2048]{1,0:T(8,128)(2,1)S(1)}) custom-call(bf16[160,2048]{1,0:T(8,128)(2,1)S(1)} %get-tuple-element.67.mine_ref, bf16[160,2048]{1,0:T(8,128)(2,1)S(1)} %collective-permute-done.8.theirs_ref, bf16[2048,704]{1,0:T(8,128)(2,1)S(1)} %get-tuple-element.68.refs_0_, ...), custom_call_target="tpu_custom_call" | custom-call | flops 2768240640 | bytes 17301504 | tf_op jit(solution)/shard_map/ffn/pallas_call | solution.py:309
  41.9 0.4 collective-permute-start.10
  42.3 0.0 collective-permute-done.9.other_low
  42.3 1.7 %collective-permute-done.10.other_high = bf16[160,2048]{1,0:T(8,128)(2,1)S(1)} collective-permute-done((bf16[160,2048]{1,0:T(8,128)(2,1)S(1)}, bf16[160,2048]{1,0:T(8,128)(2,1)S(1)}, u32[]{:S(2)}, u32[]{:S(2)}) %collective-permute-start.10) | collective-permute-done | bytes 655392 | tf_op jit(solution)/shard_map/ppermute | solution.py:267
  44.1 0.9 %ungroup.1 = (bf16[40,2048]{1,0:T(8,128)(2,1)S(1)}, bf16[40,2048]{1,0:T(8,128)(2,1)S(1)}, bf16[40,2048]{1,0:T(8,128)(2,1)S(1)}, bf16[40,2048]{1,0:T(8,128)(2,1)S...) custom-call(f32[160,2048]{1,0:T(8,128)S(1)} %get-tuple-element.66.ow, ...), custom_call_target="tpu_custom_call" | custom-call | flops 419430400 | bytes 2621440 | tf_op jit(solution)/shard_map/ungroup/pallas_call | solution.py:320
  45.0 2.1 %collective-permute-start.15 = (bf16[40,2048]{1,0:T(8,128)(2,1)S(1)}, bf16[40,2048]{1,0:T(8,128)(2,1)S(1)}, u32[]{:S(2)}, u32[]{:S(2)}) collective-permute-start(bf16[40,2048]{1,0:T(8,128)(2,1)S(1)} %get-tuple-element.82), channel_id=1, source_target_pairs={{0,2},{2,0},{4,6},{6,4},{8,10},{10,8},{12,14},{14,12},{1,3},{3,1},... | collective-permute-start | bytes 491528 | tf_op jit(solution)/shard_map/ppermute | solution.py:264
  47.1 2.4 %collective-permute-start.16 = (bf16[40,2048]{1,0:T(8,128)(2,1)S(1)}, bf16[40,2048]{1,0:T(8,128)(2,1)S(1)}, u32[]{:S(2)}, u32[]{:S(2)}) collective-permute-start(bf16[40,2048]{1,0:T(8,128)(2,1)S(1)} %get-tuple-element.83), channel_id=1, source_target_pairs={{0,12},{2,14},{4,8},{6,10},{8,4},{10,6},{12,0},{14,2},{1,13},{3,15... | collective-permute-start | bytes 491528 | tf_op jit(solution)/shard_map/ppermute | solution.py:264
  49.4 1.0 %collective-permute-start.17 = (bf16[40,2048]{1,0:T(8,128)(2,1)S(1)}, bf16[40,2048]{1,0:T(8,128)(2,1)S(1)}, u32[]{:S(2)}, u32[]{:S(2)}) collective-permute-start(bf16[40,2048]{1,0:T(8,128)(2,1)S(1)} %get-tuple-element.84), channel_id=1, source_target_pairs={{0,14},{2,12},{4,10},{6,8},{8,6},{10,4},{12,2},{14,0},{1,15},{3,13... | collective-permute-start | bytes 491528 | tf_op jit(solution)/shard_map/ppermute | solution.py:264
  50.4 4.7 %collective-permute-start.11 = (bf16[40,2048]{1,0:T(8,128)(2,1)S(1)}, bf16[40,2048]{1,0:T(8,128)(2,1)S(1)}, u32[]{:S(2)}, u32[]{:S(2)}) collective-permute-start(bf16[40,2048]{1,0:T(8,128)(2,1)S(1)} %get-tuple-element.77), channel_id=1, source_target_pairs={{0,4},{2,6},{4,0},{6,2},{8,12},{10,14},{12,8},{14,10},{1,5},{3,7},... | collective-permute-start | bytes 491528 | tf_op jit(solution)/shard_map/ppermute | solution.py:264
  55.2 0.9 %collective-permute-start.12 = (bf16[40,2048]{1,0:T(8,128)(2,1)S(1)}, bf16[40,2048]{1,0:T(8,128)(2,1)S(1)}, u32[]{:S(2)}, u32[]{:S(2)}) collective-permute-start(bf16[40,2048]{1,0:T(8,128)(2,1)S(1)} %get-tuple-element.78), channel_id=1, source_target_pairs={{0,6},{2,4},{4,2},{6,0},{8,14},{10,12},{12,10},{14,8},{1,7},{3,5},... | collective-permute-start | bytes 491528 | tf_op jit(solution)/shard_map/ppermute | solution.py:264
  56.1 0.0 collective-permute-done.15.refs_2_
  56.1 3.0 %collective-permute-start.13 = (bf16[40,2048]{1,0:T(8,128)(2,1)S(1)}, bf16[40,2048]{1,0:T(8,128)(2,1)S(1)}, u32[]{:S(2)}, u32[]{:S(2)}) collective-permute-start(bf16[40,2048]{1,0:T(8,128)(2,1)S(1)} %get-tuple-element.79), channel_id=1, source_target_pairs={{0,8},{2,10},{4,12},{6,14},{8,0},{10,2},{12,4},{14,6},{1,9},{3,11}... | collective-permute-start | bytes 491528 | tf_op jit(solution)/shard_map/ppermute | solution.py:264
  59.1 0.0 collective-permute-done.16.refs_3_
  59.2 4.4 %collective-permute-start.14 = (bf16[40,2048]{1,0:T(8,128)(2,1)S(1)}, bf16[40,2048]{1,0:T(8,128)(2,1)S(1)}, u32[]{:S(2)}, u32[]{:S(2)}) collective-permute-start(bf16[40,2048]{1,0:T(8,128)(2,1)S(1)} %get-tuple-element.80), channel_id=1, source_target_pairs={{0,10},{2,8},{4,14},{6,12},{8,2},{10,0},{12,6},{14,4},{1,11},{3,9}... | collective-permute-start | bytes 491528 | tf_op jit(solution)/shard_map/ppermute | solution.py:264
  63.6 0.0 collective-permute-done.17.refs_4_
  63.6 0.5 combine.2.refs_5_
  64.1 0.0 collective-permute-done.11.refs_1_
  64.1 1.7 %collective-permute-done.12.refs_2_ = bf16[40,2048]{1,0:T(8,128)(2,1)S(1)} collective-permute-done((bf16[40,2048]{1,0:T(8,128)(2,1)S(1)}, bf16[40,2048]{1,0:T(8,128)(2,1)S(1)}, u32[]{:S(2)}, u32[]{:S(2)}) %collective-permute-start.12) | collective-permute-done | bytes 163872 | tf_op jit(solution)/shard_map/ppermute | solution.py:264
  65.8 11.5 %collective-permute-done.13.refs_3_ = bf16[40,2048]{1,0:T(8,128)(2,1)S(1)} collective-permute-done((bf16[40,2048]{1,0:T(8,128)(2,1)S(1)}, bf16[40,2048]{1,0:T(8,128)(2,1)S(1)}, u32[]{:S(2)}, u32[]{:S(2)}) %collective-permute-start.13) | collective-permute-done | bytes 163872 | tf_op jit(solution)/shard_map/ppermute | solution.py:264
  77.3 2.6 %collective-permute-done.14.refs_4_ = bf16[40,2048]{1,0:T(8,128)(2,1)S(1)} collective-permute-done((bf16[40,2048]{1,0:T(8,128)(2,1)S(1)}, bf16[40,2048]{1,0:T(8,128)(2,1)S(1)}, u32[]{:S(2)}, u32[]{:S(2)}) %collective-permute-start.14) | collective-permute-done | bytes 163872 | tf_op jit(solution)/shard_map/ppermute | solution.py:264
  79.9 1.3 %combine.3 = bf16[128,2048]{1,0:T(8,128)(2,1)} custom-call(f32[128,128]{1,0:T(8,128)S(1)} %get-tuple-element.52._.refs_0_, bf16[40,2048]{1,0:T(8,128)(2,1)S(1)} %collective-permute-done.11.refs_1_, bf16[40,2048]{1,0:T(8,128)(2,1)S(1)} %collective-permute-done.12.refs_2_, bf16[40,2048]{1,0:T(8,128)(2,1)S(1)} %collective-permute-done.13.refs_3_, ...), custom_call_target="tpu_custom_call" | custom-call | flops 167772160 | bytes 1048576 | tf_op jit(solution)/shard_map/combine/pallas_call | solution.py:336
Async XLA Ops:
  2.2 10.0 %collective-permute-start = (bf16[40,2048]{1,0:T(8,128)(2,1)S(1)}, bf16[40,2048]{1,0:T(8,128)(2,1)S(1)}, u32[]{:S(2)}, u32[]{:S(2)}) collective-permute-start(bf16[40,2048]{1,0:T(8,128)(2,1)S(1)} %get-tuple-element.47), channel_id=1, source_target_pairs={{0,2},{2,0},{4,6},{6,4},{8,10},{10,8},{12,14},{14,12},{1,3},{3,1},... | collective-permute-start | bytes 491528 | tf_op jit(solution)/shard_map/ppermute | solution.py:264
  5.2 8.7 %collective-permute-start.1 = (bf16[40,2048]{1,0:T(8,128)(2,1)S(1)}, bf16[40,2048]{1,0:T(8,128)(2,1)S(1)}, u32[]{:S(2)}, u32[]{:S(2)}) collective-permute-start(bf16[40,2048]{1,0:T(8,128)(2,1)S(1)} %get-tuple-element.48), channel_id=1, source_target_pairs={{0,4},{2,6},{4,0},{6,2},{8,12},{10,14},{12,8},{14,10},{1,5},{3,7},... | collective-permute-start | bytes 491528 | tf_op jit(solution)/shard_map/ppermute | solution.py:264
  6.8 22.6 %collective-permute-start.3 = (bf16[40,2048]{1,0:T(8,128)(2,1)S(1)}, bf16[40,2048]{1,0:T(8,128)(2,1)S(1)}, u32[]{:S(2)}, u32[]{:S(2)}) collective-permute-start(bf16[40,2048]{1,0:T(8,128)(2,1)S(1)} %get-tuple-element.51), channel_id=1, source_target_pairs={{0,8},{2,10},{4,12},{6,14},{8,0},{10,2},{12,4},{14,6},{1,9},{3,11}... | collective-permute-start | bytes 491528 | tf_op jit(solution)/shard_map/ppermute | solution.py:264
  9.4 22.2 %collective-permute-start.4 = (bf16[40,2048]{1,0:T(8,128)(2,1)S(1)}, bf16[40,2048]{1,0:T(8,128)(2,1)S(1)}, u32[]{:S(2)}, u32[]{:S(2)}) collective-permute-start(bf16[40,2048]{1,0:T(8,128)(2,1)S(1)} %get-tuple-element.55), channel_id=1, source_target_pairs={{0,10},{2,8},{4,14},{6,12},{8,2},{10,0},{12,6},{14,4},{1,11},{3,9}... | collective-permute-start | bytes 491528 | tf_op jit(solution)/shard_map/ppermute | solution.py:264
  9.7 21.9 %collective-permute-start.5 = (bf16[40,2048]{1,0:T(8,128)(2,1)S(1)}, bf16[40,2048]{1,0:T(8,128)(2,1)S(1)}, u32[]{:S(2)}, u32[]{:S(2)}) collective-permute-start(bf16[40,2048]{1,0:T(8,128)(2,1)S(1)} %get-tuple-element.56), channel_id=1, source_target_pairs={{0,12},{2,14},{4,8},{6,10},{8,4},{10,6},{12,0},{14,2},{1,13},{3,15... | collective-permute-start | bytes 491528 | tf_op jit(solution)/shard_map/ppermute | solution.py:264
  12.2 19.4 %collective-permute-start.2 = (bf16[40,2048]{1,0:T(8,128)(2,1)S(1)}, bf16[40,2048]{1,0:T(8,128)(2,1)S(1)}, u32[]{:S(2)}, u32[]{:S(2)}) collective-permute-start(bf16[40,2048]{1,0:T(8,128)(2,1)S(1)} %get-tuple-element.50), channel_id=1, source_target_pairs={{0,6},{2,4},{4,2},{6,0},{8,14},{10,12},{12,10},{14,8},{1,7},{3,5},... | collective-permute-start | bytes 491528 | tf_op jit(solution)/shard_map/ppermute | solution.py:264
  14.0 17.6 %collective-permute-start.6 = (bf16[40,2048]{1,0:T(8,128)(2,1)S(1)}, bf16[40,2048]{1,0:T(8,128)(2,1)S(1)}, u32[]{:S(2)}, u32[]{:S(2)}) collective-permute-start(bf16[40,2048]{1,0:T(8,128)(2,1)S(1)} %get-tuple-element.58), channel_id=1, source_target_pairs={{0,14},{2,12},{4,10},{6,8},{8,6},{10,4},{12,2},{14,0},{1,15},{3,13... | collective-permute-start | bytes 491528 | tf_op jit(solution)/shard_map/ppermute | solution.py:264
  32.5 2.2 %collective-permute-start.7 = (bf16[160,2048]{1,0:T(8,128)(2,1)S(1)}, bf16[160,2048]{1,0:T(8,128)(2,1)S(1)}, u32[]{:S(2)}, u32[]{:S(2)}) collective-permute-start(bf16[160,2048]{1,0:T(8,128)(2,1)S(1)} %get-tuple-element.59.mine_ref), channel_id=1, source_target_pairs={{0,1},{1,0},{2,3},{3,2},{4,5},{5,4},{6,7},{7,6},{8,9},{9,8},{10,11... | collective-permute-start | bytes 1966088 | tf_op jit(solution)/shard_map/ppermute | solution.py:267
  32.5 5.7 %collective-permute-start.8 = (bf16[160,2048]{1,0:T(8,128)(2,1)S(1)}, bf16[160,2048]{1,0:T(8,128)(2,1)S(1)}, u32[]{:S(2)}, u32[]{:S(2)}) collective-permute-start(bf16[160,2048]{1,0:T(8,128)(2,1)S(1)} %get-tuple-element.67.mine_ref), channel_id=1, source_target_pairs={{0,1},{1,0},{2,3},{3,2},{4,5},{5,4},{6,7},{7,6},{8,9},{9,8},{10,11... | collective-permute-start | bytes 1966088 | tf_op jit(solution)/shard_map/ppermute | solution.py:267
  38.0 4.3 %collective-permute-start.9 = (bf16[160,2048]{1,0:T(8,128)(2,1)S(1)}, bf16[160,2048]{1,0:T(8,128)(2,1)S(1)}, u32[]{:S(2)}, u32[]{:S(2)}) collective-permute-start(bf16[160,2048]{1,0:T(8,128)(2,1)S(1)} %get-tuple-element.75), channel_id=1, source_target_pairs={{0,1},{1,0},{2,3},{3,2},{4,5},{5,4},{6,7},{7,6},{8,9},{9,8},{10,11... | collective-permute-start | bytes 1966088 | tf_op jit(solution)/shard_map/ppermute | solution.py:267
  41.9 2.2 %collective-permute-start.10 = (bf16[160,2048]{1,0:T(8,128)(2,1)S(1)}, bf16[160,2048]{1,0:T(8,128)(2,1)S(1)}, u32[]{:S(2)}, u32[]{:S(2)}) collective-permute-start(bf16[160,2048]{1,0:T(8,128)(2,1)S(1)} %get-tuple-element.76), channel_id=1, source_target_pairs={{0,1},{1,0},{2,3},{3,2},{4,5},{5,4},{6,7},{7,6},{8,9},{9,8},{10,11... | collective-permute-start | bytes 1966088 | tf_op jit(solution)/shard_map/ppermute | solution.py:267
  45.0 11.1 %collective-permute-start.15 = (bf16[40,2048]{1,0:T(8,128)(2,1)S(1)}, bf16[40,2048]{1,0:T(8,128)(2,1)S(1)}, u32[]{:S(2)}, u32[]{:S(2)}) collective-permute-start(bf16[40,2048]{1,0:T(8,128)(2,1)S(1)} %get-tuple-element.82), channel_id=1, source_target_pairs={{0,2},{2,0},{4,6},{6,4},{8,10},{10,8},{12,14},{14,12},{1,3},{3,1},... | collective-permute-start | bytes 491528 | tf_op jit(solution)/shard_map/ppermute | solution.py:264
  47.1 12.1 %collective-permute-start.16 = (bf16[40,2048]{1,0:T(8,128)(2,1)S(1)}, bf16[40,2048]{1,0:T(8,128)(2,1)S(1)}, u32[]{:S(2)}, u32[]{:S(2)}) collective-permute-start(bf16[40,2048]{1,0:T(8,128)(2,1)S(1)} %get-tuple-element.83), channel_id=1, source_target_pairs={{0,12},{2,14},{4,8},{6,10},{8,4},{10,6},{12,0},{14,2},{1,13},{3,15... | collective-permute-start | bytes 491528 | tf_op jit(solution)/shard_map/ppermute | solution.py:264
  49.4 14.1 %collective-permute-start.17 = (bf16[40,2048]{1,0:T(8,128)(2,1)S(1)}, bf16[40,2048]{1,0:T(8,128)(2,1)S(1)}, u32[]{:S(2)}, u32[]{:S(2)}) collective-permute-start(bf16[40,2048]{1,0:T(8,128)(2,1)S(1)} %get-tuple-element.84), channel_id=1, source_target_pairs={{0,14},{2,12},{4,10},{6,8},{8,6},{10,4},{12,2},{14,0},{1,15},{3,13... | collective-permute-start | bytes 491528 | tf_op jit(solution)/shard_map/ppermute | solution.py:264
  50.4 13.7 %collective-permute-start.11 = (bf16[40,2048]{1,0:T(8,128)(2,1)S(1)}, bf16[40,2048]{1,0:T(8,128)(2,1)S(1)}, u32[]{:S(2)}, u32[]{:S(2)}) collective-permute-start(bf16[40,2048]{1,0:T(8,128)(2,1)S(1)} %get-tuple-element.77), channel_id=1, source_target_pairs={{0,4},{2,6},{4,0},{6,2},{8,12},{10,14},{12,8},{14,10},{1,5},{3,7},... | collective-permute-start | bytes 491528 | tf_op jit(solution)/shard_map/ppermute | solution.py:264
  55.2 10.6 %collective-permute-start.12 = (bf16[40,2048]{1,0:T(8,128)(2,1)S(1)}, bf16[40,2048]{1,0:T(8,128)(2,1)S(1)}, u32[]{:S(2)}, u32[]{:S(2)}) collective-permute-start(bf16[40,2048]{1,0:T(8,128)(2,1)S(1)} %get-tuple-element.78), channel_id=1, source_target_pairs={{0,6},{2,4},{4,2},{6,0},{8,14},{10,12},{12,10},{14,8},{1,7},{3,5},... | collective-permute-start | bytes 491528 | tf_op jit(solution)/shard_map/ppermute | solution.py:264
  56.1 21.2 %collective-permute-start.13 = (bf16[40,2048]{1,0:T(8,128)(2,1)S(1)}, bf16[40,2048]{1,0:T(8,128)(2,1)S(1)}, u32[]{:S(2)}, u32[]{:S(2)}) collective-permute-start(bf16[40,2048]{1,0:T(8,128)(2,1)S(1)} %get-tuple-element.79), channel_id=1, source_target_pairs={{0,8},{2,10},{4,12},{6,14},{8,0},{10,2},{12,4},{14,6},{1,9},{3,11}... | collective-permute-start | bytes 491528 | tf_op jit(solution)/shard_map/ppermute | solution.py:264
  59.2 20.7 %collective-permute-start.14 = (bf16[40,2048]{1,0:T(8,128)(2,1)S(1)}, bf16[40,2048]{1,0:T(8,128)(2,1)S(1)}, u32[]{:S(2)}, u32[]{:S(2)}) collective-permute-start(bf16[40,2048]{1,0:T(8,128)(2,1)S(1)} %get-tuple-element.80), channel_id=1, source_target_pairs={{0,10},{2,8},{4,14},{6,12},{8,2},{10,0},{12,6},{14,4},{1,11},{3,9}... | collective-permute-start | bytes 491528 | tf_op jit(solution)/shard_map/ppermute | solution.py:264

commit v6 on v5

--- a/solution.py
+++ b/solution.py
@@ -110,8 +110,8 @@
         for g in range(groups):
             blocks[g][:, c : c + step] = got[g * block : (g + 1) * block, :]
     columns = [s.astype(jnp.float32) for s in slots] + [gates_ref[...]]
-    columns.append(jnp.zeros((rows - 2 * TOPK, rows), jnp.float32))
-    route_ref[...] = jnp.concatenate(columns, axis=0).T
+    columns.append(jnp.zeros((8 - 2 * TOPK, rows), jnp.float32))
+    route_ref[...] = jnp.concatenate(columns, axis=0)
 
 
 def regroup_kernel(local_experts, count, *refs):
@@ -152,9 +152,9 @@
             refs[k][:, at] = got[k * block : (k + 1) * block, :]
 
 
-def load_kernel(half, place_ref, _, gate_hbm, up_hbm, down_hbm, *refs):
+def load_kernel(half, place_ref, route_ref, gate_hbm, up_hbm, down_hbm, *refs):
     count = 3 * gate_hbm.shape[0]
-    outs, staged, sems = refs[:count], refs[count], refs[count + 1]
+    outs, columns_ref, staged, sems = refs[:count], refs[count], refs[count + 1], refs[count + 2]
     depth = staged.shape[0]
     first = pl.multiple_of(place_ref[1] * half, 8)
     turned, plain = [], []
@@ -166,6 +166,9 @@
         plain.append(pltpu.make_async_copy(source, outs[3 * e + 2], sems.at[3 * e + 2]))
     for at in range(depth):
         turned[at][0].start()
+    rows = route_ref.shape[1]
+    rest = jnp.zeros((rows - route_ref.shape[0], rows), jnp.float32)
+    columns_ref[...] = jnp.concatenate([route_ref[...], rest], axis=0).T
     for n, (copy, at, slot) in enumerate(turned):
         copy.wait()
         step = 256
@@ -244,7 +247,7 @@
 
     packed = pl.pallas_call(
         functools.partial(pack_kernel, local_experts, groups),
-        out_shape=[jax.ShapeDtypeStruct((rows, rows), jnp.float32)]
+        out_shape=[jax.ShapeDtypeStruct((8, rows), jnp.float32)]
         + [jax.ShapeDtypeStruct((block, width), bf16)] * groups,
         in_specs=[smem] + [hbm] * 3,
         out_specs=whole(1 + groups),
@@ -278,11 +281,12 @@
     share = jax.ShapeDtypeStruct((half, width), bf16)
     turned = jax.ShapeDtypeStruct((width, half), bf16)
     pieces = 3 * local_experts
-    weights = pl.pallas_call(
+    *weights, columns = pl.pallas_call(
         functools.partial(load_kernel, half),
-        out_shape=[turned, turned, share] * local_experts,
+        out_shape=[turned, turned, share] * local_experts
+        + [jax.ShapeDtypeStruct((rows, rows), jnp.float32)],
         in_specs=[smem] + whole(1) + [hbm] * 3,
-        out_specs=whole(pieces),
+        out_specs=whole(pieces + 1),
         scratch_shapes=[VMEM((3, half, width), bf16), pltpu.SemaphoreType.DMA((pieces,))],
         compiler_params=params(4 + 3 * 3),
         cost_estimate=cost(0, 6 * local_experts * half * width),
@@ -329,7 +333,7 @@
     returned = {k: hop(blocks[k], k) if k else blocks[k] for k in [0] + order}
 
     total = None
-    parts = [[0, 1, 6, 7], [2, 3, 4, 5]]
+    parts = [[0, 1, 6, 7, 2, 3], [4, 5]]
     for chunk in parts:
         first, final = total is None, chunk is parts[-1]
         count = len(chunk)
@@ -342,7 +346,7 @@
             compiler_params=params(4),
             cost_estimate=cost(4 * rows * count * block * width, 4 * rows * width),
             name="combine",
-        )(route, *[returned[k] for k in chunk], *([] if first else [total]))
+        )(columns, *[returned[k] for k in chunk], *([] if first else [total]))
     return total
 
 

time: 81.3 us -> 81.4 us (level)
  no operation moved by 1% of the time
where the time goes in v6:
time: 81.4 us; the launch traced here: 81.2 us
  starting transfers between devices  34.9 us (43%)
  Pallas kernels  24.7 us (30%)
  waiting for transfers between devices  21.5 us (26%)
    ppermute x14, starting transfers between devices, hop(): return lax.ppermute(x, 'expert', [(i, i ^ k) for i in range(groups)])  33.6 us
    ppermute x14, waiting for transfers between devices, hop(): return lax.ppermute(x, 'expert', [(i, i ^ k) for i in range(groups)])  18.2 us
    pallas_call x1, Pallas kernels, fast(): pl.pallas_call(functools.partial(load_kernel, half), out_shape=[turned, t...  11.9 us
    pallas_call x2, Pallas kernels, fast(): pl.pallas_call(functools.partial(ffn_kernel, groups * CAP), out_shape=[ja...  7.09 us
    ppermute x4, waiting for transfers between devices, swap(): return lax.ppermute(x, 'dp', [(0, 1), (1, 0)])  3.31 us
    pallas_call x1, Pallas kernels, fast(): pl.pallas_call(functools.partial(pack_kernel, local_experts, groups), out...  2.14 us
    pallas_call x2, Pallas kernels, fast(): pl.pallas_call(functools.partial(combine_kernel, block, chunk, first), ou...  1.78 us
  transfers between devices with their start and end apart: 18, of which 7 were waited for; matrix products, arithmetic and copies ran while one was open for 0% of the time, Pallas kernels for 24%

profile of v6, /device:TPU:0, one launch (start us, length us, event | category | flops | bytes accessed | tf_op | source)
XLA Modules:
  0.0 81.2 jit_solution(14722139746284137677)
XLA Ops:
  0.0 0.1 pad_add_fusion.place_ref
  0.1 2.1 %pack.1 = (f32[8,128]{1,0:T(8,128)S(1)}, bf16[40,2048]{1,0:T(8,128)(2,1)S(1)}, bf16[40,2048]{1,0:T(8,128)(2,1)S(1)}, bf16[40,2048]{1,0:T(8,128)(2,1)S(1)}, bf16[...) custom-call(s32[2]{0:T(128)S(1)} %pad_add_fusion.place_ref, ...), custom_call_target="tpu_custom_call" | custom-call | flops 167772160 | bytes 1572864 | tf_op jit(solution)/shard_map/pack/pallas_call | solution.py:248
  2.2 3.0 %collective-permute-start = (bf16[40,2048]{1,0:T(8,128)(2,1)S(1)}, bf16[40,2048]{1,0:T(8,128)(2,1)S(1)}, u32[]{:S(2)}, u32[]{:S(2)}) collective-permute-start(bf16[40,2048]{1,0:T(8,128)(2,1)S(1)} %get-tuple-element.47), channel_id=1, source_target_pairs={{0,2},{2,0},{4,6},{6,4},{8,10},{10,8},{12,14},{14,12},{1,3},{3,1},... | collective-permute-start | bytes 491528 | tf_op jit(solution)/shard_map/ppermute | solution.py:267
  5.2 1.6 %collective-permute-start.1 = (bf16[40,2048]{1,0:T(8,128)(2,1)S(1)}, bf16[40,2048]{1,0:T(8,128)(2,1)S(1)}, u32[]{:S(2)}, u32[]{:S(2)}) collective-permute-start(bf16[40,2048]{1,0:T(8,128)(2,1)S(1)} %get-tuple-element.48), channel_id=1, source_target_pairs={{0,4},{2,6},{4,0},{6,2},{8,12},{10,14},{12,8},{14,10},{1,5},{3,7},... | collective-permute-start | bytes 491528 | tf_op jit(solution)/shard_map/ppermute | solution.py:267
  6.8 2.6 %collective-permute-start.3 = (bf16[40,2048]{1,0:T(8,128)(2,1)S(1)}, bf16[40,2048]{1,0:T(8,128)(2,1)S(1)}, u32[]{:S(2)}, u32[]{:S(2)}) collective-permute-start(bf16[40,2048]{1,0:T(8,128)(2,1)S(1)} %get-tuple-element.54), channel_id=1, source_target_pairs={{0,8},{2,10},{4,12},{6,14},{8,0},{10,2},{12,4},{14,6},{1,9},{3,11}... | collective-permute-start | bytes 491528 | tf_op jit(solution)/shard_map/ppermute | solution.py:267
  9.4 0.3 collective-permute-start.4
  9.7 2.5 %collective-permute-start.5 = (bf16[40,2048]{1,0:T(8,128)(2,1)S(1)}, bf16[40,2048]{1,0:T(8,128)(2,1)S(1)}, u32[]{:S(2)}, u32[]{:S(2)}) collective-permute-start(bf16[40,2048]{1,0:T(8,128)(2,1)S(1)} %get-tuple-element.58), channel_id=1, source_target_pairs={{0,12},{2,14},{4,8},{6,10},{8,4},{10,6},{12,0},{14,2},{1,13},{3,15... | collective-permute-start | bytes 491528 | tf_op jit(solution)/shard_map/ppermute | solution.py:267
  12.2 0.0 collective-permute-done.refs_1_
  12.2 1.6 %collective-permute-start.2 = (bf16[40,2048]{1,0:T(8,128)(2,1)S(1)}, bf16[40,2048]{1,0:T(8,128)(2,1)S(1)}, u32[]{:S(2)}, u32[]{:S(2)}) collective-permute-start(bf16[40,2048]{1,0:T(8,128)(2,1)S(1)} %get-tuple-element.53), channel_id=1, source_target_pairs={{0,6},{2,4},{4,2},{6,0},{8,14},{10,12},{12,10},{14,8},{1,7},{3,5},... | collective-permute-start | bytes 491528 | tf_op jit(solution)/shard_map/ppermute | solution.py:267
  13.8 0.2 collective-permute-done.1.refs_2_
  14.0 3.5 %collective-permute-start.6 = (bf16[40,2048]{1,0:T(8,128)(2,1)S(1)}, bf16[40,2048]{1,0:T(8,128)(2,1)S(1)}, u32[]{:S(2)}, u32[]{:S(2)}) collective-permute-start(bf16[40,2048]{1,0:T(8,128)(2,1)S(1)} %get-tuple-element.60), channel_id=1, source_target_pairs={{0,14},{2,12},{4,10},{6,8},{8,6},{10,4},{12,2},{14,0},{1,15},{3,13... | collective-permute-start | bytes 491528 | tf_op jit(solution)/shard_map/ppermute | solution.py:267
  17.5 11.9 %load.1 = (bf16[2048,704]{1,0:T(8,128)(2,1)S(1)}, bf16[2048,704]{1,0:T(8,128)(2,1)S(1)}, bf16[704,2048]{1,0:T(8,128)(2,1)S(1)}, bf16[2048,704]{1,0:T(8,128)(2,1)...) custom-call(s32[2]{0:T(128)S(1)} %pad_add_fusion.place_ref, ...), custom_call_target="tpu_custom_call" | custom-call | bytes 34603008 | tf_op jit(solution)/shard_map/load/pallas_call | solution.py:284
  29.4 0.0 collective-permute-done.3.refs_4_
  29.4 2.2 %collective-permute-done.4.refs_5_ = bf16[40,2048]{1,0:T(8,128)(2,1)S(1)} collective-permute-done((bf16[40,2048]{1,0:T(8,128)(2,1)S(1)}, bf16[40,2048]{1,0:T(8,128)(2,1)S(1)}, u32[]{:S(2)}, u32[]{:S(2)}) %collective-permute-start.4) | collective-permute-done | bytes 163872 | tf_op jit(solution)/shard_map/ppermute | solution.py:267
  31.6 0.0 collective-permute-done.5.refs_6_
  31.6 0.0 collective-permute-done.2.refs_3_
  31.6 0.0 collective-permute-done.6.refs_7_
  31.6 0.9 %regroup.1 = (bf16[160,2048]{1,0:T(8,128)(2,1)S(1)}, bf16[160,2048]{1,0:T(8,128)(2,1)S(1)}) custom-call(bf16[40,2048]{1,0:T(8,128)(2,1)S(1)} %get-tuple-element.51.refs_0_, bf16[40,2048]{1,0:T(8,128)(2,1)S(1)} %collective-permute-done.refs_1_, bf16[40,2048]{1,0:T(8,128)(2,1)S(1)} %collective-permute-done.1.refs_2_, ...), custom_call_target="tpu_custom_call" | custom-call | flops 419430400 | bytes 2621440 | tf_op jit(solution)/shard_map/regroup/pallas_call | solution.py:300
  32.5 0.1 collective-permute-start.7
  32.5 0.5 collective-permute-start.8
  33.0 1.6 %collective-permute-done.7.theirs_ref = bf16[160,2048]{1,0:T(8,128)(2,1)S(1)} collective-permute-done((bf16[160,2048]{1,0:T(8,128)(2,1)S(1)}, bf16[160,2048]{1,0:T(8,128)(2,1)S(1)}, u32[]{:S(2)}, u32[]{:S(2)}) %collective-permute-start.7) | collective-permute-done | bytes 655392 | tf_op jit(solution)/shard_map/ppermute | solution.py:270
  34.6 3.4 %ffn.2 = (f32[160,2048]{1,0:T(8,128)S(1)}, bf16[160,2048]{1,0:T(8,128)(2,1)S(1)}) custom-call(bf16[160,2048]{1,0:T(8,128)(2,1)S(1)} %get-tuple-element.61.mine_ref, bf16[160,2048]{1,0:T(8,128)(2,1)S(1)} %collective-permute-done.7.theirs_ref, bf16[2048,704]{1,0:T(8,128)(2,1)S(1)} %get-tuple-element.62.refs_0_, ...), custom_call_target="tpu_custom_call" | custom-call | flops 2768240640 | bytes 17301504 | tf_op jit(solution)/shard_map/ffn/pallas_call | solution.py:313
  38.1 0.2 collective-permute-start.9
  38.3 0.0 collective-permute-done.8.theirs_ref
  38.3 3.6 %ffn.3 = (f32[160,2048]{1,0:T(8,128)S(1)}, bf16[160,2048]{1,0:T(8,128)(2,1)S(1)}) custom-call(bf16[160,2048]{1,0:T(8,128)(2,1)S(1)} %get-tuple-element.69.mine_ref, bf16[160,2048]{1,0:T(8,128)(2,1)S(1)} %collective-permute-done.8.theirs_ref, bf16[2048,704]{1,0:T(8,128)(2,1)S(1)} %get-tuple-element.70.refs_0_, ...), custom_call_target="tpu_custom_call" | custom-call | flops 2768240640 | bytes 17301504 | tf_op jit(solution)/shard_map/ffn/pallas_call | solution.py:313
  41.9 0.4 collective-permute-start.10
  42.4 0.0 collective-permute-done.9.other_low
  42.4 1.7 %collective-permute-done.10.other_high = bf16[160,2048]{1,0:T(8,128)(2,1)S(1)} collective-permute-done((bf16[160,2048]{1,0:T(8,128)(2,1)S(1)}, bf16[160,2048]{1,0:T(8,128)(2,1)S(1)}, u32[]{:S(2)}, u32[]{:S(2)}) %collective-permute-start.10) | collective-permute-done | bytes 655392 | tf_op jit(solution)/shard_map/ppermute | solution.py:270
  44.1 0.9 %ungroup.1 = (bf16[40,2048]{1,0:T(8,128)(2,1)S(1)}, bf16[40,2048]{1,0:T(8,128)(2,1)S(1)}, bf16[40,2048]{1,0:T(8,128)(2,1)S(1)}, bf16[40,2048]{1,0:T(8,128)(2,1)S...) custom-call(f32[160,2048]{1,0:T(8,128)S(1)} %get-tuple-element.68.ow, ...), custom_call_target="tpu_custom_call" | custom-call | flops 419430400 | bytes 2621440 | tf_op jit(solution)/shard_map/ungroup/pallas_call | solution.py:324
  45.0 2.1 %collective-permute-start.13 = (bf16[40,2048]{1,0:T(8,128)(2,1)S(1)}, bf16[40,2048]{1,0:T(8,128)(2,1)S(1)}, u32[]{:S(2)}, u32[]{:S(2)}) collective-permute-start(bf16[40,2048]{1,0:T(8,128)(2,1)S(1)} %get-tuple-element.82), channel_id=1, source_target_pairs={{0,2},{2,0},{4,6},{6,4},{8,10},{10,8},{12,14},{14,12},{1,3},{3,1},... | collective-permute-start | bytes 491528 | tf_op jit(solution)/shard_map/ppermute | solution.py:267
  47.1 2.4 %collective-permute-start.14 = (bf16[40,2048]{1,0:T(8,128)(2,1)S(1)}, bf16[40,2048]{1,0:T(8,128)(2,1)S(1)}, u32[]{:S(2)}, u32[]{:S(2)}) collective-permute-start(bf16[40,2048]{1,0:T(8,128)(2,1)S(1)} %get-tuple-element.83), channel_id=1, source_target_pairs={{0,12},{2,14},{4,8},{6,10},{8,4},{10,6},{12,0},{14,2},{1,13},{3,15... | collective-permute-start | bytes 491528 | tf_op jit(solution)/shard_map/ppermute | solution.py:267
  49.5 1.0 %collective-permute-start.15 = (bf16[40,2048]{1,0:T(8,128)(2,1)S(1)}, bf16[40,2048]{1,0:T(8,128)(2,1)S(1)}, u32[]{:S(2)}, u32[]{:S(2)}) collective-permute-start(bf16[40,2048]{1,0:T(8,128)(2,1)S(1)} %get-tuple-element.84), channel_id=1, source_target_pairs={{0,14},{2,12},{4,10},{6,8},{8,6},{10,4},{12,2},{14,0},{1,15},{3,13... | collective-permute-start | bytes 491528 | tf_op jit(solution)/shard_map/ppermute | solution.py:267
  50.5 4.8 %collective-permute-start.16 = (bf16[40,2048]{1,0:T(8,128)(2,1)S(1)}, bf16[40,2048]{1,0:T(8,128)(2,1)S(1)}, u32[]{:S(2)}, u32[]{:S(2)}) collective-permute-start(bf16[40,2048]{1,0:T(8,128)(2,1)S(1)} %get-tuple-element.85), channel_id=1, source_target_pairs={{0,4},{2,6},{4,0},{6,2},{8,12},{10,14},{12,8},{14,10},{1,5},{3,7},... | collective-permute-start | bytes 491528 | tf_op jit(solution)/shard_map/ppermute | solution.py:267
  55.2 0.9 %collective-permute-start.17 = (bf16[40,2048]{1,0:T(8,128)(2,1)S(1)}, bf16[40,2048]{1,0:T(8,128)(2,1)S(1)}, u32[]{:S(2)}, u32[]{:S(2)}) collective-permute-start(bf16[40,2048]{1,0:T(8,128)(2,1)S(1)} %get-tuple-element.86), channel_id=1, source_target_pairs={{0,6},{2,4},{4,2},{6,0},{8,14},{10,12},{12,10},{14,8},{1,7},{3,5},... | collective-permute-start | bytes 491528 | tf_op jit(solution)/shard_map/ppermute | solution.py:267
  56.2 0.0 collective-permute-done.13.refs_2_
  56.2 3.1 %collective-permute-start.11 = (bf16[40,2048]{1,0:T(8,128)(2,1)S(1)}, bf16[40,2048]{1,0:T(8,128)(2,1)S(1)}, u32[]{:S(2)}, u32[]{:S(2)}) collective-permute-start(bf16[40,2048]{1,0:T(8,128)(2,1)S(1)} %get-tuple-element.79), channel_id=1, source_target_pairs={{0,8},{2,10},{4,12},{6,14},{8,0},{10,2},{12,4},{14,6},{1,9},{3,11}... | collective-permute-start | bytes 491528 | tf_op jit(solution)/shard_map/ppermute | solution.py:267
  59.2 0.0 collective-permute-done.14.refs_3_
  59.2 4.4 %collective-permute-start.12 = (bf16[40,2048]{1,0:T(8,128)(2,1)S(1)}, bf16[40,2048]{1,0:T(8,128)(2,1)S(1)}, u32[]{:S(2)}, u32[]{:S(2)}) collective-permute-start(bf16[40,2048]{1,0:T(8,128)(2,1)S(1)} %get-tuple-element.80), channel_id=1, source_target_pairs={{0,10},{2,8},{4,14},{6,12},{8,2},{10,0},{12,6},{14,4},{1,11},{3,9}... | collective-permute-start | bytes 491528 | tf_op jit(solution)/shard_map/ppermute | solution.py:267
  63.7 0.0 collective-permute-done.15.refs_4_
  63.7 0.0 collective-permute-done.16.refs_5_
  63.7 2.1 %collective-permute-done.17.refs_6_ = bf16[40,2048]{1,0:T(8,128)(2,1)S(1)} collective-permute-done((bf16[40,2048]{1,0:T(8,128)(2,1)S(1)}, bf16[40,2048]{1,0:T(8,128)(2,1)S(1)}, u32[]{:S(2)}, u32[]{:S(2)}) %collective-permute-start.17) | collective-permute-done | bytes 163872 | tf_op jit(solution)/shard_map/ppermute | solution.py:267
  65.8 0.5 combine.2.refs_3_
  66.3 11.1 %collective-permute-done.11.refs_1_ = bf16[40,2048]{1,0:T(8,128)(2,1)S(1)} collective-permute-done((bf16[40,2048]{1,0:T(8,128)(2,1)S(1)}, bf16[40,2048]{1,0:T(8,128)(2,1)S(1)}, u32[]{:S(2)}, u32[]{:S(2)}) %collective-permute-start.11) | collective-permute-done | bytes 163872 | tf_op jit(solution)/shard_map/ppermute | solution.py:267
  77.4 2.5 %collective-permute-done.12.refs_2_ = bf16[40,2048]{1,0:T(8,128)(2,1)S(1)} collective-permute-done((bf16[40,2048]{1,0:T(8,128)(2,1)S(1)}, bf16[40,2048]{1,0:T(8,128)(2,1)S(1)}, u32[]{:S(2)}, u32[]{:S(2)}) %collective-permute-start.12) | collective-permute-done | bytes 163872 | tf_op jit(solution)/shard_map/ppermute | solution.py:267
  79.9 1.3 %combine.3 = bf16[128,2048]{1,0:T(8,128)(2,1)} custom-call(f32[128,128]{1,0:T(8,128)S(1)} %get-tuple-element.50.refs_0_, bf16[40,2048]{1,0:T(8,128)(2,1)S(1)} %collective-permute-done.11.refs_1_, bf16[40,2048]{1,0:T(8,128)(2,1)S(1)} %collective-permute-done.12.refs_2_, f32[128,2048]{1,0:T(8,128)S(1)} %combine.2.refs_3_), custom_call_target="tpu_custom_call" | custom-call | flops 83886080 | bytes 1048576 | tf_op jit(solution)/shard_map/combine/pallas_call | solution.py:340
Async XLA Ops:
  2.2 10.0 %collective-permute-start = (bf16[40,2048]{1,0:T(8,128)(2,1)S(1)}, bf16[40,2048]{1,0:T(8,128)(2,1)S(1)}, u32[]{:S(2)}, u32[]{:S(2)}) collective-permute-start(bf16[40,2048]{1,0:T(8,128)(2,1)S(1)} %get-tuple-element.47), channel_id=1, source_target_pairs={{0,2},{2,0},{4,6},{6,4},{8,10},{10,8},{12,14},{14,12},{1,3},{3,1},... | collective-permute-start | bytes 491528 | tf_op jit(solution)/shard_map/ppermute | solution.py:267
  5.2 8.8 %collective-permute-start.1 = (bf16[40,2048]{1,0:T(8,128)(2,1)S(1)}, bf16[40,2048]{1,0:T(8,128)(2,1)S(1)}, u32[]{:S(2)}, u32[]{:S(2)}) collective-permute-start(bf16[40,2048]{1,0:T(8,128)(2,1)S(1)} %get-tuple-element.48), channel_id=1, source_target_pairs={{0,4},{2,6},{4,0},{6,2},{8,12},{10,14},{12,8},{14,10},{1,5},{3,7},... | collective-permute-start | bytes 491528 | tf_op jit(solution)/shard_map/ppermute | solution.py:267
  6.8 22.6 %collective-permute-start.3 = (bf16[40,2048]{1,0:T(8,128)(2,1)S(1)}, bf16[40,2048]{1,0:T(8,128)(2,1)S(1)}, u32[]{:S(2)}, u32[]{:S(2)}) collective-permute-start(bf16[40,2048]{1,0:T(8,128)(2,1)S(1)} %get-tuple-element.54), channel_id=1, source_target_pairs={{0,8},{2,10},{4,12},{6,14},{8,0},{10,2},{12,4},{14,6},{1,9},{3,11}... | collective-permute-start | bytes 491528 | tf_op jit(solution)/shard_map/ppermute | solution.py:267
  9.4 22.2 %collective-permute-start.4 = (bf16[40,2048]{1,0:T(8,128)(2,1)S(1)}, bf16[40,2048]{1,0:T(8,128)(2,1)S(1)}, u32[]{:S(2)}, u32[]{:S(2)}) collective-permute-start(bf16[40,2048]{1,0:T(8,128)(2,1)S(1)} %get-tuple-element.57), channel_id=1, source_target_pairs={{0,10},{2,8},{4,14},{6,12},{8,2},{10,0},{12,6},{14,4},{1,11},{3,9}... | collective-permute-start | bytes 491528 | tf_op jit(solution)/shard_map/ppermute | solution.py:267
  9.7 21.9 %collective-permute-start.5 = (bf16[40,2048]{1,0:T(8,128)(2,1)S(1)}, bf16[40,2048]{1,0:T(8,128)(2,1)S(1)}, u32[]{:S(2)}, u32[]{:S(2)}) collective-permute-start(bf16[40,2048]{1,0:T(8,128)(2,1)S(1)} %get-tuple-element.58), channel_id=1, source_target_pairs={{0,12},{2,14},{4,8},{6,10},{8,4},{10,6},{12,0},{14,2},{1,13},{3,15... | collective-permute-start | bytes 491528 | tf_op jit(solution)/shard_map/ppermute | solution.py:267
  12.2 19.4 %collective-permute-start.2 = (bf16[40,2048]{1,0:T(8,128)(2,1)S(1)}, bf16[40,2048]{1,0:T(8,128)(2,1)S(1)}, u32[]{:S(2)}, u32[]{:S(2)}) collective-permute-start(bf16[40,2048]{1,0:T(8,128)(2,1)S(1)} %get-tuple-element.53), channel_id=1, source_target_pairs={{0,6},{2,4},{4,2},{6,0},{8,14},{10,12},{12,10},{14,8},{1,7},{3,5},... | collective-permute-start | bytes 491528 | tf_op jit(solution)/shard_map/ppermute | solution.py:267
  14.0 17.6 %collective-permute-start.6 = (bf16[40,2048]{1,0:T(8,128)(2,1)S(1)}, bf16[40,2048]{1,0:T(8,128)(2,1)S(1)}, u32[]{:S(2)}, u32[]{:S(2)}) collective-permute-start(bf16[40,2048]{1,0:T(8,128)(2,1)S(1)} %get-tuple-element.60), channel_id=1, source_target_pairs={{0,14},{2,12},{4,10},{6,8},{8,6},{10,4},{12,2},{14,0},{1,15},{3,13... | collective-permute-start | bytes 491528 | tf_op jit(solution)/shard_map/ppermute | solution.py:267
  32.5 2.2 %collective-permute-start.7 = (bf16[160,2048]{1,0:T(8,128)(2,1)S(1)}, bf16[160,2048]{1,0:T(8,128)(2,1)S(1)}, u32[]{:S(2)}, u32[]{:S(2)}) collective-permute-start(bf16[160,2048]{1,0:T(8,128)(2,1)S(1)} %get-tuple-element.61.mine_ref), channel_id=1, source_target_pairs={{0,1},{1,0},{2,3},{3,2},{4,5},{5,4},{6,7},{7,6},{8,9},{9,8},{10,11... | collective-permute-start | bytes 1966088 | tf_op jit(solution)/shard_map/ppermute | solution.py:270
  32.5 5.7 %collective-permute-start.8 = (bf16[160,2048]{1,0:T(8,128)(2,1)S(1)}, bf16[160,2048]{1,0:T(8,128)(2,1)S(1)}, u32[]{:S(2)}, u32[]{:S(2)}) collective-permute-start(bf16[160,2048]{1,0:T(8,128)(2,1)S(1)} %get-tuple-element.69.mine_ref), channel_id=1, source_target_pairs={{0,1},{1,0},{2,3},{3,2},{4,5},{5,4},{6,7},{7,6},{8,9},{9,8},{10,11... | collective-permute-start | bytes 1966088 | tf_op jit(solution)/shard_map/ppermute | solution.py:270
  38.1 4.3 %collective-permute-start.9 = (bf16[160,2048]{1,0:T(8,128)(2,1)S(1)}, bf16[160,2048]{1,0:T(8,128)(2,1)S(1)}, u32[]{:S(2)}, u32[]{:S(2)}) collective-permute-start(bf16[160,2048]{1,0:T(8,128)(2,1)S(1)} %get-tuple-element.77), channel_id=1, source_target_pairs={{0,1},{1,0},{2,3},{3,2},{4,5},{5,4},{6,7},{7,6},{8,9},{9,8},{10,11... | collective-permute-start | bytes 1966088 | tf_op jit(solution)/shard_map/ppermute | solution.py:270
  41.9 2.2 %collective-permute-start.10 = (bf16[160,2048]{1,0:T(8,128)(2,1)S(1)}, bf16[160,2048]{1,0:T(8,128)(2,1)S(1)}, u32[]{:S(2)}, u32[]{:S(2)}) collective-permute-start(bf16[160,2048]{1,0:T(8,128)(2,1)S(1)} %get-tuple-element.78), channel_id=1, source_target_pairs={{0,1},{1,0},{2,3},{3,2},{4,5},{5,4},{6,7},{7,6},{8,9},{9,8},{10,11... | collective-permute-start | bytes 1966088 | tf_op jit(solution)/shard_map/ppermute | solution.py:270
  45.0 11.1 %collective-permute-start.13 = (bf16[40,2048]{1,0:T(8,128)(2,1)S(1)}, bf16[40,2048]{1,0:T(8,128)(2,1)S(1)}, u32[]{:S(2)}, u32[]{:S(2)}) collective-permute-start(bf16[40,2048]{1,0:T(8,128)(2,1)S(1)} %get-tuple-element.82), channel_id=1, source_target_pairs={{0,2},{2,0},{4,6},{6,4},{8,10},{10,8},{12,14},{14,12},{1,3},{3,1},... | collective-permute-start | bytes 491528 | tf_op jit(solution)/shard_map/ppermute | solution.py:267
  47.1 12.1 %collective-permute-start.14 = (bf16[40,2048]{1,0:T(8,128)(2,1)S(1)}, bf16[40,2048]{1,0:T(8,128)(2,1)S(1)}, u32[]{:S(2)}, u32[]{:S(2)}) collective-permute-start(bf16[40,2048]{1,0:T(8,128)(2,1)S(1)} %get-tuple-element.83), channel_id=1, source_target_pairs={{0,12},{2,14},{4,8},{6,10},{8,4},{10,6},{12,0},{14,2},{1,13},{3,15... | collective-permute-start | bytes 491528 | tf_op jit(solution)/shard_map/ppermute | solution.py:267
  49.5 14.2 %collective-permute-start.15 = (bf16[40,2048]{1,0:T(8,128)(2,1)S(1)}, bf16[40,2048]{1,0:T(8,128)(2,1)S(1)}, u32[]{:S(2)}, u32[]{:S(2)}) collective-permute-start(bf16[40,2048]{1,0:T(8,128)(2,1)S(1)} %get-tuple-element.84), channel_id=1, source_target_pairs={{0,14},{2,12},{4,10},{6,8},{8,6},{10,4},{12,2},{14,0},{1,15},{3,13... | collective-permute-start | bytes 491528 | tf_op jit(solution)/shard_map/ppermute | solution.py:267
  50.5 13.2 %collective-permute-start.16 = (bf16[40,2048]{1,0:T(8,128)(2,1)S(1)}, bf16[40,2048]{1,0:T(8,128)(2,1)S(1)}, u32[]{:S(2)}, u32[]{:S(2)}) collective-permute-start(bf16[40,2048]{1,0:T(8,128)(2,1)S(1)} %get-tuple-element.85), channel_id=1, source_target_pairs={{0,4},{2,6},{4,0},{6,2},{8,12},{10,14},{12,8},{14,10},{1,5},{3,7},... | collective-permute-start | bytes 491528 | tf_op jit(solution)/shard_map/ppermute | solution.py:267
  55.2 10.6 %collective-permute-start.17 = (bf16[40,2048]{1,0:T(8,128)(2,1)S(1)}, bf16[40,2048]{1,0:T(8,128)(2,1)S(1)}, u32[]{:S(2)}, u32[]{:S(2)}) collective-permute-start(bf16[40,2048]{1,0:T(8,128)(2,1)S(1)} %get-tuple-element.86), channel_id=1, source_target_pairs={{0,6},{2,4},{4,2},{6,0},{8,14},{10,12},{12,10},{14,8},{1,7},{3,5},... | collective-permute-start | bytes 491528 | tf_op jit(solution)/shard_map/ppermute | solution.py:267
  56.2 21.2 %collective-permute-start.11 = (bf16[40,2048]{1,0:T(8,128)(2,1)S(1)}, bf16[40,2048]{1,0:T(8,128)(2,1)S(1)}, u32[]{:S(2)}, u32[]{:S(2)}) collective-permute-start(bf16[40,2048]{1,0:T(8,128)(2,1)S(1)} %get-tuple-element.79), channel_id=1, source_target_pairs={{0,8},{2,10},{4,12},{6,14},{8,0},{10,2},{12,4},{14,6},{1,9},{3,11}... | collective-permute-start | bytes 491528 | tf_op jit(solution)/shard_map/ppermute | solution.py:267
  59.2 20.7 %collective-permute-start.12 = (bf16[40,2048]{1,0:T(8,128)(2,1)S(1)}, bf16[40,2048]{1,0:T(8,128)(2,1)S(1)}, u32[]{:S(2)}, u32[]{:S(2)}) collective-permute-start(bf16[40,2048]{1,0:T(8,128)(2,1)S(1)} %get-tuple-element.80), channel_id=1, source_target_pairs={{0,10},{2,8},{4,14},{6,12},{8,2},{10,0},{12,6},{14,4},{1,11},{3,9}... | collective-permute-start | bytes 491528 | tf_op jit(solution)/shard_map/ppermute | solution.py:267

commit v7 on v5

--- a/solution.py
+++ b/solution.py
@@ -115,7 +115,7 @@
 
 
 def regroup_kernel(local_experts, count, *refs):
-    ins, low_ref, high_ref, held = refs[:count], refs[count], refs[count + 1], refs[count + 2]
+    ins, outs, held = refs[:count], refs[count:-1], refs[-1]
     block, each = local_experts * CAP, count * CAP
     for b in range(count):
         held[b * block : (b + 1) * block, :] = ins[b][...]
@@ -125,15 +125,17 @@
     b = (j * 205) >> 11
     source = b * block + e * CAP + (j - b * CAP)
     mover = (iota((local_experts * each, count * block), 1) == source).astype(jnp.bfloat16)
-    step, middle = 512, low_ref.shape[0]
+    step, tall = 512, outs[0].shape[0]
     for c in range(0, held.shape[1], step):
         got = dot(mover, held[:, c : c + step]).astype(jnp.bfloat16)
-        low_ref[:, c : c + step] = got[:middle, :]
-        high_ref[:, c : c + step] = got[middle:, :]
-
-
-def ungroup_kernel(local_experts, count, own_low, own_high, other_low, other_high, *refs):
+        for k, out_ref in enumerate(outs):
+            out_ref[:, c : c + step] = got[k * tall : (k + 1) * tall, :]
+
+
+def ungroup_kernel(local_experts, count, *refs):
     block, each = local_experts * CAP, count * CAP
+    kept, refs = refs[:-count], refs[-count:]
+    halves = list(zip(kept[: len(kept) // 2], kept[len(kept) // 2 :]))
     s = iota((count * block, 1), 0)
     b = (s * 1639) >> 16
     t = s - b * block
@@ -141,11 +143,11 @@
     source = e * each + b * CAP + (t - e * CAP)
     mover = (iota((count * block, local_experts * each), 1) == source).astype(jnp.bfloat16)
     step = 512
-    for c in range(0, own_low.shape[1], step):
+    for c in range(0, kept[0].shape[1], step):
         at = slice(c, c + step)
         parts = [
             (own[:, at] + other[:, at].astype(jnp.float32)).astype(jnp.bfloat16)
-            for own, other in ((own_low, other_low), (own_high, other_high))
+            for own, other in halves
         ]
         got = dot(mover, jnp.concatenate(parts, axis=0)).astype(jnp.bfloat16)
         for k in range(count):
@@ -292,35 +294,36 @@
     weights = [gate_now] + list(weights[1:])
 
     tall = groups * CAP * local_experts
-    half_rows = jax.ShapeDtypeStruct((tall // 2, width), bf16)
+    splits = 4
+    part_rows = jax.ShapeDtypeStruct((tall // splits, width), bf16)
     mine = pl.pallas_call(
         functools.partial(regroup_kernel, local_experts, groups),
-        out_shape=[half_rows] * 2,
+        out_shape=[part_rows] * splits,
         in_specs=whole(groups),
-        out_specs=whole(2),
+        out_specs=whole(splits),
         scratch_shapes=[VMEM((groups * block, width), bf16)],
         compiler_params=params(4),
         cost_estimate=cost(2 * tall * groups * block * width, 4 * tall * width),
         name="regroup",
     )(*[incoming[k] for k in range(groups)])
     own, other = [], []
-    for h in range(2):
+    for h in range(splits):
         theirs = swap(mine[h])
         kept, send = pl.pallas_call(
             functools.partial(ffn_kernel, groups * CAP),
-            out_shape=[jax.ShapeDtypeStruct((tall // 2, width), jnp.float32), half_rows],
-            in_specs=whole(2 + pieces // 2),
+            out_shape=[jax.ShapeDtypeStruct((tall // splits, width), jnp.float32), part_rows],
+            in_specs=whole(2 + pieces // splits),
             out_specs=whole(2),
             compiler_params=params(8),
-            cost_estimate=cost(6 * tall * width * half, 3 * local_experts * half * width),
+            cost_estimate=cost(12 * tall * width * half // splits, 6 * local_experts * half * width // splits),
             name="ffn",
-        )(mine[h], theirs, *weights[h * pieces // 2 : (h + 1) * pieces // 2])
+        )(mine[h], theirs, *weights[h * pieces // splits : (h + 1) * pieces // splits])
         own.append(kept)
         other.append(swap(send))
     blocks = pl.pallas_call(
         functools.partial(ungroup_kernel, local_experts, groups),
         out_shape=[jax.ShapeDtypeStruct((block, width), bf16)] * groups,
-        in_specs=whole(4),
+        in_specs=whole(2 * splits),
         out_specs=whole(groups),
         compiler_params=params(4),
         cost_estimate=cost(2 * tall * groups * block * width, 4 * tall * width),

time: 81.3 us -> 81.3 us (level)
  waiting for transfers between devices: 21.5 us -> 20.1 us
  starting transfers between devices: 34.9 us -> 36 us
    ppermute x4 -> x8, waiting for transfers between devices: 3.31 us -> 1.87 us  [swap(): return lax.ppermute(x, 'dp', [(0, 1), (1, 0)])]
    ppermute x4 -> x8, starting transfers between devices: 1.2 us -> 2.36 us  [swap(): return lax.ppermute(x, 'dp', [(0, 1), (1, 0)])]
    pallas_call x2 -> x4, Pallas kernels: 7.04 us -> 7.34 us  [fast(): pl.pallas_call(functools.partial(ffn_kernel, groups * CAP), out_shape=[ja...]
  transfers between devices with their start and end apart: 18 -> 22, of which waited for: 7 -> 7; matrix products, arithmetic and copies ran while one was open for 0% -> 0% of each run, Pallas kernels for 24% -> 24%
where the time goes in v7:
time: 81.3 us; the launch traced here: 81.2 us
  starting transfers between devices  36 us (44%)
  Pallas kernels  24.9 us (31%)
  waiting for transfers between devices  20.1 us (25%)
    ppermute x14, starting transfers between devices, hop(): return lax.ppermute(x, 'expert', [(i, i ^ k) for i in range(groups)])  33.7 us
    ppermute x14, waiting for transfers between devices, hop(): return lax.ppermute(x, 'expert', [(i, i ^ k) for i in range(groups)])  18.2 us
    pallas_call x1, Pallas kernels, fast(): pl.pallas_call(functools.partial(load_kernel, half), out_shape=[turned, t...  11.9 us
    pallas_call x4, Pallas kernels, fast(): pl.pallas_call(functools.partial(ffn_kernel, groups * CAP), out_shape=[ja...  7.34 us
    ppermute x8, starting transfers between devices, swap(): return lax.ppermute(x, 'dp', [(0, 1), (1, 0)])  2.36 us
    pallas_call x1, Pallas kernels, fast(): pl.pallas_call(functools.partial(pack_kernel, local_experts, groups), out...  2.14 us
    ppermute x8, waiting for transfers between devices, swap(): return lax.ppermute(x, 'dp', [(0, 1), (1, 0)])  1.87 us
    pallas_call x2, Pallas kernels, fast(): pl.pallas_call(functools.partial(combine_kernel, block, chunk, first), ou...  1.76 us
  transfers between devices with their start and end apart: 22, of which 7 were waited for; matrix products, arithmetic and copies ran while one was open for 0% of the time, Pallas kernels for 24%

profile of v7, /device:TPU:0, one launch (start us, length us, event | category | flops | bytes accessed | tf_op | source)
XLA Modules:
  0.0 81.2 jit_solution(496576195730433462)
XLA Ops:
  0.0 0.1 pad_add_fusion.place_ref
  0.1 2.1 %pack.1 = (f32[128,128]{1,0:T(8,128)S(1)}, bf16[40,2048]{1,0:T(8,128)(2,1)S(1)}, bf16[40,2048]{1,0:T(8,128)(2,1)S(1)}, bf16[40,2048]{1,0:T(8,128)(2,1)S(1)}, bf1...) custom-call(s32[2]{0:T(128)S(1)} %pad_add_fusion.place_ref, ...), custom_call_target="tpu_custom_call" | custom-call | flops 167772160 | bytes 1572864 | tf_op jit(solution)/shard_map/pack/pallas_call | solution.py:247
  2.2 3.0 %collective-permute-start = (bf16[40,2048]{1,0:T(8,128)(2,1)S(1)}, bf16[40,2048]{1,0:T(8,128)(2,1)S(1)}, u32[]{:S(2)}, u32[]{:S(2)}) collective-permute-start(bf16[40,2048]{1,0:T(8,128)(2,1)S(1)} %get-tuple-element.53), channel_id=1, source_target_pairs={{0,2},{2,0},{4,6},{6,4},{8,10},{10,8},{12,14},{14,12},{1,3},{3,1},... | collective-permute-start | bytes 491528 | tf_op jit(solution)/shard_map/ppermute | solution.py:266
  5.2 1.6 %collective-permute-start.1 = (bf16[40,2048]{1,0:T(8,128)(2,1)S(1)}, bf16[40,2048]{1,0:T(8,128)(2,1)S(1)}, u32[]{:S(2)}, u32[]{:S(2)}) collective-permute-start(bf16[40,2048]{1,0:T(8,128)(2,1)S(1)} %get-tuple-element.54), channel_id=1, source_target_pairs={{0,4},{2,6},{4,0},{6,2},{8,12},{10,14},{12,8},{14,10},{1,5},{3,7},... | collective-permute-start | bytes 491528 | tf_op jit(solution)/shard_map/ppermute | solution.py:266
  6.8 2.6 %collective-permute-start.3 = (bf16[40,2048]{1,0:T(8,128)(2,1)S(1)}, bf16[40,2048]{1,0:T(8,128)(2,1)S(1)}, u32[]{:S(2)}, u32[]{:S(2)}) collective-permute-start(bf16[40,2048]{1,0:T(8,128)(2,1)S(1)} %get-tuple-element.57), channel_id=1, source_target_pairs={{0,8},{2,10},{4,12},{6,14},{8,0},{10,2},{12,4},{14,6},{1,9},{3,11}... | collective-permute-start | bytes 491528 | tf_op jit(solution)/shard_map/ppermute | solution.py:266
  9.4 0.3 collective-permute-start.4
  9.7 2.5 %collective-permute-start.5 = (bf16[40,2048]{1,0:T(8,128)(2,1)S(1)}, bf16[40,2048]{1,0:T(8,128)(2,1)S(1)}, u32[]{:S(2)}, u32[]{:S(2)}) collective-permute-start(bf16[40,2048]{1,0:T(8,128)(2,1)S(1)} %get-tuple-element.62), channel_id=1, source_target_pairs={{0,12},{2,14},{4,8},{6,10},{8,4},{10,6},{12,0},{14,2},{1,13},{3,15... | collective-permute-start | bytes 491528 | tf_op jit(solution)/shard_map/ppermute | solution.py:266
  12.2 0.0 collective-permute-done.refs_1_
  12.2 1.6 %collective-permute-start.2 = (bf16[40,2048]{1,0:T(8,128)(2,1)S(1)}, bf16[40,2048]{1,0:T(8,128)(2,1)S(1)}, u32[]{:S(2)}, u32[]{:S(2)}) collective-permute-start(bf16[40,2048]{1,0:T(8,128)(2,1)S(1)} %get-tuple-element.56), channel_id=1, source_target_pairs={{0,6},{2,4},{4,2},{6,0},{8,14},{10,12},{12,10},{14,8},{1,7},{3,5},... | collective-permute-start | bytes 491528 | tf_op jit(solution)/shard_map/ppermute | solution.py:266
  13.8 0.2 collective-permute-done.1.refs_2_
  14.0 3.5 %collective-permute-start.6 = (bf16[40,2048]{1,0:T(8,128)(2,1)S(1)}, bf16[40,2048]{1,0:T(8,128)(2,1)S(1)}, u32[]{:S(2)}, u32[]{:S(2)}) collective-permute-start(bf16[40,2048]{1,0:T(8,128)(2,1)S(1)} %get-tuple-element.64), channel_id=1, source_target_pairs={{0,14},{2,12},{4,10},{6,8},{8,6},{10,4},{12,2},{14,0},{1,15},{3,13... | collective-permute-start | bytes 491528 | tf_op jit(solution)/shard_map/ppermute | solution.py:266
  17.5 11.9 %load.1 = (bf16[2048,704]{1,0:T(8,128)(2,1)S(1)}, bf16[2048,704]{1,0:T(8,128)(2,1)S(1)}, bf16[704,2048]{1,0:T(8,128)(2,1)S(1)}, bf16[2048,704]{1,0:T(8,128)(2,1)...) custom-call(s32[2]{0:T(128)S(1)} %pad_add_fusion.place_ref, ...), custom_call_target="tpu_custom_call" | custom-call | bytes 34603008 | tf_op jit(solution)/shard_map/load/pallas_call | solution.py:283
  29.4 0.0 collective-permute-done.3.refs_4_
  29.4 2.2 %collective-permute-done.4.refs_5_ = bf16[40,2048]{1,0:T(8,128)(2,1)S(1)} collective-permute-done((bf16[40,2048]{1,0:T(8,128)(2,1)S(1)}, bf16[40,2048]{1,0:T(8,128)(2,1)S(1)}, u32[]{:S(2)}, u32[]{:S(2)}) %collective-permute-start.4) | collective-permute-done | bytes 163872 | tf_op jit(solution)/shard_map/ppermute | solution.py:266
  31.6 0.0 collective-permute-done.5.refs_6_
  31.6 0.0 collective-permute-done.2.refs_3_
  31.6 0.0 collective-permute-done.6.refs_7_
  31.6 0.9 %regroup.1 = (bf16[80,2048]{1,0:T(8,128)(2,1)S(1)}, bf16[80,2048]{1,0:T(8,128)(2,1)S(1)}, bf16[80,2048]{1,0:T(8,128)(2,1)S(1)}, bf16[80,2048]{1,0:T(8,128)(2,1)S(1)}) custom-call(bf16[40,2048]{1,0:T(8,128)(2,1)S(1)} %get-tuple-element.52.refs_0_, bf16[40,2048]{1,0:T(8,128)(2,1)S(1)} %collective-permute-done.refs_1_, ...), custom_call_target="tpu_custom_call" | custom-call | flops 419430400 | bytes 2621440 | tf_op jit(solution)/shard_map/regroup/pallas_call | solution.py:299
  32.5 0.1 collective-permute-start.7
  32.5 0.5 collective-permute-start.8
  33.0 0.1 collective-permute-start.9
  33.1 0.4 collective-permute-start.10
  33.6 0.6 collective-permute-done.7.theirs_ref
  34.2 1.8 %ffn.4 = (f32[80,2048]{1,0:T(8,128)S(1)}, bf16[80,2048]{1,0:T(8,128)(2,1)S(1)}) custom-call(bf16[80,2048]{1,0:T(8,128)(2,1)S(1)} %get-tuple-element.65.mine_ref, bf16[80,2048]{1,0:T(8,128)(2,1)S(1)} %collective-permute-done.7.theirs_ref, bf16[2048,704]{1,0:T(8,128)(2,1)S(1)} %get-tuple-element.66.refs_0_, bf16[2048,704]{1,0:T(8,128)(2,1)S(1)} %get-tuple-element.67.refs_1_, ...), custom_call_target="tpu_custom_call" | custom-call | flops 1384120320 | bytes 8650752 | tf_op jit(solution)/shard_map/ffn/pallas_call | solution.py:312
  36.0 0.2 collective-permute-start.11
  36.2 0.0 collective-permute-done.8.theirs_ref
  36.2 1.8 %ffn.5 = (f32[80,2048]{1,0:T(8,128)S(1)}, bf16[80,2048]{1,0:T(8,128)(2,1)S(1)}) custom-call(bf16[80,2048]{1,0:T(8,128)(2,1)S(1)} %get-tuple-element.70.mine_ref, bf16[80,2048]{1,0:T(8,128)(2,1)S(1)} %collective-permute-done.8.theirs_ref, bf16[2048,704]{1,0:T(8,128)(2,1)S(1)} %get-tuple-element.71.refs_0_, bf16[2048,704]{1,0:T(8,128)(2,1)S(1)} %get-tuple-element.72.refs_1_, ...), custom_call_target="tpu_custom_call" | custom-call | flops 1384120320 | bytes 8650752 | tf_op jit(solution)/shard_map/ffn/pallas_call | solution.py:312
  38.0 0.4 collective-permute-start.12
  38.4 0.0 collective-permute-done.9.theirs_ref
  38.4 2.0 %ffn.6 = (f32[80,2048]{1,0:T(8,128)S(1)}, bf16[80,2048]{1,0:T(8,128)(2,1)S(1)}) custom-call(bf16[80,2048]{1,0:T(8,128)(2,1)S(1)} %get-tuple-element.75.mine_ref, bf16[80,2048]{1,0:T(8,128)(2,1)S(1)} %collective-permute-done.9.theirs_ref, bf16[2048,704]{1,0:T(8,128)(2,1)S(1)} %get-tuple-element.76.refs_0_, bf16[2048,704]{1,0:T(8,128)(2,1)S(1)} %get-tuple-element.77.refs_1_, ...), custom_call_target="tpu_custom_call" | custom-call | flops 1384120320 | bytes 8650752 | tf_op jit(solution)/shard_map/ffn/pallas_call | solution.py:312
  40.4 0.2 collective-permute-start.13
  40.6 0.0 collective-permute-done.10.theirs_ref
  40.6 1.8 %ffn.7 = (f32[80,2048]{1,0:T(8,128)S(1)}, bf16[80,2048]{1,0:T(8,128)(2,1)S(1)}) custom-call(bf16[80,2048]{1,0:T(8,128)(2,1)S(1)} %get-tuple-element.80.mine_ref, bf16[80,2048]{1,0:T(8,128)(2,1)S(1)} %collective-permute-done.10.theirs_ref, bf16[2048,704]{1,0:T(8,128)(2,1)S(1)} %get-tuple-element.81.refs_0_, bf16[2048,704]{1,0:T(8,128)(2,1)S(1)} %get-tuple-element.82.refs_1_, ...), custom_call_target="tpu_custom_call" | custom-call | flops 1384120320 | bytes 8650752 | tf_op jit(solution)/shard_map/ffn/pallas_call | solution.py:312
  42.4 0.4 collective-permute-start.14
  42.8 0.0 collective-permute-done.11.refs_4_
  42.8 0.0 collective-permute-done.12.refs_5_
  42.8 0.0 collective-permute-done.13.refs_6_
  42.8 1.2 %collective-permute-done.14.refs_7_ = bf16[80,2048]{1,0:T(8,128)(2,1)S(1)} collective-permute-done((bf16[80,2048]{1,0:T(8,128)(2,1)S(1)}, bf16[80,2048]{1,0:T(8,128)(2,1)S(1)}, u32[]{:S(2)}, u32[]{:S(2)}) %collective-permute-start.14) | collective-permute-done | bytes 327712 | tf_op jit(solution)/shard_map/ppermute | solution.py:269
  44.1 0.9 %ungroup.1 = (bf16[40,2048]{1,0:T(8,128)(2,1)S(1)}, bf16[40,2048]{1,0:T(8,128)(2,1)S(1)}, bf16[40,2048]{1,0:T(8,128)(2,1)S(1)}, bf16[40,2048]{1,0:T(8,128)(2,1)S...) custom-call(f32[80,2048]{1,0:T(8,128)S(1)} %get-tuple-element.69.ref, ...), custom_call_target="tpu_custom_call" | custom-call | flops 419430400 | bytes 2621440 | tf_op jit(solution)/shard_map/ungroup/pallas_call | solution.py:323
  45.0 2.1 %collective-permute-start.19 = (bf16[40,2048]{1,0:T(8,128)(2,1)S(1)}, bf16[40,2048]{1,0:T(8,128)(2,1)S(1)}, u32[]{:S(2)}, u32[]{:S(2)}) collective-permute-start(bf16[40,2048]{1,0:T(8,128)(2,1)S(1)} %get-tuple-element.94), channel_id=1, source_target_pairs={{0,2},{2,0},{4,6},{6,4},{8,10},{10,8},{12,14},{14,12},{1,3},{3,1},... | collective-permute-start | bytes 491528 | tf_op jit(solution)/shard_map/ppermute | solution.py:266
  47.1 2.4 %collective-permute-start.20 = (bf16[40,2048]{1,0:T(8,128)(2,1)S(1)}, bf16[40,2048]{1,0:T(8,128)(2,1)S(1)}, u32[]{:S(2)}, u32[]{:S(2)}) collective-permute-start(bf16[40,2048]{1,0:T(8,128)(2,1)S(1)} %get-tuple-element.95), channel_id=1, source_target_pairs={{0,12},{2,14},{4,8},{6,10},{8,4},{10,6},{12,0},{14,2},{1,13},{3,15... | collective-permute-start | bytes 491528 | tf_op jit(solution)/shard_map/ppermute | solution.py:266
  49.5 1.0 %collective-permute-start.21 = (bf16[40,2048]{1,0:T(8,128)(2,1)S(1)}, bf16[40,2048]{1,0:T(8,128)(2,1)S(1)}, u32[]{:S(2)}, u32[]{:S(2)}) collective-permute-start(bf16[40,2048]{1,0:T(8,128)(2,1)S(1)} %get-tuple-element.96), channel_id=1, source_target_pairs={{0,14},{2,12},{4,10},{6,8},{8,6},{10,4},{12,2},{14,0},{1,15},{3,13... | collective-permute-start | bytes 491528 | tf_op jit(solution)/shard_map/ppermute | solution.py:266
  50.4 4.7 %collective-permute-start.15 = (bf16[40,2048]{1,0:T(8,128)(2,1)S(1)}, bf16[40,2048]{1,0:T(8,128)(2,1)S(1)}, u32[]{:S(2)}, u32[]{:S(2)}) collective-permute-start(bf16[40,2048]{1,0:T(8,128)(2,1)S(1)} %get-tuple-element.89), channel_id=1, source_target_pairs={{0,4},{2,6},{4,0},{6,2},{8,12},{10,14},{12,8},{14,10},{1,5},{3,7},... | collective-permute-start | bytes 491528 | tf_op jit(solution)/shard_map/ppermute | solution.py:266
  55.2 0.9 %collective-permute-start.16 = (bf16[40,2048]{1,0:T(8,128)(2,1)S(1)}, bf16[40,2048]{1,0:T(8,128)(2,1)S(1)}, u32[]{:S(2)}, u32[]{:S(2)}) collective-permute-start(bf16[40,2048]{1,0:T(8,128)(2,1)S(1)} %get-tuple-element.90), channel_id=1, source_target_pairs={{0,6},{2,4},{4,2},{6,0},{8,14},{10,12},{12,10},{14,8},{1,7},{3,5},... | collective-permute-start | bytes 491528 | tf_op jit(solution)/shard_map/ppermute | solution.py:266
  56.1 0.0 collective-permute-done.19.refs_2_
  56.1 3.0 %collective-permute-start.17 = (bf16[40,2048]{1,0:T(8,128)(2,1)S(1)}, bf16[40,2048]{1,0:T(8,128)(2,1)S(1)}, u32[]{:S(2)}, u32[]{:S(2)}) collective-permute-start(bf16[40,2048]{1,0:T(8,128)(2,1)S(1)} %get-tuple-element.91), channel_id=1, source_target_pairs={{0,8},{2,10},{4,12},{6,14},{8,0},{10,2},{12,4},{14,6},{1,9},{3,11}... | collective-permute-start | bytes 491528 | tf_op jit(solution)/shard_map/ppermute | solution.py:266
  59.2 0.0 collective-permute-done.20.refs_3_
  59.2 4.4 %collective-permute-start.18 = (bf16[40,2048]{1,0:T(8,128)(2,1)S(1)}, bf16[40,2048]{1,0:T(8,128)(2,1)S(1)}, u32[]{:S(2)}, u32[]{:S(2)}) collective-permute-start(bf16[40,2048]{1,0:T(8,128)(2,1)S(1)} %get-tuple-element.92), channel_id=1, source_target_pairs={{0,10},{2,8},{4,14},{6,12},{8,2},{10,0},{12,6},{14,4},{1,11},{3,9}... | collective-permute-start | bytes 491528 | tf_op jit(solution)/shard_map/ppermute | solution.py:266
  63.6 0.0 collective-permute-done.21.refs_4_
  63.6 0.5 combine.2.refs_5_
  64.1 0.0 collective-permute-done.15.refs_1_
  64.1 1.7 %collective-permute-done.16.refs_2_ = bf16[40,2048]{1,0:T(8,128)(2,1)S(1)} collective-permute-done((bf16[40,2048]{1,0:T(8,128)(2,1)S(1)}, bf16[40,2048]{1,0:T(8,128)(2,1)S(1)}, u32[]{:S(2)}, u32[]{:S(2)}) %collective-permute-start.16) | collective-permute-done | bytes 163872 | tf_op jit(solution)/shard_map/ppermute | solution.py:266
  65.8 11.6 %collective-permute-done.17.refs_3_ = bf16[40,2048]{1,0:T(8,128)(2,1)S(1)} collective-permute-done((bf16[40,2048]{1,0:T(8,128)(2,1)S(1)}, bf16[40,2048]{1,0:T(8,128)(2,1)S(1)}, u32[]{:S(2)}, u32[]{:S(2)}) %collective-permute-start.17) | collective-permute-done | bytes 163872 | tf_op jit(solution)/shard_map/ppermute | solution.py:266
  77.3 2.6 %collective-permute-done.18.refs_4_ = bf16[40,2048]{1,0:T(8,128)(2,1)S(1)} collective-permute-done((bf16[40,2048]{1,0:T(8,128)(2,1)S(1)}, bf16[40,2048]{1,0:T(8,128)(2,1)S(1)}, u32[]{:S(2)}, u32[]{:S(2)}) %collective-permute-start.18) | collective-permute-done | bytes 163872 | tf_op jit(solution)/shard_map/ppermute | solution.py:266
  79.9 1.3 %combine.3 = bf16[128,2048]{1,0:T(8,128)(2,1)} custom-call(f32[128,128]{1,0:T(8,128)S(1)} %get-tuple-element.58._.refs_0_, bf16[40,2048]{1,0:T(8,128)(2,1)S(1)} %collective-permute-done.15.refs_1_, bf16[40,2048]{1,0:T(8,128)(2,1)S(1)} %collective-permute-done.16.refs_2_, bf16[40,2048]{1,0:T(8,128)(2,1)S(1)} %collective-permute-done.17.refs_3_, ...), custom_call_target="tpu_custom_call" | custom-call | flops 167772160 | bytes 1048576 | tf_op jit(solution)/shard_map/combine/pallas_call | solution.py:339
Async XLA Ops:
  2.2 10.0 %collective-permute-start = (bf16[40,2048]{1,0:T(8,128)(2,1)S(1)}, bf16[40,2048]{1,0:T(8,128)(2,1)S(1)}, u32[]{:S(2)}, u32[]{:S(2)}) collective-permute-start(bf16[40,2048]{1,0:T(8,128)(2,1)S(1)} %get-tuple-element.53), channel_id=1, source_target_pairs={{0,2},{2,0},{4,6},{6,4},{8,10},{10,8},{12,14},{14,12},{1,3},{3,1},... | collective-permute-start | bytes 491528 | tf_op jit(solution)/shard_map/ppermute | solution.py:266
  5.2 8.7 %collective-permute-start.1 = (bf16[40,2048]{1,0:T(8,128)(2,1)S(1)}, bf16[40,2048]{1,0:T(8,128)(2,1)S(1)}, u32[]{:S(2)}, u32[]{:S(2)}) collective-permute-start(bf16[40,2048]{1,0:T(8,128)(2,1)S(1)} %get-tuple-element.54), channel_id=1, source_target_pairs={{0,4},{2,6},{4,0},{6,2},{8,12},{10,14},{12,8},{14,10},{1,5},{3,7},... | collective-permute-start | bytes 491528 | tf_op jit(solution)/shard_map/ppermute | solution.py:266
  6.8 22.6 %collective-permute-start.3 = (bf16[40,2048]{1,0:T(8,128)(2,1)S(1)}, bf16[40,2048]{1,0:T(8,128)(2,1)S(1)}, u32[]{:S(2)}, u32[]{:S(2)}) collective-permute-start(bf16[40,2048]{1,0:T(8,128)(2,1)S(1)} %get-tuple-element.57), channel_id=1, source_target_pairs={{0,8},{2,10},{4,12},{6,14},{8,0},{10,2},{12,4},{14,6},{1,9},{3,11}... | collective-permute-start | bytes 491528 | tf_op jit(solution)/shard_map/ppermute | solution.py:266
  9.4 22.2 %collective-permute-start.4 = (bf16[40,2048]{1,0:T(8,128)(2,1)S(1)}, bf16[40,2048]{1,0:T(8,128)(2,1)S(1)}, u32[]{:S(2)}, u32[]{:S(2)}) collective-permute-start(bf16[40,2048]{1,0:T(8,128)(2,1)S(1)} %get-tuple-element.61), channel_id=1, source_target_pairs={{0,10},{2,8},{4,14},{6,12},{8,2},{10,0},{12,6},{14,4},{1,11},{3,9}... | collective-permute-start | bytes 491528 | tf_op jit(solution)/shard_map/ppermute | solution.py:266
  9.7 21.9 %collective-permute-start.5 = (bf16[40,2048]{1,0:T(8,128)(2,1)S(1)}, bf16[40,2048]{1,0:T(8,128)(2,1)S(1)}, u32[]{:S(2)}, u32[]{:S(2)}) collective-permute-start(bf16[40,2048]{1,0:T(8,128)(2,1)S(1)} %get-tuple-element.62), channel_id=1, source_target_pairs={{0,12},{2,14},{4,8},{6,10},{8,4},{10,6},{12,0},{14,2},{1,13},{3,15... | collective-permute-start | bytes 491528 | tf_op jit(solution)/shard_map/ppermute | solution.py:266
  12.2 19.4 %collective-permute-start.2 = (bf16[40,2048]{1,0:T(8,128)(2,1)S(1)}, bf16[40,2048]{1,0:T(8,128)(2,1)S(1)}, u32[]{:S(2)}, u32[]{:S(2)}) collective-permute-start(bf16[40,2048]{1,0:T(8,128)(2,1)S(1)} %get-tuple-element.56), channel_id=1, source_target_pairs={{0,6},{2,4},{4,2},{6,0},{8,14},{10,12},{12,10},{14,8},{1,7},{3,5},... | collective-permute-start | bytes 491528 | tf_op jit(solution)/shard_map/ppermute | solution.py:266
  14.0 17.6 %collective-permute-start.6 = (bf16[40,2048]{1,0:T(8,128)(2,1)S(1)}, bf16[40,2048]{1,0:T(8,128)(2,1)S(1)}, u32[]{:S(2)}, u32[]{:S(2)}) collective-permute-start(bf16[40,2048]{1,0:T(8,128)(2,1)S(1)} %get-tuple-element.64), channel_id=1, source_target_pairs={{0,14},{2,12},{4,10},{6,8},{8,6},{10,4},{12,2},{14,0},{1,15},{3,13... | collective-permute-start | bytes 491528 | tf_op jit(solution)/shard_map/ppermute | solution.py:266
  32.5 1.7 %collective-permute-start.7 = (bf16[80,2048]{1,0:T(8,128)(2,1)S(1)}, bf16[80,2048]{1,0:T(8,128)(2,1)S(1)}, u32[]{:S(2)}, u32[]{:S(2)}) collective-permute-start(bf16[80,2048]{1,0:T(8,128)(2,1)S(1)} %get-tuple-element.65.mine_ref), channel_id=1, source_target_pairs={{0,1},{1,0},{2,3},{3,2},{4,5},{5,4},{6,7},{7,6},{8,9},{9,8},{10,11... | collective-permute-start | bytes 983048 | tf_op jit(solution)/shard_map/ppermute | solution.py:269
  32.5 3.6 %collective-permute-start.8 = (bf16[80,2048]{1,0:T(8,128)(2,1)S(1)}, bf16[80,2048]{1,0:T(8,128)(2,1)S(1)}, u32[]{:S(2)}, u32[]{:S(2)}) collective-permute-start(bf16[80,2048]{1,0:T(8,128)(2,1)S(1)} %get-tuple-element.70.mine_ref), channel_id=1, source_target_pairs={{0,1},{1,0},{2,3},{3,2},{4,5},{5,4},{6,7},{7,6},{8,9},{9,8},{10,11... | collective-permute-start | bytes 983048 | tf_op jit(solution)/shard_map/ppermute | solution.py:269
  33.0 5.4 %collective-permute-start.9 = (bf16[80,2048]{1,0:T(8,128)(2,1)S(1)}, bf16[80,2048]{1,0:T(8,128)(2,1)S(1)}, u32[]{:S(2)}, u32[]{:S(2)}) collective-permute-start(bf16[80,2048]{1,0:T(8,128)(2,1)S(1)} %get-tuple-element.75.mine_ref), channel_id=1, source_target_pairs={{0,1},{1,0},{2,3},{3,2},{4,5},{5,4},{6,7},{7,6},{8,9},{9,8},{10,11... | collective-permute-start | bytes 983048 | tf_op jit(solution)/shard_map/ppermute | solution.py:269
  33.1 7.5 %collective-permute-start.10 = (bf16[80,2048]{1,0:T(8,128)(2,1)S(1)}, bf16[80,2048]{1,0:T(8,128)(2,1)S(1)}, u32[]{:S(2)}, u32[]{:S(2)}) collective-permute-start(bf16[80,2048]{1,0:T(8,128)(2,1)S(1)} %get-tuple-element.80.mine_ref), channel_id=1, source_target_pairs={{0,1},{1,0},{2,3},{3,2},{4,5},{5,4},{6,7},{7,6},{8,9},{9,8},{10,11... | collective-permute-start | bytes 983048 | tf_op jit(solution)/shard_map/ppermute | solution.py:269
  36.0 6.9 %collective-permute-start.11 = (bf16[80,2048]{1,0:T(8,128)(2,1)S(1)}, bf16[80,2048]{1,0:T(8,128)(2,1)S(1)}, u32[]{:S(2)}, u32[]{:S(2)}) collective-permute-start(bf16[80,2048]{1,0:T(8,128)(2,1)S(1)} %get-tuple-element.85), channel_id=1, source_target_pairs={{0,1},{1,0},{2,3},{3,2},{4,5},{5,4},{6,7},{7,6},{8,9},{9,8},{10,11... | collective-permute-start | bytes 983048 | tf_op jit(solution)/shard_map/ppermute | solution.py:269
  38.0 4.9 %collective-permute-start.12 = (bf16[80,2048]{1,0:T(8,128)(2,1)S(1)}, bf16[80,2048]{1,0:T(8,128)(2,1)S(1)}, u32[]{:S(2)}, u32[]{:S(2)}) collective-permute-start(bf16[80,2048]{1,0:T(8,128)(2,1)S(1)} %get-tuple-element.86), channel_id=1, source_target_pairs={{0,1},{1,0},{2,3},{3,2},{4,5},{5,4},{6,7},{7,6},{8,9},{9,8},{10,11... | collective-permute-start | bytes 983048 | tf_op jit(solution)/shard_map/ppermute | solution.py:269
  40.4 2.5 %collective-permute-start.13 = (bf16[80,2048]{1,0:T(8,128)(2,1)S(1)}, bf16[80,2048]{1,0:T(8,128)(2,1)S(1)}, u32[]{:S(2)}, u32[]{:S(2)}) collective-permute-start(bf16[80,2048]{1,0:T(8,128)(2,1)S(1)} %get-tuple-element.87), channel_id=1, source_target_pairs={{0,1},{1,0},{2,3},{3,2},{4,5},{5,4},{6,7},{7,6},{8,9},{9,8},{10,11... | collective-permute-start | bytes 983048 | tf_op jit(solution)/shard_map/ppermute | solution.py:269
  42.4 1.7 %collective-permute-start.14 = (bf16[80,2048]{1,0:T(8,128)(2,1)S(1)}, bf16[80,2048]{1,0:T(8,128)(2,1)S(1)}, u32[]{:S(2)}, u32[]{:S(2)}) collective-permute-start(bf16[80,2048]{1,0:T(8,128)(2,1)S(1)} %get-tuple-element.88), channel_id=1, source_target_pairs={{0,1},{1,0},{2,3},{3,2},{4,5},{5,4},{6,7},{7,6},{8,9},{9,8},{10,11... | collective-permute-start | bytes 983048 | tf_op jit(solution)/shard_map/ppermute | solution.py:269
  45.0 11.1 %collective-permute-start.19 = (bf16[40,2048]{1,0:T(8,128)(2,1)S(1)}, bf16[40,2048]{1,0:T(8,128)(2,1)S(1)}, u32[]{:S(2)}, u32[]{:S(2)}) collective-permute-start(bf16[40,2048]{1,0:T(8,128)(2,1)S(1)} %get-tuple-element.94), channel_id=1, source_target_pairs={{0,2},{2,0},{4,6},{6,4},{8,10},{10,8},{12,14},{14,12},{1,3},{3,1},... | collective-permute-start | bytes 491528 | tf_op jit(solution)/shard_map/ppermute | solution.py:266
  47.1 12.1 %collective-permute-start.20 = (bf16[40,2048]{1,0:T(8,128)(2,1)S(1)}, bf16[40,2048]{1,0:T(8,128)(2,1)S(1)}, u32[]{:S(2)}, u32[]{:S(2)}) collective-permute-start(bf16[40,2048]{1,0:T(8,128)(2,1)S(1)} %get-tuple-element.95), channel_id=1, source_target_pairs={{0,12},{2,14},{4,8},{6,10},{8,4},{10,6},{12,0},{14,2},{1,13},{3,15... | collective-permute-start | bytes 491528 | tf_op jit(solution)/shard_map/ppermute | solution.py:266
  49.5 14.2 %collective-permute-start.21 = (bf16[40,2048]{1,0:T(8,128)(2,1)S(1)}, bf16[40,2048]{1,0:T(8,128)(2,1)S(1)}, u32[]{:S(2)}, u32[]{:S(2)}) collective-permute-start(bf16[40,2048]{1,0:T(8,128)(2,1)S(1)} %get-tuple-element.96), channel_id=1, source_target_pairs={{0,14},{2,12},{4,10},{6,8},{8,6},{10,4},{12,2},{14,0},{1,15},{3,13... | collective-permute-start | bytes 491528 | tf_op jit(solution)/shard_map/ppermute | solution.py:266
  50.4 13.7 %collective-permute-start.15 = (bf16[40,2048]{1,0:T(8,128)(2,1)S(1)}, bf16[40,2048]{1,0:T(8,128)(2,1)S(1)}, u32[]{:S(2)}, u32[]{:S(2)}) collective-permute-start(bf16[40,2048]{1,0:T(8,128)(2,1)S(1)} %get-tuple-element.89), channel_id=1, source_target_pairs={{0,4},{2,6},{4,0},{6,2},{8,12},{10,14},{12,8},{14,10},{1,5},{3,7},... | collective-permute-start | bytes 491528 | tf_op jit(solution)/shard_map/ppermute | solution.py:266
  55.2 10.6 %collective-permute-start.16 = (bf16[40,2048]{1,0:T(8,128)(2,1)S(1)}, bf16[40,2048]{1,0:T(8,128)(2,1)S(1)}, u32[]{:S(2)}, u32[]{:S(2)}) collective-permute-start(bf16[40,2048]{1,0:T(8,128)(2,1)S(1)} %get-tuple-element.90), channel_id=1, source_target_pairs={{0,6},{2,4},{4,2},{6,0},{8,14},{10,12},{12,10},{14,8},{1,7},{3,5},... | collective-permute-start | bytes 491528 | tf_op jit(solution)/shard_map/ppermute | solution.py:266
  56.1 21.2 %collective-permute-start.17 = (bf16[40,2048]{1,0:T(8,128)(2,1)S(1)}, bf16[40,2048]{1,0:T(8,128)(2,1)S(1)}, u32[]{:S(2)}, u32[]{:S(2)}) collective-permute-start(bf16[40,2048]{1,0:T(8,128)(2,1)S(1)} %get-tuple-element.91), channel_id=1, source_target_pairs={{0,8},{2,10},{4,12},{6,14},{8,0},{10,2},{12,4},{14,6},{1,9},{3,11}... | collective-permute-start | bytes 491528 | tf_op jit(solution)/shard_map/ppermute | solution.py:266
  59.2 20.7 %collective-permute-start.18 = (bf16[40,2048]{1,0:T(8,128)(2,1)S(1)}, bf16[40,2048]{1,0:T(8,128)(2,1)S(1)}, u32[]{:S(2)}, u32[]{:S(2)}) collective-permute-start(bf16[40,2048]{1,0:T(8,128)(2,1)S(1)} %get-tuple-element.92), channel_id=1, source_target_pairs={{0,10},{2,8},{4,14},{6,12},{8,2},{10,0},{12,6},{14,4},{1,11},{3,9}... | collective-permute-start | bytes 491528 | tf_op jit(solution)/shard_map/ppermute | solution.py:266
